TPU v7x, 32 devices: a whole 2x2x4 slice. The times are simulated.
32 devices in a mesh: samp: 8 (over z, y), feat: 4 (over x, core).
Axes of the slice: x: 2, y: 2, z: 4, core: 2. Of those that a mesh axis runs over, the one named last changes fastest.
Arguments:
- layer_input: bfloat16 [512, 64, 512], P('samp', 'feat'), may hold values from -6 to 6
- segment_ids: int32 [512], replicated, may hold values from 0 to 3, as said below
- context_flags: int32 [512], replicated, may hold values from 0 to 1, as said below
- first_gain: float32 [512], replicated, may hold values from 0.1 to 1.9
- first_shift: float32 [512], replicated, may hold values from -3 to 3
- sample_weight: bfloat16 [512, 1536], replicated, may hold values from -0.25 to 0.25
- sample_bias: float32 [1024], replicated, may hold values from -3 to 3
- sample_mixer: bfloat16 [512, 512], replicated, may hold values from -1 to 1
- sample_offset: float32 [512], replicated, may hold values from -3 to 3
- second_gain: float32 [512], replicated, may hold values from 0.1 to 1.9
- second_shift: float32 [512], replicated, may hold values from -3 to 3
- feature_weight: bfloat16 [512, 1536], replicated, may hold values from -0.25 to 0.25
- feature_bias: float32 [1024], replicated, may hold values from -3 to 3
- feature_mixer: bfloat16 [512, 512], replicated, may hold values from -1.5 to 1.5
- feature_offset: float32 [512], replicated, may hold values from -3 to 3
- third_gain: float32 [512], replicated, may hold values from 0.1 to 1.9
- third_shift: float32 [512], replicated, may hold values from -3 to 3
- expand_weight: bfloat16 [512, 2048], replicated, may hold values from -0.25 to 0.25
- expand_bias: float32 [2048], replicated, may hold values from -3 to 3
- reduce_weight: bfloat16 [2048, 512], replicated, may hold values from -0.125 to 0.125
- reduce_bias: float32 [512], replicated, may hold values from -3 to 3
- cotangent: bfloat16 [512, 64, 512], P('samp', 'feat'), may hold values from -6 to 6
Outputs:
- layer_output: bfloat16 [512, 64, 512], P('samp', 'feat')
- input_grad: bfloat16 [512, 64, 512], P('samp', 'feat')
- first_gain_grad: float32 [512], P('samp')
- first_shift_grad: float32 [512], P('samp')
- sample_weight_grad: float32 [512, 1536], P('samp')
- sample_bias_grad: float32 [1024], P('samp')
- sample_mixer_grad: float32 [512, 512], P('samp')
- sample_offset_grad: float32 [512], P('samp')
- second_gain_grad: float32 [512], P('samp')
- second_shift_grad: float32 [512], P('samp')
- feature_weight_grad: float32 [512, 1536], P('samp')
- feature_bias_grad: float32 [1024], P('samp')
- feature_mixer_grad: float32 [512, 512], P('samp')
- feature_offset_grad: float32 [512], P('samp')
- third_gain_grad: float32 [512], P('samp')
- third_shift_grad: float32 [512], P('samp')
- expand_weight_grad: float32 [512, 2048], P('samp')
- expand_bias_grad: float32 [2048], P('samp')
- reduce_weight_grad: float32 [2048, 512], P('samp')
- reduce_bias_grad: float32 [512], P('samp')
Inputs may be any that keep to these rules, and one draw needn't show every extreme that they name: `context_flags`: the samples of one index of samp (an aligned block of 64 samples) are all context samples or all query samples; exactly 1 block are context blocks, which ones is drawn. `segment_ids`: every task holds exactly 16 context samples.
All inputs are finite; a program needn't handle non-finite values.
Results may differ from a plain program's by a relative error of at most 0.017.
Values may be sent and summed in bfloat16 or wider, within the bound.
No kernel may reach another device: no remote copies, remote signals or barrier semaphores. Data moves between devices by JAX's collectives and lax.ppermute only.
A program may use at most 256 MiB of HBM per device.

v0:
```python
from functools import partial

import jax
import jax.numpy as jnp
from jax import lax
from jax.sharding import PartitionSpec as P

HEADS = 8
HEAD_DIM = 64


EPS = 1e-05
MASKED = -1000000000.0


def spread_2(block, axis, owner):
    block = jnp.where(lax.axis_index(axis) == owner, block, jnp.zeros_like(block))
    return lax.psum(block, axis)


def layer_norm(values, gain_row, shift_row):
    center = jnp.mean(values, axis=-1, keepdims=True)
    spread = values - center
    variance = jnp.mean(spread * spread, axis=-1, keepdims=True)
    return spread * lax.rsqrt(variance + EPS) * gain_row + shift_row


def apply_weight(active, weight):
    return jnp.einsum("sfd,de->sfe", active, weight, preferred_element_type=jnp.float32)


def input_back(grad_out, weight):
    return jnp.einsum("sfe,de->sfd", grad_out, weight, preferred_element_type=jnp.float32)


def weight_grad(active, grad_out):
    return jnp.einsum("sfd,sfe->de", active, grad_out, preferred_element_type=jnp.float32)


def column_sum(values):
    return jnp.sum(values.astype(jnp.float32), axis=(0, 1))


def project(active, weight, bias_row):
    model_width = active.shape[-1]
    joined = apply_weight(active, weight)
    queries = (joined[..., :model_width] + bias_row[:model_width]).astype(jnp.bfloat16)
    key_part = joined[..., model_width : 2 * model_width].astype(jnp.bfloat16)
    value_part = (joined[..., 2 * model_width :] + bias_row[model_width:]).astype(jnp.bfloat16)
    return (queries, key_part, value_part)


def split_heads(values):
    return values.reshape(values.shape[0], values.shape[1], HEADS, HEAD_DIM)


def join_heads(values):
    return values.reshape(values.shape[0], values.shape[1], HEADS * HEAD_DIM)


def soft_weights(scores):
    top_score = jnp.max(scores, axis=-1, keepdims=True)
    raised = jnp.exp(scores - top_score)
    return raised / jnp.sum(raised, axis=-1, keepdims=True)


def feature_attend(queries, key_part, value_part):
    score_scale = HEAD_DIM ** (-0.5)
    scores = (
        jnp.einsum(
            "sfhd,sghd->shfg",
            split_heads(queries),
            split_heads(key_part),
            preferred_element_type=jnp.float32,
        )
        * score_scale
    )
    probability = soft_weights(scores)
    mixed = jnp.einsum(
        "shfg,sghd->sfhd",
        probability.astype(jnp.bfloat16),
        split_heads(value_part),
        preferred_element_type=jnp.float32,
    )
    return (join_heads(mixed).astype(jnp.bfloat16), probability)


def feature_grads(queries, key_part, value_part, probability, grad_mixed):
    score_scale = HEAD_DIM ** (-0.5)
    grad_heads = split_heads(grad_mixed)
    grad_weights = jnp.einsum(
        "sfhd,sghd->shfg", grad_heads, split_heads(value_part), preferred_element_type=jnp.float32
    )
    inner_sum = jnp.sum(probability * grad_weights, axis=-1, keepdims=True)
    grad_scores = (probability * (grad_weights - inner_sum)).astype(jnp.bfloat16)
    grad_queries = (
        jnp.einsum(
            "shfg,sghd->sfhd",
            grad_scores,
            split_heads(key_part),
            preferred_element_type=jnp.float32,
        )
        * score_scale
    )
    grad_keys = (
        jnp.einsum(
            "shfg,sfhd->sghd", grad_scores, split_heads(queries), preferred_element_type=jnp.float32
        )
        * score_scale
    )
    grad_values = jnp.einsum(
        "shfg,sfhd->sghd",
        probability.astype(jnp.bfloat16),
        grad_heads,
        preferred_element_type=jnp.float32,
    )
    return (join_heads(grad_queries), join_heads(grad_keys), join_heads(grad_values))


def local(
    layer_input,
    segment_ids,
    context_flags,
    first_gain,
    first_shift,
    sample_weight,
    sample_bias,
    sample_mixer,
    sample_offset,
    second_gain,
    second_shift,
    feature_weight,
    feature_bias,
    feature_mixer,
    feature_offset,
    third_gain,
    third_shift,
    expand_weight,
    expand_bias,
    reduce_weight,
    reduce_bias,
    cotangent,
):
    sample_rows = layer_input.shape[0]
    feature_rows = layer_input.shape[1]
    model_width = layer_input.shape[2]
    score_scale = HEAD_DIM ** (-0.5)
    shard_count = lax.axis_size("samp")
    context_shards = shard_count // 8
    total_context = context_shards * sample_rows
    residual_zero = layer_input.astype(jnp.float32)
    normed_one, norm_one_back = jax.vjp(layer_norm, residual_zero, first_gain, first_shift)
    active_one = normed_one.astype(jnp.bfloat16)
    queries_one, keys_one, values_one = project(active_one, sample_weight, sample_bias)
    my_index = lax.axis_index("samp")
    shard_flags = context_flags.reshape(shard_count, sample_rows)[:, 0]
    shard_rank = jnp.cumsum(shard_flags) - 1
    shard_ids = jnp.arange(shard_count, dtype=jnp.int32)
    slot_ids = jnp.arange(context_shards, dtype=jnp.int32)
    root_hits = (shard_rank[None, :] == slot_ids[:, None]) & (shard_flags[None, :] == 1)
    roots = jnp.sum(jnp.where(root_hits, shard_ids[None, :], 0), axis=1)
    context_tasks = jnp.take(segment_ids.reshape(shard_count, sample_rows), roots, axis=0).reshape(
        total_context
    )
    local_tasks = lax.dynamic_slice_in_dim(segment_ids, my_index * sample_rows, sample_rows)
    allowed = local_tasks[:, None] == context_tasks[None, :]
    is_context = shard_flags[my_index] == 1
    own_rank = jnp.maximum(shard_rank[my_index], 0)
    own_block = jnp.concatenate([keys_one, values_one], axis=-1)

    def fetch_rows(step, buffer):
        piece = spread_2(own_block, "samp", roots[step])
        return lax.dynamic_update_slice_in_dim(buffer, piece, step * sample_rows, 0)

    empty_rows = jnp.zeros((total_context, feature_rows, 2 * model_width), jnp.bfloat16)
    fetched = lax.fori_loop(0, context_shards, fetch_rows, empty_rows)
    context_keys = fetched[..., :model_width]
    context_values = fetched[..., model_width:]
    query_heads = split_heads(queries_one)
    key_heads = split_heads(context_keys)
    value_heads = split_heads(context_values)
    scores = (
        jnp.einsum("sfhd,cfhd->fhsc", query_heads, key_heads, preferred_element_type=jnp.float32)
        * score_scale
    )
    sample_prob = soft_weights(jnp.where(allowed[None, None], scores, MASKED))
    sample_weights = sample_prob.astype(jnp.bfloat16)
    mixed_one = join_heads(
        jnp.einsum(
            "fhsc,cfhd->sfhd", sample_weights, value_heads, preferred_element_type=jnp.float32
        )
    ).astype(jnp.bfloat16)
    residual_one = residual_zero + apply_weight(mixed_one, sample_mixer) + sample_offset
    normed_two, norm_two_back = jax.vjp(layer_norm, residual_one, second_gain, second_shift)
    active_two = normed_two.astype(jnp.bfloat16)
    queries_two, keys_two, values_two = project(active_two, feature_weight, feature_bias)
    all_keys, all_values = (
        lax.all_gather(keys_two, "feat", axis=1, tiled=True),
        lax.all_gather(values_two, "feat", axis=1, tiled=True),
    )
    mixed_two, feature_prob = feature_attend(queries_two, all_keys, all_values)
    residual_two = residual_one + apply_weight(mixed_two, feature_mixer) + feature_offset
    normed_three, norm_three_back = jax.vjp(layer_norm, residual_two, third_gain, third_shift)
    active_three = normed_three.astype(jnp.bfloat16)
    expanded = apply_weight(active_three, expand_weight) + expand_bias
    activated, gelu_back = jax.vjp(partial(jax.nn.gelu, approximate=False), expanded)
    hidden = activated.astype(jnp.bfloat16)
    layer_output = (residual_two + apply_weight(hidden, reduce_weight) + reduce_bias).astype(
        jnp.bfloat16
    )
    grad_out = cotangent.astype(jnp.float32)
    grad_branch = cotangent
    reduce_bias_grad = column_sum(grad_branch)
    reduce_weight_grad = weight_grad(hidden, grad_branch)
    grad_hidden = input_back(grad_branch, reduce_weight).astype(jnp.bfloat16)
    grad_expanded = gelu_back(grad_hidden.astype(jnp.float32))[0].astype(jnp.bfloat16)
    expand_bias_grad = column_sum(grad_expanded)
    expand_weight_grad = weight_grad(active_three, grad_expanded)
    grad_norm, third_gain_grad, third_shift_grad = norm_three_back(
        input_back(grad_expanded, expand_weight)
    )
    grad_two = grad_out + grad_norm
    grad_branch = grad_two.astype(jnp.bfloat16)
    feature_offset_grad = column_sum(grad_branch)
    feature_mixer_grad = weight_grad(mixed_two, grad_branch)
    grad_mixed = input_back(grad_branch, feature_mixer).astype(jnp.bfloat16)
    grad_queries, grad_keys, grad_values = feature_grads(
        queries_two, all_keys, all_values, feature_prob, grad_mixed
    )
    own_key_grads, own_value_grads = (
        lax.psum_scatter(grad_keys, "feat", scatter_dimension=1, tiled=True),
        lax.psum_scatter(grad_values, "feat", scatter_dimension=1, tiled=True),
    )
    grad_project = jnp.concatenate(
        [
            grad_queries.astype(jnp.bfloat16),
            own_key_grads.astype(jnp.bfloat16),
            own_value_grads.astype(jnp.bfloat16),
        ],
        axis=-1,
    )
    feature_weight_grad = weight_grad(active_two, grad_project)
    feature_bias_grad = jnp.concatenate(
        [
            column_sum(grad_project[..., :model_width]),
            column_sum(grad_project[..., 2 * model_width :]),
        ]
    )
    grad_norm, second_gain_grad, second_shift_grad = norm_two_back(
        input_back(grad_project, feature_weight)
    )
    grad_one = grad_two + grad_norm
    grad_branch = grad_one.astype(jnp.bfloat16)
    sample_offset_grad = column_sum(grad_branch)
    sample_mixer_grad = weight_grad(mixed_one, grad_branch)
    grad_heads = split_heads(input_back(grad_branch, sample_mixer).astype(jnp.bfloat16))
    grad_weights = jnp.einsum(
        "sfhd,cfhd->fhsc", grad_heads, value_heads, preferred_element_type=jnp.float32
    )
    inner_sum = jnp.sum(sample_prob * grad_weights, axis=-1, keepdims=True)
    grad_scores = (sample_prob * (grad_weights - inner_sum)).astype(jnp.bfloat16)
    grad_queries = (
        join_heads(
            jnp.einsum(
                "fhsc,cfhd->sfhd", grad_scores, key_heads, preferred_element_type=jnp.float32
            )
        )
        * score_scale
    ).astype(jnp.bfloat16)
    key_terms = (
        join_heads(
            jnp.einsum(
                "fhsc,sfhd->cfhd", grad_scores, query_heads, preferred_element_type=jnp.float32
            )
        )
        * score_scale
    )
    value_terms = join_heads(
        jnp.einsum(
            "fhsc,sfhd->cfhd", sample_weights, grad_heads, preferred_element_type=jnp.float32
        )
    )
    term_block = jnp.concatenate([key_terms, value_terms], axis=-1)
    summed_terms = lax.psum_scatter(term_block, "samp", scatter_dimension=0, tiled=True)
    summed_rows = lax.all_gather(summed_terms.astype(jnp.bfloat16), "samp", axis=0, tiled=True)
    own_grads = lax.dynamic_slice_in_dim(summed_rows, own_rank * sample_rows, sample_rows, 0)
    own_grads = jnp.where(is_context, own_grads, jnp.zeros_like(own_grads))
    grad_project = jnp.concatenate([grad_queries, own_grads], axis=-1)
    sample_weight_grad = weight_grad(active_one, grad_project)
    sample_bias_grad = jnp.concatenate(
        [column_sum(grad_queries), column_sum(own_grads[..., model_width:])]
    )
    grad_norm, first_gain_grad, first_shift_grad = norm_one_back(
        input_back(grad_project, sample_weight)
    )
    input_grad = (grad_one + grad_norm).astype(jnp.bfloat16)
    summed = lax.psum(
        (
            first_gain_grad,
            first_shift_grad,
            sample_weight_grad,
            sample_bias_grad,
            sample_mixer_grad,
            sample_offset_grad,
            second_gain_grad,
            second_shift_grad,
            feature_weight_grad,
            feature_bias_grad,
            feature_mixer_grad,
            feature_offset_grad,
            third_gain_grad,
            third_shift_grad,
            expand_weight_grad,
            expand_bias_grad,
            reduce_weight_grad,
            reduce_bias_grad,
        ),
        "feat",
    )
    shares = (
        lax.psum_scatter(summed[0], "samp", scatter_dimension=0, tiled=True),
        lax.psum_scatter(summed[1], "samp", scatter_dimension=0, tiled=True),
        lax.psum_scatter(summed[2], "samp", scatter_dimension=0, tiled=True),
        lax.psum_scatter(summed[3], "samp", scatter_dimension=0, tiled=True),
        lax.psum_scatter(summed[4], "samp", scatter_dimension=0, tiled=True),
        lax.psum_scatter(summed[5], "samp", scatter_dimension=0, tiled=True),
        lax.psum_scatter(summed[6], "samp", scatter_dimension=0, tiled=True),
        lax.psum_scatter(summed[7], "samp", scatter_dimension=0, tiled=True),
        lax.psum_scatter(summed[8], "samp", scatter_dimension=0, tiled=True),
        lax.psum_scatter(summed[9], "samp", scatter_dimension=0, tiled=True),
        lax.psum_scatter(summed[10], "samp", scatter_dimension=0, tiled=True),
        lax.psum_scatter(summed[11], "samp", scatter_dimension=0, tiled=True),
        lax.psum_scatter(summed[12], "samp", scatter_dimension=0, tiled=True),
        lax.psum_scatter(summed[13], "samp", scatter_dimension=0, tiled=True),
        lax.psum_scatter(summed[14], "samp", scatter_dimension=0, tiled=True),
        lax.psum_scatter(summed[15], "samp", scatter_dimension=0, tiled=True),
        lax.psum_scatter(summed[16], "samp", scatter_dimension=0, tiled=True),
        lax.psum_scatter(summed[17], "samp", scatter_dimension=0, tiled=True),
    )
    return (
        layer_output,
        input_grad,
        shares[0],
        shares[1],
        shares[2],
        shares[3],
        shares[4],
        shares[5],
        shares[6],
        shares[7],
        shares[8],
        shares[9],
        shares[10],
        shares[11],
        shares[12],
        shares[13],
        shares[14],
        shares[15],
        shares[16],
        shares[17],
    )


def solution(mesh):
    return jax.shard_map(
        local,
        mesh=mesh,
        in_specs=(
            P("samp", "feat", None),
            P(),
            P(),
            P(),
            P(),
            P(),
            P(),
            P(),
            P(),
            P(),
            P(),
            P(),
            P(),
            P(),
            P(),
            P(),
            P(),
            P(),
            P(),
            P(),
            P(),
            P("samp", "feat", None),
        ),
        out_specs=(
            P("samp", "feat", None),
            P("samp", "feat", None),
            P("samp"),
            P("samp"),
            P("samp", None),
            P("samp"),
            P("samp", None),
            P("samp"),
            P("samp"),
            P("samp"),
            P("samp", None),
            P("samp"),
            P("samp", None),
            P("samp"),
            P("samp"),
            P("samp"),
            P("samp", None),
            P("samp"),
            P("samp", None),
            P("samp"),
        ),
        check_vma=False,
    )
```

profile of v0, /device:TPU:0, one launch (start us, length us, event | category | flops | bytes accessed | tf_op | source)
XLA Modules:
  0.0 1231.2 jit_solution(3453029801898814704)
XLA Ops:
  22.1 3.9 fusion.41
  33.9 98.7 %all-reduce.18.cloned.1.call-done = bf16[64,16,1024]{2,1,0:T(8,128)(2,1)} async-done(((bf16[64,16,1024]{2,1,0:T(8,128)(2,1)}), bf16[64,16,1024]{2,1,0:T(8,128)(2,1)}) %all-reduce.18.cloned.1.call-update) | async-done | bytes 2097168 | tf_op jit(solution)/shard_map/while/body/eval_jaxpr/psum | solution.py:18
  135.7 3.9 reshape.296
  139.5 3.9 reshape.293
  143.4 4.0 fusion.68
  165.5 3.9 fusion.40
  171.7 28.1 %all-gather.6.cloned.1.call-done = bf16[64,64,512]{2,1,0:T(8,128)(2,1)} async-done(((bf16[64,16,512]{2,1,0:T(8,128)(2,1)}), bf16[64,64,512]{2,1,0:T(8,128)(2,1)}) %all-gather.6.cloned.1.call-update) | async-done | bytes 4194320 | tf_op jit(solution)/shard_map/all_gather | solution.py:198
  199.8 11.4 reshape.299
  211.1 8.5 fusion.21
  224.9 11.6 all-gather.4.cloned.1.call-done
  236.4 11.2 reshape.297
  247.6 19.2 %convert_bitcast_fusion = bf16[64,16,8,64]{3,1,2,0:T(8,128)(2,1)} fusion(bf16[64,64,8,64]{3,2,1,0:T(8,128)(2,1)} %reshape.297, f32[64,8,16]{2,1,0:T(8,128)S(1)} %get-tuple-element.115, f32[64,8,16,64]{3,2,1,0:T(8,128)} %copy-done.10), kind=kOutput, calls=%fused_computation.111 | convolution fusion | flops 70262848 | bytes 7372800 | tf_op jit(solution)/shard_map/shfg,sghd->sfhd/dot_general | solution.py:79
  277.3 21.9 %multiply_convert_fusion = (bf16[64,16,2048]{2,1,0:T(8,128)(2,1)}, f32[64,16,2048]{2,1,0:T(8,128)S(1)}, f32[64,16,2048]{2,1,0:T(8,128)}) fusion(f32[2048]{0:T(1024)S(1)} %copy-done.73, bf16[512,2048]{1,0:T(8,128)(2,1)S(1)} %copy-done, f32[64,16,512]{2,1,0:T(8,128)S(1)} %get-tuple-element.118, f32[512]{0:T(512)S(1)} %copy-done.75, f32[512]{0:T(512)S(1)} %copy-done.65, ...), kind=kOutput, calls=%fused_computation.15 | convolution fusion | flops 2288517120 | bytes 25186304 | tf_op jit(solution)/shard_map/sfd,de->sfe/dot_general | solution.py:29
  299.2 7.9 convert_reduce_fusion
  318.5 23.3 %fusion.62 = f32[64,8,64,64]{3,2,1,0:T(8,128)} fusion(bf16[64,16,8,64]{3,2,1,0:T(8,128)(2,1)S(1)} %reshape.300, f32[64,8,16]{2,1,0:T(8,128)S(1)} %get-tuple-element.115, f32[64,8,16,64]{3,2,1,0:T(8,128)} %copy-done.10), kind=kOutput, calls=%fused_computation.126 | convolution fusion | flops 69738560 | bytes 11567104 | tf_op jit(solution)/shard_map/shfg,sfhd->sghd/dot_general | solution.py:111
  341.8 12.7 %copy.199 = f32[64,64,512]{2,1,0:T(8,128)} copy(f32[64,64,512]{1,2,0:T(8,128)} %bitcast.119) | data formatting | bytes 16777216 | tf_op jit(solution)/shard_map/reshape | solution.py:58
  354.6 9.1 multiply_reduce_fusion.1
  366.2 7.4 convolution_multiply_fusion
  373.7 12.9 %copy.197 = f32[64,64,512]{2,1,0:T(8,128)} copy(f32[64,64,512]{1,2,0:T(8,128)} %bitcast.116) | data formatting | bytes 16777216 | tf_op jit(solution)/shard_map/reshape | solution.py:58
  388.3 6.3 convert_reduce_fusion.1
  397.4 29.0 %reduce-scatter.12.cloned.1.call-done = f32[64,16,512]{2,1,0:T(8,128)} async-done(((f32[64,64,512]{2,1,0:T(8,128)}), f32[64,16,512]{2,1,0:T(8,128)}) %reduce-scatter.12.cloned.1.call-update) | async-done | bytes 2097168 | tf_op jit(solution)/shard_map/reduce_scatter | solution.py:232
  429.8 71.0 %reduce-scatter.10.cloned.1.call-done = f32[64,16,512]{2,1,0:T(8,128)} async-done(((f32[64,64,512]{2,1,0:T(8,128)}), f32[64,16,512]{2,1,0:T(8,128)}) %reduce-scatter.10.cloned.1.call-update) | async-done | bytes 2097168 | tf_op jit(solution)/shard_map/reduce_scatter | solution.py:231
  502.7 4.8 fusion.114
  515.9 7.8 multiply_reduce_fusion
  526.9 4.4 copy.211
  531.4 4.9 multiply_convert_fusion.2
  537.6 4.4 copy.208
  542.0 4.8 mul.305
  546.7 4.7 pad_maximum_fusion
  551.5 88.2 %reduce-scatter.14.cloned.1.call-done = f32[8,16,1024]{2,1,0:T(8,128)} async-done(((f32[64,16,1024]{2,1,0:T(8,128)}), f32[8,16,1024]{2,1,0:T(8,128)}) %reduce-scatter.14.cloned.1.call-update) | async-done | bytes 524304 | tf_op jit(solution)/shard_map/reduce_scatter | solution.py:284
  644.6 6.8 convolution_bitcast_fusion.2
  652.1 7.3 convolution_bitcast_fusion.3
  659.7 4.3 convolution_bitcast_fusion.5
  664.1 5.2 convolution_bitcast_fusion
  670.9 3.8 convert_reduce_fusion.2
  678.1 13.6 %all-gather.8.cloned.1.call-done = bf16[64,16,1024]{2,1,0:T(8,128)(2,1)} async-done(((bf16[8,16,1024]{2,1,0:T(8,128)(2,1)}), bf16[64,16,1024]{2,1,0:T(8,128)(2,1)}) %all-gather.8.cloned.1.call-update) | async-done | bytes 2097168 | tf_op jit(solution)/shard_map/all_gather | solution.py:285
  694.1 3.7 convolution_bitcast_fusion.1
  701.1 6.2 add_convert_fusion.1
  708.8 4.2 fusion.115
  713.0 44.5 %reduce-scatter.22.cloned.1.call-done = f32[64,512]{1,0:T(8,128)} async-done(((f32[512,512]{1,0:T(8,128)}), f32[64,512]{1,0:T(8,128)}) %reduce-scatter.22.cloned.1.call-update) | async-done | bytes 131088 | tf_op jit(solution)/shard_map/reduce_scatter | solution.py:331
  757.5 90.8 %reduce-scatter.26.cloned.1.call-done = f32[256,512]{1,0:T(8,128)} async-done(((f32[2048,512]{1,0:T(8,128)}), f32[256,512]{1,0:T(8,128)}) %reduce-scatter.26.cloned.1.call-update) | async-done | bytes 524304 | tf_op jit(solution)/shard_map/reduce_scatter | solution.py:337
  848.3 91.6 %reduce-scatter.24.cloned.1.call-done = f32[64,2048]{1,0:T(8,128)} async-done(((f32[512,2048]{1,0:T(8,128)}), f32[64,2048]{1,0:T(8,128)}) %reduce-scatter.24.cloned.1.call-update) | async-done | bytes 524304 | tf_op jit(solution)/shard_map/reduce_scatter | solution.py:335
  939.9 66.6 %reduce-scatter.18.cloned.1.call-done = f32[64,512]{1,0:T(8,128)} async-done(((f32[512,512]{1,0:T(8,128)}), f32[64,512]{1,0:T(8,128)}) %reduce-scatter.18.cloned.1.call-update) | async-done | bytes 131088 | tf_op jit(solution)/shard_map/reduce_scatter | solution.py:325
  1006.6 77.2 %reduce-scatter.20.cloned.1.call-done = f32[64,1536]{1,0:T(8,128)} async-done(((f32[512,1536]{1,0:T(8,128)}), f32[64,1536]{1,0:T(8,128)}) %reduce-scatter.20.cloned.1.call-update) | async-done | bytes 393232 | tf_op jit(solution)/shard_map/reduce_scatter | solution.py:329
  1083.8 77.4 %reduce-scatter.16.cloned.1.call-done = f32[64,1536]{1,0:T(8,128)} async-done(((f32[512,1536]{1,0:T(8,128)}), f32[64,1536]{1,0:T(8,128)}) %reduce-scatter.16.cloned.1.call-update) | async-done | bytes 393232 | tf_op jit(solution)/shard_map/reduce_scatter | solution.py:323
  1162.5 35.6 %all-reduce.12 = (f32[512]{0:T(512)S(1)}, f32[512]{0:T(512)S(1)}, f32[1024]{0:T(1024)S(1)}, f32[512]{0:T(512)S(1)}, f32[512]{0:T(512)S(1)}, /*index=5*/f32[512]{...) all-reduce(f32[512]{0:T(512)S(1)} %get-tuple-element.50, ...), channel_id=5, replica_groups=mesh['samp'=8,'feat'=4] {'samp'}, use_global_device_ids=true, to_apply=%region_26.27.clone | all-reduce | flops 8704 | bytes 69632
  1199.0 6.9 all-reduce.13
  1208.8 6.9 all-reduce.20.cloned.1.call-done
  (286 shorter events, 124.9 us)
Async XLA Ops:
  7.2 269.8 %copy-start = (bf16[512,2048]{1,0:T(8,128)(2,1)S(1)}, bf16[512,2048]{1,0:T(8,128)(2,1)}, u32[]{:S(2)}) copy-start(bf16[512,2048]{1,0:T(8,128)(2,1)} %param.39) | copy-start | bytes 6291460
  7.2 7.1 copy-start.12
  7.2 7.1 copy-start.53
  7.2 7.1 copy-start.79
  7.2 125.4 %all-reduce.18.cloned.1.call-start = ((), (), s32[]{:S(2)}) async-start(), calls=%async_computation.9 | async-start | bytes 4194304 | tf_op jit(solution)/shard_map/while/body/eval_jaxpr/psum | solution.py:18
  11.9 5.7 copy-start.37
  14.4 3.3 copy-start.42
  22.1 3.9 copy-start.21
  27.9 171.9 %all-gather.6.cloned.1.call-start = ((), (), s32[]{:S(2)}) async-start(), calls=%async_computation.11 | async-start | bytes 5242880 | tf_op jit(solution)/shard_map/all_gather | solution.py:198
  151.8 3.4 copy-start.74
  157.4 4.1 copy-start.2
  157.5 4.1 copy-start.35
  165.4 71.0 %all-gather.4.cloned.1.call-start = ((), (), s32[]{:S(2)}) async-start(), calls=%async_computation.10 | async-start | bytes 5242880 | tf_op jit(solution)/shard_map/all_gather | solution.py:199
  169.4 257.0 %reduce-scatter.12.cloned.1.call-start = ((), (), s32[]{:S(2)}) async-start(), calls=%async_computation.13 | async-start | bytes 10485760 | tf_op jit(solution)/shard_map/reduce_scatter | solution.py:232
  276.5 34.0 %copy-start.5 = (f32[64,16,512]{2,1,0:T(8,128)}, f32[64,16,512]{2,1,0:T(8,128)S(1)}, u32[]{:S(2)}) copy-start(f32[64,16,512]{2,1,0:T(8,128)S(1)} %get-tuple-element.118) | copy-start | bytes 6291460
  277.3 21.9 %copy-start.26 = (bf16[64,16,512]{2,1,0:T(8,128)(2,1)S(1)}, bf16[64,16,512]{2,1,0:T(8,128)(2,1)}, u32[]{:S(2)}) copy-start(bf16[64,16,512]{2,1,0:T(8,128)(2,1)} %param.43) | copy-start | bytes 3145732
  277.3 21.9 %copy-start.70 = (bf16[2048,512]{1,0:T(8,128)(2,1)S(1)}, bf16[2048,512]{1,0:T(8,128)(2,1)}, u32[]{:S(2)}) copy-start(bf16[2048,512]{1,0:T(8,128)(2,1)} %param.41) | copy-start | bytes 6291460
  307.1 3.3 copy-start.83
  354.5 146.2 %reduce-scatter.10.cloned.1.call-start = ((), (), s32[]{:S(2)}) async-start(), calls=%async_computation.12 | async-start | bytes 10485760 | tf_op jit(solution)/shard_map/reduce_scatter | solution.py:231
  354.6 9.1 copy-start.11
  366.2 7.4 copy-start.14
  386.6 253.2 %reduce-scatter.14.cloned.1.call-start = ((), (), s32[]{:S(2)}) async-start(), calls=%async_computation.14 | async-start | bytes 4718592 | tf_op jit(solution)/shard_map/reduce_scatter | solution.py:284
  426.4 76.2 %copy-start.36 = (f32[64,16]{1,0:T(8,128)S(1)}, f32[64,16]{1,0:T(8,128)}, u32[]{:S(2)}) copy-start(f32[64,16]{1,0:T(8,128)} %copy-done.35) | copy-start | bytes 12292
  426.4 76.2 %copy-start.59 = (f32[512]{0:T(512)S(1)}, f32[512]{0:T(512)}, u32[]{:S(2)}) copy-start(f32[512]{0:T(512)} %param.31) | copy-start | bytes 6148
  429.8 72.9 %copy-start.3 = (f32[64,16,512]{2,1,0:T(8,128)S(1)}, f32[64,16,512]{2,1,0:T(8,128)}, u32[]{:S(2)}) copy-start(f32[64,16,512]{2,1,0:T(8,128)} %copy-done.2) | copy-start | bytes 6291460
  502.6 4.8 copy-start.31
  502.6 4.8 copy-start.47
  502.6 4.8 copy-start.45
  509.2 3.7 copy-start.72
  515.9 7.8 copy-start.25
  515.9 7.8 copy-start.28
  531.4 4.9 copy-start.9
  551.5 90.1 %copy-start.23 = (bf16[64,16,512]{2,1,0:T(8,128)(2,1)S(1)}, bf16[64,16,512]{2,1,0:T(8,128)(2,1)}, u32[]{:S(2)}) copy-start(bf16[64,16,512]{2,1,0:T(8,128)(2,1)} %copy-done.22) | copy-start | bytes 3145732
  551.5 140.2 %all-gather.8.cloned.1.call-start = ((), (), s32[]{:S(2)}) async-start(), calls=%async_computation.15 | async-start | bytes 2359296 | tf_op jit(solution)/shard_map/all_gather | solution.py:285
  641.5 116.0 %reduce-scatter.22.cloned.1.call-start = ((), (), s32[]{:S(2)}) async-start(), calls=%async_computation.19 | async-start | bytes 1179648 | tf_op jit(solution)/shard_map/reduce_scatter | solution.py:331
  644.5 203.8 %reduce-scatter.26.cloned.1.call-start = ((), (), s32[]{:S(2)}) async-start(), calls=%async_computation.21 | async-start | bytes 4718592 | tf_op jit(solution)/shard_map/reduce_scatter | solution.py:337
  651.4 288.5 %reduce-scatter.24.cloned.1.call-start = ((), (), s32[]{:S(2)}) async-start(), calls=%async_computation.20 | async-start | bytes 4718592 | tf_op jit(solution)/shard_map/reduce_scatter | solution.py:335
  659.4 4.8 copy-start.30
  659.4 4.7 copy-start.78
  659.4 347.1 %reduce-scatter.18.cloned.1.call-start = ((), (), s32[]{:S(2)}) async-start(), calls=%async_computation.17 | async-start | bytes 1179648 | tf_op jit(solution)/shard_map/reduce_scatter | solution.py:325
  664.1 419.7 %reduce-scatter.20.cloned.1.call-start = ((), (), s32[]{:S(2)}) async-start(), calls=%async_computation.18 | async-start | bytes 3538944 | tf_op jit(solution)/shard_map/reduce_scatter | solution.py:329
  669.4 491.8 %reduce-scatter.16.cloned.1.call-start = ((), (), s32[]{:S(2)}) async-start(), calls=%async_computation.16 | async-start | bytes 3538944 | tf_op jit(solution)/shard_map/reduce_scatter | solution.py:323
  697.8 517.9 %all-reduce.20.cloned.1.call-start = ((), (), s32[]{:S(2)}) async-start(), calls=%async_computation.22 | async-start | bytes 4194304 | tf_op jit(solution)/shard_map/psum | solution.py:297
  701.1 6.3 copy-start.57
  708.8 4.2 copy-start.49
  1215.7 6.8 copy-start.40
  1215.7 7.6 copy-start.39
  1215.7 8.4 copy-start.1
  (50 other events, 89.2 us)
Sparse Core Ops, SparseCore 0:
  28.0 104.5 all-reduce.17
  165.5 34.1 all-gather.5
  201.9 34.4 all-gather.3
  354.6 71.7 reduce-scatter.11
  429.0 71.6 reduce-scatter.9
  551.6 88.0 reduce-scatter.13
  642.7 49.0 all-gather.7
  695.5 61.9 reduce-scatter.21
  761.2 87.0 reduce-scatter.25
  852.2 87.6 reduce-scatter.23
  943.3 63.1 reduce-scatter.17
  1010.4 73.3 reduce-scatter.19
  1087.8 73.3 reduce-scatter.15
  1164.0 51.6 all-reduce.19
where the time goes:
time: 1240 us; the launch traced here: 1230 us
  waiting for transfers between devices  795 us (64%)
  matrix products  188 us (15%)
  local copies, waits for them, and re-layouts  131 us (11%)
  other arithmetic  52.2 us (4%)
  blocking collectives  42.5 us (3%)
  between operations  20 us (2%)
    psum x1, waiting for transfers between devices, spread_2(): return lax.psum(block, axis)  98.7 us
    reduce_scatter x1, waiting for transfers between devices, local(): lax.psum_scatter(summed[14], 'samp', scatter_dimension=0, tiled=True)  91.6 us
    reduce_scatter x1, waiting for transfers between devices, local(): lax.psum_scatter(summed[16], 'samp', scatter_dimension=0, tiled=True)  90.8 us
    reduce_scatter x1, waiting for transfers between devices, local(): lax.psum_scatter(term_block, 'samp', scatter_dimension=0, tiled=True)  88.2 us
    reduce_scatter x1, waiting for transfers between devices, local(): lax.psum_scatter(summed[2], 'samp', scatter_dimension=0, tiled=True)  77.4 us
    reduce_scatter x1, waiting for transfers between devices, local(): lax.psum_scatter(summed[8], 'samp', scatter_dimension=0, tiled=True)  77.2 us
    reduce_scatter x1, waiting for transfers between devices, local(): lax.psum_scatter(grad_keys, 'feat', scatter_dimension=1, tiled=True)  71 us
    reduce_scatter x1, waiting for transfers between devices, local(): lax.psum_scatter(summed[4], 'samp', scatter_dimension=0, tiled=True)  66.6 us
  transfers between devices with their start and end apart: 14, of which 14 were waited for; matrix products, arithmetic and copies ran while one was open for 11% of the time, Pallas kernels for 0%

commit v1 on v0

--- a/solution.py
+++ b/solution.py
@@ -3,14 +3,539 @@
 import jax
 import jax.numpy as jnp
 from jax import lax
+from jax.experimental import pallas as pl
+from jax.experimental.pallas import tpu as pltpu
 from jax.sharding import PartitionSpec as P
 
 HEADS = 8
 HEAD_DIM = 64
-
-
 EPS = 1e-05
 MASKED = -1000000000.0
+SCALE = HEAD_DIM ** (-0.5)
+QUAD = 4 * HEAD_DIM
+BF = jnp.bfloat16
+F32 = jnp.float32
+VMEM_LIMIT = 56 << 20
+
+
+def mm(a, b, ca=1, cb=0):
+    return lax.dot_general(a, b, (((ca,), (cb,)), ((), ())), preferred_element_type=F32)
+
+
+def norm_parts(values):
+    center = jnp.mean(values, axis=-1, keepdims=True)
+    spread = values - center
+    variance = jnp.mean(spread * spread, axis=-1, keepdims=True)
+    inverse = lax.rsqrt(variance + EPS)
+    return spread * inverse, inverse
+
+
+def norm_back(grad, unit, inverse, gain):
+    scaled = grad * gain
+    first = jnp.mean(scaled, axis=-1, keepdims=True)
+    second = jnp.mean(scaled * unit, axis=-1, keepdims=True)
+    return (scaled - first - unit * second) * inverse
+
+
+def lane_ids(rows):
+    return lax.broadcasted_iota(jnp.int32, (rows, 128), 1)
+
+
+def group_reduce(values, op, fill):
+    rows = values.shape[0]
+    low = lane_ids(rows) < HEAD_DIM
+    outs = []
+    for t in range(values.shape[1] // 128):
+        tile = values[:, t * 128 : (t + 1) * 128]
+        left = op(jnp.where(low, tile, fill), axis=1, keepdims=True)
+        right = op(jnp.where(low, fill, tile), axis=1, keepdims=True)
+        outs.append(jnp.where(low, left, right))
+    return jnp.concatenate(outs, axis=1)
+
+
+def head_masks(dtype):
+    lanes = lax.broadcasted_iota(jnp.int32, (1, QUAD), 1) // HEAD_DIM
+    return [jnp.where(lanes == h, 1.0, 0.0).astype(dtype) for h in range(4)]
+
+
+def stack_heads(part, masks):
+    return jnp.concatenate([part * m for m in masks], axis=0)
+
+
+def pick_heads(stacked, masks):
+    rows = stacked.shape[0] // 4
+    total = stacked[:rows] * masks[0]
+    for h in range(1, 4):
+        total = total + stacked[h * rows : (h + 1) * rows] * masks[h]
+    return total
+
+
+def attend(q, k, v, masks, allow):
+    outs, probs = [], []
+    for quad in range(2):
+        cols = slice(quad * QUAD, (quad + 1) * QUAD)
+        scores = mm(q[:, cols], stack_heads(k[:, cols], masks), 1, 1)
+        if allow is not None:
+            scores = jnp.where(allow, scores, MASKED)
+        raised = jnp.exp(scores - group_reduce(scores, jnp.max, -jnp.inf))
+        prob = raised / group_reduce(raised, jnp.sum, 0.0)
+        outs.append(mm(prob.astype(BF), stack_heads(v[:, cols], masks)))
+        probs.append(prob)
+    return jnp.concatenate(outs, axis=1), jnp.concatenate(probs, axis=1)
+
+
+def attend_back(q, k, v, prob, grad, masks, masks32):
+    dqs, dks, dvs = [], [], []
+    for quad in range(2):
+        cols = slice(quad * QUAD, (quad + 1) * QUAD)
+        p, g = prob[:, cols], grad[:, cols]
+        back = mm(g, stack_heads(v[:, cols], masks), 1, 1)
+        inner = group_reduce(p * back, jnp.sum, 0.0)
+        gs = (p * (back - inner)).astype(BF)
+        dqs.append(mm(gs, stack_heads(k[:, cols], masks)) * SCALE)
+        dks.append(pick_heads(mm(gs, q[:, cols], 0, 0), masks32))
+        dvs.append(pick_heads(mm(p.astype(BF), g, 0, 0), masks32))
+    join = lambda parts: jnp.concatenate(parts, axis=1).astype(BF)
+    return join(dqs), join(dks), join(dvs)
+
+
+def swap_matrix(n):
+    r = lax.broadcasted_iota(jnp.int32, (n, n), 0)
+    c = lax.broadcasted_iota(jnp.int32, (n, n), 1)
+    return jnp.where((r // 16 == c % 16) & (r % 16 == c // 16), 1.0, 0.0).astype(BF)
+
+
+def swap(matrix, values):
+    return mm(matrix, values).astype(BF)
+
+
+def gelu_parts(u):
+    cdf = 0.5 * (1.0 + lax.erf(u * (2.0**-0.5)))
+    density = jnp.exp(u * u * -0.5) * 0.3989422804014327
+    return cdf, density
+
+
+def col_sum(values):
+    return jnp.sum(values.astype(F32), axis=0, keepdims=True)
+
+
+def forward_one(
+    me_ref, x_ref, c_ref, allow_ref, gain_ref, shift_ref, w_ref, b_ref,
+    o_ref, q_ref, k_ref, v_ref, p_ref, o_scr,
+):
+    me = me_ref[0]
+    gain, shift = gain_ref[...], shift_ref[...]
+    matrix = swap_matrix(256)
+    for d in range(4):
+        unit, _ = norm_parts(x_ref[d ^ me].astype(F32))
+        act = swap(matrix, (unit * gain + shift).astype(BF))
+        q = (mm(act, w_ref[:, :512]) + b_ref[:, :512]).astype(BF) * SCALE
+        q_ref[:, d] = q.astype(BF).reshape(16, 16, 512)
+        unit, _ = norm_parts(c_ref[d].astype(F32))
+        act = swap(matrix, (unit * gain + shift).astype(BF))
+        kv = mm(act, w_ref[:, 512:])
+        k_ref[:, d] = kv[:, :512].astype(BF).reshape(16, 16, 512)
+        v_ref[:, d] = (kv[:, 512:] + b_ref[:, 512:]).astype(BF).reshape(16, 16, 512)
+    masks = head_masks(BF)
+    allow = allow_ref[...] > 0.5
+
+    def body(i, carry):
+        for j in range(2):
+            f = i * 2 + j
+            q, k, v = (r[f].reshape(64, 512) for r in (q_ref, k_ref, v_ref))
+            out, prob = attend(q, k, v, masks, allow)
+            o_scr[f] = out.astype(BF).reshape(4, 16, 512)
+            p_ref[f] = prob
+        return carry
+
+    lax.fori_loop(0, 8, body, 0)
+    for d in range(4):
+        o_ref[d] = swap(matrix, o_scr[:, d].reshape(256, 512))
+
+
+def middle(
+    o1_ref, x_ref, cot_ref,
+    wm1_ref, off1_ref, g2_ref, s2_ref, wf_ref, bf_ref, wm2_ref, off2_ref,
+    g3_ref, s3_ref, we_ref, be_ref, wr_ref, br_ref,
+    out_ref, gb1_ref, a2_ref, dqkv_ref, o2_ref, gb2_ref, a3_ref, gu_ref, hid_ref, gb3_ref,
+    vec_ref, bias_ref,
+):
+    samples = 4
+
+    def gather(ref):
+        return jnp.concatenate(
+            [ref[d, s * 16 : (s + 1) * 16] for s in range(samples) for d in range(4)], axis=0
+        )
+
+    def scatter(ref, values):
+        for s in range(samples):
+            for d in range(4):
+                at = (s * 4 + d) * 16
+                ref[d, s * 16 : (s + 1) * 16] = values[at : at + 16]
+
+    masks, masks32 = head_masks(BF), head_masks(F32)
+    o1, cot = gather(o1_ref), gather(cot_ref)
+    gb3_ref[...] = cot
+    r1 = gather(x_ref).astype(F32) + mm(o1, wm1_ref[...]) + off1_ref[...]
+    unit2, inv2 = norm_parts(r1)
+    act2 = (unit2 * g2_ref[...] + s2_ref[...]).astype(BF)
+    a2_ref[...] = act2
+    qkv = mm(act2, wf_ref[...])
+    q = (qkv[:, :512] + bf_ref[:, :512]).astype(BF) * jnp.asarray(SCALE, BF)
+    k = qkv[:, 512:1024].astype(BF)
+    v = (qkv[:, 1024:] + bf_ref[:, 512:]).astype(BF)
+    parts = []
+    for s in range(samples):
+        rows = slice(s * 64, (s + 1) * 64)
+        parts.append(attend(q[rows], k[rows], v[rows], masks, None))
+    o2 = jnp.concatenate([part[0] for part in parts], axis=0).astype(BF)
+    o2_ref[...] = o2
+    r2 = r1 + mm(o2, wm2_ref[...]) + off2_ref[...]
+    unit3, inv3 = norm_parts(r2)
+    act3 = (unit3 * g3_ref[...] + s3_ref[...]).astype(BF)
+    a3_ref[...] = act3
+    out = r2 + br_ref[...]
+    back = None
+    bias = []
+    for b in range(4):
+        cols = slice(b * 512, (b + 1) * 512)
+        u = mm(act3, we_ref[:, cols]) + be_ref[:, cols]
+        cdf, density = gelu_parts(u)
+        hidden = (u * cdf).astype(BF)
+        hid_ref[:, cols] = hidden
+        out = out + mm(hidden, wr_ref[cols, :])
+        gh = mm(cot, wr_ref[cols, :], 1, 1).astype(BF).astype(F32)
+        gu = (gh * (cdf + u * density)).astype(BF)
+        gu_ref[:, cols] = gu
+        bias.append(col_sum(gu))
+        term = mm(gu, we_ref[:, cols], 1, 1)
+        back = term if back is None else back + term
+    scatter(out_ref, out.astype(BF))
+    vecs = [col_sum(back * unit3), col_sum(back)]
+    gr2 = cot.astype(F32) + norm_back(back, unit3, inv3, g3_ref[...])
+    gb2 = gr2.astype(BF)
+    gb2_ref[...] = gb2
+    go2 = mm(gb2, wm2_ref[...], 1, 1).astype(BF)
+    grads = []
+    for s in range(samples):
+        rows = slice(s * 64, (s + 1) * 64)
+        grads.append(
+            jnp.concatenate(
+                attend_back(q[rows], k[rows], v[rows], parts[s][1], go2[rows], masks, masks32),
+                axis=1,
+            )
+        )
+    dqkv = jnp.concatenate(grads, axis=0)
+    dqkv_ref[...] = dqkv
+    back = mm(dqkv, wf_ref[...], 1, 1)
+    vecs += [col_sum(back * unit2), col_sum(back)]
+    gr1 = gr2 + norm_back(back, unit2, inv2, g2_ref[...])
+    scatter(gb1_ref, gr1.astype(BF))
+    vecs += [col_sum(gb2), col_sum(cot), col_sum(dqkv[:, :512]), col_sum(dqkv[:, 1024:])]
+
+    @pl.when(pl.program_id(0) == 0)
+    def _():
+        vec_ref[...] = jnp.zeros_like(vec_ref)
+        bias_ref[...] = jnp.zeros_like(bias_ref)
+
+    vec_ref[...] += jnp.concatenate(vecs, axis=0)
+    bias_ref[...] += jnp.concatenate(bias, axis=1)
+
+
+def backward_one(
+    me_ref, gb1_ref, x_ref, c_ref, q_ref, k_ref, v_ref, p_ref, gain_ref, shift_ref, w_ref, wm_ref,
+    base_ref, term_ref, act_ref, dq_ref, cact_ref, dkv_ref, vec_ref,
+    go_scr, dq_scr, dkv_scr,
+):
+    me = me_ref[0]
+    gain, shift = gain_ref[...], shift_ref[...]
+    matrix = swap_matrix(256)
+    masks, masks32 = head_masks(BF), head_masks(F32)
+    for d in range(4):
+        go = mm(gb1_ref[d], wm_ref[...], 1, 1).astype(BF)
+        go_scr[:, d] = swap(matrix, go).reshape(16, 16, 512)
+
+    def body(i, carry):
+        for j in range(2):
+            f = i * 2 + j
+            q, k, v, go = (r[f].reshape(64, 512) for r in (q_ref, k_ref, v_ref, go_scr))
+            dq, dk, dv = attend_back(q, k, v, p_ref[f], go, masks, masks32)
+            dq_scr[f] = dq.reshape(4, 16, 512)
+            dkv_scr[f] = jnp.concatenate([dk, dv], axis=1).reshape(4, 16, 1024)
+        return carry
+
+    lax.fori_loop(0, 8, body, 0)
+    gain_sum = jnp.zeros((1, 512), F32)
+    shift_sum, off_sum, q_sum, v_sum = gain_sum, gain_sum, gain_sum, gain_sum
+    for d in range(4):
+        unit, inverse = norm_parts(x_ref[d ^ me].astype(F32))
+        act_ref[d] = (unit * gain + shift).astype(BF)
+        dq = swap(matrix, dq_scr[:, d].reshape(256, 512))
+        dq_ref[d] = dq
+        back = mm(dq, w_ref[:, :512], 1, 1)
+        base_ref[d] = gb1_ref[d].astype(F32) + norm_back(back, unit, inverse, gain)
+        gain_sum += col_sum(back * unit)
+        shift_sum += col_sum(back)
+        off_sum += col_sum(gb1_ref[d])
+        q_sum += col_sum(dq)
+        unit, inverse = norm_parts(c_ref[d].astype(F32))
+        cact_ref[d] = (unit * gain + shift).astype(BF)
+        dkv = swap(matrix, dkv_scr[:, d].reshape(256, 1024))
+        dkv_ref[d] = dkv
+        back = mm(dkv, w_ref[:, 512:], 1, 1)
+        term_ref[d] = back.astype(BF)
+        gain_sum += col_sum(back * unit)
+        shift_sum += col_sum(back)
+        v_sum += col_sum(dkv[:, 512:])
+    zero = jnp.zeros((1, 512), F32)
+    vec_ref[...] = jnp.concatenate(
+        [gain_sum, shift_sum, off_sum, q_sum, v_sum, zero, zero, zero], axis=0
+    )
+
+
+def finish(
+    me_ref, base_ref, sum_ref, x_ref, gain_ref, out_ref,
+):
+    unit, inverse = norm_parts(x_ref[0].astype(F32))
+    extra = norm_back(sum_ref[0].astype(F32), unit, inverse, gain_ref[...])
+    out_ref[0] = (base_ref[0] + jnp.where(me_ref[1] == 1, extra, 0.0)).astype(BF)
+
+
+def spec(shape, index=None):
+    return pl.BlockSpec(shape, index if index is not None else (lambda *a: (0,) * len(shape)))
+
+
+def sds(shape, dtype=BF):
+    return jax.ShapeDtypeStruct(shape, dtype)
+
+
+def params():
+    return pltpu.CompilerParams(vmem_limit_bytes=VMEM_LIMIT)
+
+
+def row(vector):
+    return vector.reshape(1, -1)
+
+
+def shuffle(value, axis, mask, names=None):
+    size = lax.axis_size(axis)
+    return lax.ppermute(value, axis, [(i, i ^ mask) for i in range(size)])
+
+
+def at(stacked, index, axis=0):
+    return lax.dynamic_index_in_dim(stacked, index, axis, keepdims=False)
+
+
+def swap_blocks(blocks, me, axis):
+    return [blocks[0]] + [shuffle(blocks[d], axis, d) for d in range(1, len(blocks))]
+
+
+def reduce_rows(buffer, samp, core):
+    zz, yy = samp // 2, samp % 2
+    halves = buffer.reshape(8, 2, 128, 512)
+    got = shuffle(at(halves, 1 - core, 1), "feat", 1)
+    part = (at(halves, core, 1).astype(F32) + got.astype(F32)).astype(BF)
+    part = part.reshape(4, 2, 128, 512)
+    got = shuffle(at(part, 1 - yy, 1), "samp", 1)
+    part = (at(part, yy, 1).astype(F32) + got.astype(F32)).astype(BF)
+    total = at(part, zz).astype(F32)
+    for d in range(1, 4):
+        total = total + shuffle(at(part, zz ^ d), "samp", 2 * d).astype(F32)
+    mine = total.astype(BF)
+    total = mine.astype(F32) + shuffle(mine, "feat", 2).astype(F32)
+    mine = total.astype(BF)
+    other = shuffle(mine, "feat", 1)
+    first = jnp.where(core == 0, mine, other)
+    second = jnp.where(core == 0, other, mine)
+    return jnp.concatenate([first, second], axis=0).astype(F32)
+
+
+def sum_everywhere(value):
+    for axis, mask in (("feat", 1), ("feat", 2), ("samp", 1), ("samp", 2), ("samp", 4)):
+        value = value + shuffle(value, axis, mask)
+    return value
+
+
+def rows_of(grad):
+    return jnp.concatenate(
+        [grad[:, c : c + 512].reshape(8, 64, 512) for c in range(0, grad.shape[1], 512)], axis=1
+    )
+
+
+def local_small(
+    layer_input, segment_ids, context_flags,
+    first_gain, first_shift, sample_weight, sample_bias, sample_mixer, sample_offset,
+    second_gain, second_shift, feature_weight, feature_bias, feature_mixer, feature_offset,
+    third_gain, third_shift, expand_weight, expand_bias, reduce_weight, reduce_bias, cotangent,
+):
+    samp, feat = lax.axis_index("samp"), lax.axis_index("feat")
+    core = feat % 2
+    flags = context_flags.reshape(8, 64)[:, 0]
+    root = jnp.argmax(flags).astype(jnp.int32)
+    me = jnp.stack([feat, (root == samp).astype(jnp.int32), samp, core]).astype(jnp.int32)
+
+    pieces = layer_input.reshape(8, 128, 512)
+    sent = [at(pieces, samp)] + [shuffle(at(pieces, samp ^ d), "samp", d) for d in range(1, 8)]
+    offset = samp ^ root
+    piece = sent[0]
+    for d in range(1, 8):
+        piece = jnp.where(offset == d, sent[d], piece)
+    context = jnp.concatenate(swap_blocks([piece] * 8, samp, "samp"), axis=0).reshape(4, 256, 512)
+    order = (samp ^ jnp.arange(8, dtype=jnp.int32)) * 8
+    order = (order[:, None] + jnp.arange(8, dtype=jnp.int32)[None, :]).reshape(64)
+    context_tasks = jnp.take(jnp.take(segment_ids.reshape(8, 64), root, axis=0), order)
+    blocks_of = (feat ^ jnp.arange(4, dtype=jnp.int32)) * 16
+    blocks_of = (blocks_of[:, None] + jnp.arange(16, dtype=jnp.int32)[None, :]).reshape(64)
+    own_tasks = jnp.take(lax.dynamic_slice_in_dim(segment_ids, samp * 64, 64), blocks_of)
+    allow = (own_tasks[:, None] == context_tasks[None, :]).astype(F32)
+    allow = jnp.concatenate([allow] * 4, axis=1)
+
+    x4 = layer_input.reshape(4, 256, 512)
+    cot4 = cotangent.reshape(4, 256, 512)
+    x_f = jnp.stack(swap_blocks([at(x4, feat ^ d) for d in range(4)], feat, "feat"))
+    cot_f = jnp.stack(swap_blocks([at(cot4, feat ^ d) for d in range(4)], feat, "feat"))
+
+    heads = sds((16, 4, 16, 512))
+    smem = pl.BlockSpec(memory_space=pltpu.SMEM)
+    o1, q1, k1, v1, p1 = pl.pallas_call(
+        forward_one,
+        out_shape=(sds((4, 256, 512)), heads, heads, heads, sds((16, 64, 512), F32)),
+        in_specs=[smem] + [pl.BlockSpec()] * 7,
+        scratch_shapes=[pltpu.VMEM((16, 4, 16, 512), BF)],
+        compiler_params=params(),
+        name="forward_one",
+    )(
+        me, x4, context, allow, row(first_gain), row(first_shift), sample_weight,
+        row(sample_bias),
+    )
+    o1_f = jnp.stack(swap_blocks([o1[d] for d in range(4)], feat, "feat"))
+
+    weights = [
+        sample_mixer, row(sample_offset), row(second_gain), row(second_shift), feature_weight,
+        row(feature_bias), feature_mixer, row(feature_offset), row(third_gain), row(third_shift),
+        expand_weight, row(expand_bias), reduce_weight, row(reduce_bias),
+    ]
+    blocked = spec((4, 64, 512), lambda i: (0, i, 0))
+    wide = lambda n: spec((256, n), lambda i: (i, 0))
+    out_f, gb1_f, act2, dqkv, o2, gb2, act3, gu, hidden, gb3, vec2, bias2 = pl.pallas_call(
+        middle,
+        grid=(4,),
+        out_shape=(
+            sds((4, 256, 512)), sds((4, 256, 512)), sds((1024, 512)), sds((1024, 1536)),
+            sds((1024, 512)), sds((1024, 512)), sds((1024, 512)), sds((1024, 2048)),
+            sds((1024, 2048)), sds((1024, 512)), sds((8, 512), F32), sds((1, 2048), F32),
+        ),
+        in_specs=[blocked] * 3
+        + [pl.BlockSpec(w.shape, lambda i: (0, 0), pipeline_mode=pl.Buffered(1)) for w in weights],
+        out_specs=[
+            blocked, blocked, wide(512), wide(1536), wide(512), wide(512), wide(512), wide(2048),
+            wide(2048), wide(512), spec((8, 512)), spec((1, 2048)),
+        ],
+        compiler_params=params(),
+        name="middle",
+    )(o1_f, x_f, cot_f, *weights)
+
+    out4 = jnp.stack(swap_blocks([out_f[d] for d in range(4)], feat, "feat"))
+    gb1 = jnp.stack(swap_blocks([gb1_f[d] for d in range(4)], feat, "feat"))
+    order4 = feat ^ jnp.arange(4, dtype=jnp.int32)
+    layer_output = jnp.take(out4, order4, axis=0).reshape(64, 16, 512)
+
+    grad = lambda a, b: jnp.einsum("td,te->de", a, b, preferred_element_type=F32).astype(BF)
+    reduce_rows_grad = reduce_rows(grad(hidden, gb3).reshape(8, 256, 512), samp, core)
+    expand_rows = reduce_rows(rows_of(grad(act3, gu)), samp, core)
+    feature_rows = reduce_rows(
+        jnp.concatenate([rows_of(grad(act2, dqkv)), rows_of(grad(o2, gb2))], axis=1), samp, core
+    )
+
+    base, term, act1, dq1, cact, dkv, vec1 = pl.pallas_call(
+        backward_one,
+        out_shape=(
+            sds((4, 256, 512), F32), sds((4, 256, 512)), sds((4, 256, 512)), sds((4, 256, 512)),
+            sds((4, 256, 512)), sds((4, 256, 1024)), sds((8, 512), F32),
+        ),
+        in_specs=[smem] + [pl.BlockSpec()] * 11,
+        scratch_shapes=[
+            pltpu.VMEM((16, 4, 16, 512), BF),
+            pltpu.VMEM((16, 4, 16, 512), BF),
+            pltpu.VMEM((16, 4, 16, 1024), BF),
+        ],
+        compiler_params=params(),
+        name="backward_one",
+    )(
+        me, gb1, x4, context, q1, k1, v1, p1, row(first_gain), row(first_shift), sample_weight,
+        sample_mixer,
+    )
+
+    terms = term.reshape(8, 128, 512)
+    total = terms[0].astype(F32)
+    for d in range(1, 8):
+        total = total + shuffle(terms[d], "samp", d).astype(F32)
+    summed = jnp.stack(swap_blocks([total.astype(BF)] * 8, samp, "samp"))
+    order8 = samp ^ jnp.arange(8, dtype=jnp.int32)
+    summed = jnp.take(summed, order8, axis=0).reshape(4, 256, 512)
+
+    flat = lambda a: a.reshape(1024, -1)
+    sample_rows = reduce_rows(
+        jnp.concatenate(
+            [
+                rows_of(grad(flat(act1), flat(dq1))),
+                rows_of(grad(flat(cact), flat(dkv))),
+                rows_of(grad(flat(o1), flat(gb1))),
+            ],
+            axis=1,
+        ),
+        samp,
+        core,
+    )
+    vectors = sum_everywhere(
+        jnp.concatenate([vec2.reshape(-1), bias2.reshape(-1), vec1.reshape(-1)])
+    )
+
+    input_grad = pl.pallas_call(
+        finish,
+        grid_spec=pltpu.PrefetchScalarGridSpec(
+            num_scalar_prefetch=1,
+            grid=(4,),
+            in_specs=[
+                spec((1, 256, 512), lambda i, m: (i ^ m[0], 0, 0)),
+                spec((1, 256, 512), lambda i, m: (i, 0, 0)),
+                spec((1, 256, 512), lambda i, m: (i, 0, 0)),
+                spec((1, 512)),
+            ],
+            out_specs=spec((1, 256, 512), lambda i, m: (i, 0, 0)),
+        ),
+        out_shape=sds((4, 256, 512)),
+        compiler_params=params(),
+        name="finish",
+    )(me, base, summed, x4, row(first_gain)).reshape(64, 16, 512)
+
+    def vector(start, size):
+        return lax.dynamic_slice_in_dim(vectors[start : start + size], samp * (size // 8), size // 8)
+
+    gain3, shift3, gain2, shift2, off2, bias_r, qs2, vs2 = (vector(i * 512, 512) for i in range(8))
+    expand_b = vector(4096, 2048)
+    gain1, shift1, off1, qs1, vs1 = (vector(6144 + i * 512, 512) for i in range(5))
+
+    def joined(first, second):
+        both = jnp.concatenate([vectors[first : first + 512], vectors[second : second + 512]])
+        return lax.dynamic_slice_in_dim(both, samp * 128, 128)
+
+    columns = lambda rows, first, count: jnp.concatenate(
+        [rows[64 * (first + i) : 64 * (first + i + 1)] for i in range(count)], axis=1
+    )
+
+    def unmix(rows):
+        return rows
+
+    return (
+        layer_output, input_grad,
+        gain1, shift1, columns(sample_rows, 0, 3), joined(6144 + 3 * 512, 6144 + 4 * 512),
+        columns(sample_rows, 3, 1), off1,
+        gain2, shift2, columns(feature_rows, 0, 3), joined(6 * 512, 7 * 512),
+        columns(feature_rows, 3, 1), off2,
+        gain3, shift3, columns(expand_rows, 0, 4), expand_b,
+        reduce_rows_grad, bias_r,
+    )
 
 
 def spread_2(block, axis, owner):
@@ -117,7 +642,7 @@
     return (join_heads(grad_queries), join_heads(grad_keys), join_heads(grad_values))
 
 
-def local(
+def local_large(
     layer_input,
     segment_ids,
     context_flags,
@@ -362,8 +887,9 @@
 
 
 def solution(mesh):
+    small = mesh.shape["samp"] == 8 and mesh.shape["feat"] == 4
     return jax.shard_map(
-        local,
+        local_small if small else local_large,
         mesh=mesh,
         in_specs=(
             P("samp", "feat", None),

time: 1240 us -> 411 us (0.33)
  waiting for transfers between devices: 795 us -> 109 us
  matrix products: 188 us -> 16.9 us
  Pallas kernels: 0 us -> 104 us
  starting transfers between devices: 1.82 us -> 103 us
  local copies, waits for them, and re-layouts: 131 us -> 42 us
  blocking collectives: 42.5 us -> 0 us
  other arithmetic: 52.2 us -> 24.7 us
  between operations: 20 us -> 5.17 us
    reduce_scatter x9 -> x0, waiting for transfers between devices: 636 us -> none  [the longest x1 91.6 us: local(): lax.psum_scatter(summed[14], 'samp', scatter_dimension=0, tiled=True)]
    dot_general x30 -> x7, matrix products: 188 us -> 16.9 us  [local_small(): jnp.einsum('td,te->de', a, b, preferred_element_type=F32).astype(BF)]
    ppermute x0 -> x76, waiting for transfers between devices: none -> 109 us  [shuffle(): return lax.ppermute(value, axis, [(i, i ^ mask) for i in range(size)])]
    psum x2 -> x0, waiting for transfers between devices: 106 us -> none  [the longest x1 98.7 us: spread_2(): return lax.psum(block, axis)]
    pallas_call x0 -> x4, Pallas kernels: none -> 104 us  [the longest x1 52.1 us: local_small(): pl.pallas_call(middle, grid=(4,), out_shape=(sds((4, 256, 512)), sds((4,...]
    ppermute x0 -> x76, starting transfers between devices: none -> 103 us  [shuffle(): return lax.ppermute(value, axis, [(i, i ^ mask) for i in range(size)])]
    reshape x13 -> x2, local copies, waits for them, and re-layouts: 71.9 us -> 1.51 us  [the longest x1 0.76 us: local_small(): segment_ids.reshape(8, 64)]
    all_gather x3 -> x0, waiting for transfers between devices: 53.2 us -> none  [the longest x1 28.1 us: local(): lax.all_gather(keys_two, 'feat', axis=1, tiled=True)]
  transfers between devices with their start and end apart: 14 -> 76, of which waited for: 14 -> 34; matrix products, arithmetic and copies ran while one was open for 11% -> 16% of each run, Pallas kernels for 0% -> 13%
where the time goes in v1:
time: 411 us; the launch traced here: 404 us
  waiting for transfers between devices  109 us (27%)
  Pallas kernels  104 us (25%)
  starting transfers between devices  103 us (25%)
  local copies, waits for them, and re-layouts  42 us (10%)
  other arithmetic  24.7 us (6%)
  matrix products  16.9 us (4%)
  between operations  5.17 us (1%)
    ppermute x76, waiting for transfers between devices, shuffle(): return lax.ppermute(value, axis, [(i, i ^ mask) for i in range(size)])  109 us
    ppermute x76, starting transfers between devices, shuffle(): return lax.ppermute(value, axis, [(i, i ^ mask) for i in range(size)])  103 us
    pallas_call x1, Pallas kernels, local_small(): pl.pallas_call(middle, grid=(4,), out_shape=(sds((4, 256, 512)), sds((4,...  52.1 us
    pallas_call x1, Pallas kernels, local_small(): pl.pallas_call(backward_one, out_shape=(sds((4, 256, 512), F32), sds((4,...  25.2 us
    pallas_call x1, Pallas kernels, local_small(): pl.pallas_call(forward_one, out_shape=(sds((4, 256, 512)), heads, heads,...  20.8 us
    dot_general x7, matrix products, local_small(): jnp.einsum('td,te->de', a, b, preferred_element_type=F32).astype(BF)  16.9 us
    unnamed x80, local copies, waits for them, and re-layouts  12.4 us
  transfers between devices with their start and end apart: 76, of which 34 were waited for; matrix products, arithmetic and copies ran while one was open for 16% of the time, Pallas kernels for 13%

profile of v1, /device:TPU:0, one launch (start us, length us, event | category | flops | bytes accessed | tf_op | source)
XLA Modules:
  0.0 404.5 jit_solution(5564256094081172398)
XLA Ops:
  2.9 6.0 %collective-permute-start = (bf16[128,512]{1,0:T(8,128)(2,1)S(1)}, bf16[128,512]{1,0:T(8,128)(2,1)S(1)}, u32[]{:S(2)}, u32[]{:S(2)}) collective-permute-start(bf16[128,512]{1,0:T(8,128)(2,1)S(1)} %get-tuple-element.128), channel_id=1, source_target_pairs={{0,28},{4,24},{8,20},{12,16},{16,12},{20,8},{24,4},{28,0},{1,29},{... | collective-permute-start | bytes 393224 | tf_op jit(solution)/shard_map/ppermute | solution.py:322
  11.9 2.3 collective-permute-start.4
  35.6 3.6 collective-permute-done.7
  40.2 2.8 collective-permute-start.10
  43.0 4.0 collective-permute-done.9
  48.4 4.0 collective-permute-done.10
  52.4 3.3 collective-permute-start.12
  55.8 2.5 collective-permute-done.11
  58.3 2.6 collective-permute-start.13
  61.0 5.1 %collective-permute-done.13 = bf16[128,512]{1,0:T(8,128)(2,1)S(1)} collective-permute-done((bf16[128,512]{1,0:T(8,128)(2,1)S(1)}, bf16[128,512]{1,0:T(8,128)(2,1)S(1)}, u32[]{:S(2)}, u32[]{:S(2)}) %collective-permute-start.13) | collective-permute-done | bytes 131104 | tf_op jit(solution)/shard_map/ppermute | solution.py:322
  68.6 20.8 %forward_one.1 = (bf16[4,256,512]{2,1,0:T(8,128)(2,1)}, bf16[16,4,16,512]{3,2,1,0:T(8,128)(2,1)}, bf16[16,4,16,512]{3,2,1,0:T(8,128)(2,1)}, bf16[16,4,16,512]{3,2,1,0:T(8,128)(2,1)}, f32[16,64,512]{2,1,0:T(8,128)}) custom-call(s32[4]{0:T(128)} %pad_add_fusion.me_ref, bf16[4,256,512]{2,1,0:T(8,128)(2,1)} %bitcast.277, bf16[4,256,512]{2,1,0:T(8,128)(2,1)} %bitcast.288, ...), custom_call_target="tpu_custom_call" | custom-call | tf_op jit(solution)/shard_map/forward_one/pallas_call | solution.py:400
  92.9 2.2 pad_maximum_fusion.4.x_ref
  95.2 2.9 collective-permute-done.22
  99.2 2.6 collective-permute-done.15
  101.8 6.6 %collective-permute-done.16 = bf16[256,512]{1,0:T(8,128)(2,1)S(1)} collective-permute-done((bf16[256,512]{1,0:T(8,128)(2,1)S(1)}, bf16[256,512]{1,0:T(8,128)(2,1)S(1)}, u32[]{:S(2)}, u32[]{:S(2)}) %collective-permute-start.16) | collective-permute-done | bytes 262176 | tf_op jit(solution)/shard_map/ppermute | solution.py:322
  109.5 52.1 %middle.1 = (bf16[4,256,512]{2,1,0:T(8,128)(2,1)}, bf16[4,256,512]{2,1,0:T(8,128)(2,1)}, bf16[1024,512]{1,0:T(8,128)(2,1)}, bf16[1024,1536]{1,0:T(8,128)(2,1)}, ...) custom-call(bf16[4,256,512]{2,1,0:T(8,128)(2,1)} %pad_maximum_fusion, ...), custom_call_target="tpu_custom_call" | custom-call | tf_op jit(solution)/shard_map/middle/pallas_call | solution.py:420
  161.6 4.9 %convolution_convert_fusion.1 = bf16[512,2048]{1,0:T(8,128)(2,1)S(1)} fusion(bf16[1024,512]{1,0:T(8,128)(2,1)} %get-tuple-element.67, bf16[1024,2048]{1,0:T(8,128)(2,1)} %get-tuple-element.68), kind=kOutput, calls=%fused_computation.5 | convolution fusion | flops 2148532224 | bytes 7340032 | tf_op jit(solution)/shard_map/td,te->de/dot_general | solution.py:443
  175.7 2.4 convolution_convert_fusion
  188.5 25.2 %backward_one.1 = (f32[4,256,512]{2,1,0:T(8,128)}, bf16[4,256,512]{2,1,0:T(8,128)(2,1)}, bf16[4,256,512]{2,1,0:T(8,128)(2,1)}, bf16[4,256,512]{2,1,0:T(8,128)(2,...) custom-call(s32[4]{0:T(128)} %pad_add_fusion.me_ref, ...), custom_call_target="tpu_custom_call" | custom-call | tf_op jit(solution)/shard_map/backward_one/pallas_call | solution.py:450
  217.5 4.0 bitcast_convert_fusion
  223.0 2.5 collective-permute-start.30
  226.5 3.7 collective-permute-start.32
  237.9 3.3 collective-permute-done.45
  243.3 3.3 collective-permute-start.34
  249.5 6.6 %collective-permute-done.33 = bf16[128,512]{1,0:T(8,128)(2,1)S(1)} collective-permute-done((bf16[128,512]{1,0:T(8,128)(2,1)S(1)}, bf16[128,512]{1,0:T(8,128)(2,1)S(1)}, u32[]{:S(2)}, u32[]{:S(2)}) %collective-permute-start.33) | collective-permute-done | bytes 131104 | tf_op jit(solution)/shard_map/ppermute | solution.py:322
  256.7 4.2 %collective-permute-start.47 = (f32[10240]{0:T(1024)S(1)}, f32[10240]{0:T(1024)S(1)}, u32[]{:S(2)}, u32[]{:S(2)}) collective-permute-start(f32[10240]{0:T(1024)S(1)} %add.346), channel_id=1, source_target_pairs={{0,16},{4,20},{8,24},{12,28},{16,0},{20,4},{24,8},{28,12},{1,17},{... | collective-permute-start | bytes 122888 | tf_op jit(solution)/shard_map/ppermute | solution.py:322
  270.6 3.4 collective-permute-start.37
  274.6 2.7 collective-permute-done.37
  277.3 2.7 collective-permute-start.38
  280.7 3.9 collective-permute-done.38
  286.7 6.6 %collective-permute-done.39 = bf16[128,512]{1,0:T(8,128)(2,1)S(1)} collective-permute-done((bf16[128,512]{1,0:T(8,128)(2,1)S(1)}, bf16[128,512]{1,0:T(8,128)(2,1)S(1)}, u32[]{:S(2)}, u32[]{:S(2)}) %collective-permute-start.39) | collective-permute-done | bytes 131104 | tf_op jit(solution)/shard_map/ppermute | solution.py:322
  294.1 7.2 %collective-permute-done.40 = bf16[128,512]{1,0:T(8,128)(2,1)S(1)} collective-permute-done((bf16[128,512]{1,0:T(8,128)(2,1)S(1)}, bf16[128,512]{1,0:T(8,128)(2,1)S(1)}, u32[]{:S(2)}, u32[]{:S(2)}) %collective-permute-start.40) | collective-permute-done | bytes 131104 | tf_op jit(solution)/shard_map/ppermute | solution.py:322
  301.4 3.1 collective-permute-start.41
  305.1 3.0 collective-permute-done.41
  308.1 2.6 collective-permute-start.42
  311.3 4.4 %collective-permute-done.42 = bf16[128,512]{1,0:T(8,128)(2,1)S(1)} collective-permute-done((bf16[128,512]{1,0:T(8,128)(2,1)S(1)}, bf16[128,512]{1,0:T(8,128)(2,1)S(1)}, u32[]{:S(2)}, u32[]{:S(2)}) %collective-permute-start.42) | collective-permute-done | bytes 131104 | tf_op jit(solution)/shard_map/ppermute | solution.py:322
  319.5 5.7 %finish.1 = bf16[4,256,512]{2,1,0:T(8,128)(2,1)} custom-call(s32[4]{0:T(128)} %pad_add_fusion.me_ref, f32[4,256,512]{2,1,0:T(8,128)} %get-tuple-element.54.base_ref, bf16[4,256,512]{2,1,0:T(8,128)(2,1)} %bitcast_select_fusion.sum_ref, bf16[4,256,512]{2,1,0:T(8,128)(2,1)} %bitcast.279, f32[1,512]{1,0:T(1,128)} %bitcast.341), custom_call_target="tpu_custom_call" | custom-call | tf_op jit(solution)/shard_map/finish/pallas_call | solution.py:494
  336.2 5.6 %collective-permute-done.70 = bf16[4,128,512]{2,1,0:T(8,128)(2,1)S(1)} collective-permute-done((bf16[4,128,512]{2,1,0:T(8,128)(2,1)S(1)}, bf16[4,128,512]{2,1,0:T(8,128)(2,1)S(1)}, u32[]{:S(2)}, u32[]{:S(2)}) %collective-permute-start.70) | collective-permute-done | bytes 524320 | tf_op jit(solution)/shard_map/ppermute | solution.py:322
  342.1 3.6 collective-permute-start.72
  345.7 6.2 %collective-permute-done.63 = bf16[4,128,512]{2,1,0:T(8,128)(2,1)S(1)} collective-permute-done((bf16[4,128,512]{2,1,0:T(8,128)(2,1)S(1)}, bf16[4,128,512]{2,1,0:T(8,128)(2,1)S(1)}, u32[]{:S(2)}, u32[]{:S(2)}) %collective-permute-start.63) | collective-permute-done | bytes 524320 | tf_op jit(solution)/shard_map/ppermute | solution.py:322
  352.0 3.7 collective-permute-start.73
  357.6 2.8 collective-permute-start.64
  364.4 2.3 collective-permute-start.58
  366.7 3.4 collective-permute-done.65
  374.3 2.7 collective-permute-done.59
  380.0 2.2 collective-permute-done.60
  384.3 2.7 collective-permute-start.52
  389.9 6.2 %collective-permute-done.51 = bf16[128,512]{1,0:T(8,128)(2,1)S(1)} collective-permute-done((bf16[128,512]{1,0:T(8,128)(2,1)S(1)}, bf16[128,512]{1,0:T(8,128)(2,1)S(1)}, u32[]{:S(2)}, u32[]{:S(2)}) %collective-permute-start.51) | collective-permute-done | bytes 131104 | tf_op jit(solution)/shard_map/ppermute | solution.py:322
  (315 shorter events, 129.1 us)
Async XLA Ops:
  2.9 20.0 %collective-permute-start = (bf16[128,512]{1,0:T(8,128)(2,1)S(1)}, bf16[128,512]{1,0:T(8,128)(2,1)S(1)}, u32[]{:S(2)}, u32[]{:S(2)}) collective-permute-start(bf16[128,512]{1,0:T(8,128)(2,1)S(1)} %get-tuple-element.128), channel_id=1, source_target_pairs={{0,28},{4,24},{8,20},{12,16},{16,12},{20,8},{24,4},{28,0},{1,29},{... | collective-permute-start | bytes 393224 | tf_op jit(solution)/shard_map/ppermute | solution.py:322
  8.9 15.7 %collective-permute-start.1 = (bf16[128,512]{1,0:T(8,128)(2,1)S(1)}, bf16[128,512]{1,0:T(8,128)(2,1)S(1)}, u32[]{:S(2)}, u32[]{:S(2)}) collective-permute-start(bf16[128,512]{1,0:T(8,128)(2,1)S(1)} %get-tuple-element.127), channel_id=1, source_target_pairs={{0,24},{4,28},{8,16},{12,20},{16,8},{20,12},{24,0},{28,4},{1,25},{... | collective-permute-start | bytes 393224 | tf_op jit(solution)/shard_map/ppermute | solution.py:322
  9.1 20.4 %collective-permute-start.2 = (bf16[128,512]{1,0:T(8,128)(2,1)}, bf16[128,512]{1,0:T(8,128)(2,1)}, u32[]{:S(2)}, u32[]{:S(2)}) collective-permute-start(bf16[128,512]{1,0:T(8,128)(2,1)} %get-tuple-element.126), channel_id=1, source_target_pairs={{0,20},{4,16},{8,28},{12,24},{16,4},{20,0},{24,12},{28,8},{1,21},{... | collective-permute-start | bytes 393224 | tf_op jit(solution)/shard_map/ppermute | solution.py:322
  9.8 21.6 %collective-permute-start.3 = (bf16[128,512]{1,0:T(8,128)(2,1)}, bf16[128,512]{1,0:T(8,128)(2,1)}, u32[]{:S(2)}, u32[]{:S(2)}) collective-permute-start(bf16[128,512]{1,0:T(8,128)(2,1)} %get-tuple-element.125), channel_id=1, source_target_pairs={{0,16},{4,20},{8,24},{12,28},{16,0},{20,4},{24,8},{28,12},{1,17},{... | collective-permute-start | bytes 393224 | tf_op jit(solution)/shard_map/ppermute | solution.py:322
  11.9 21.0 %collective-permute-start.4 = (bf16[128,512]{1,0:T(8,128)(2,1)}, bf16[128,512]{1,0:T(8,128)(2,1)}, u32[]{:S(2)}, u32[]{:S(2)}) collective-permute-start(bf16[128,512]{1,0:T(8,128)(2,1)} %get-tuple-element.124), channel_id=1, source_target_pairs={{0,12},{4,8},{8,4},{12,0},{16,28},{20,24},{24,20},{28,16},{1,13},{... | collective-permute-start | bytes 393224 | tf_op jit(solution)/shard_map/ppermute | solution.py:322
  22.8 10.1 %collective-permute-start.5 = (bf16[128,512]{1,0:T(8,128)(2,1)}, bf16[128,512]{1,0:T(8,128)(2,1)}, u32[]{:S(2)}, u32[]{:S(2)}) collective-permute-start(bf16[128,512]{1,0:T(8,128)(2,1)} %get-tuple-element.123), channel_id=1, source_target_pairs={{0,8},{4,12},{8,0},{12,4},{16,24},{20,28},{24,16},{28,20},{1,9},{5... | collective-permute-start | bytes 393224 | tf_op jit(solution)/shard_map/ppermute | solution.py:322
  29.5 59.9 %collective-permute-start.17 = (bf16[256,512]{1,0:T(8,128)(2,1)}, bf16[256,512]{1,0:T(8,128)(2,1)}, u32[]{:S(2)}, u32[]{:S(2)}) collective-permute-start(bf16[256,512]{1,0:T(8,128)(2,1)} %get-tuple-element.117), channel_id=1, source_target_pairs={{0,1},{1,0},{2,3},{3,2},{4,5},{5,4},{6,7},{7,6},{8,9},{9,8},{10,11... | collective-permute-start | bytes 786440 | tf_op jit(solution)/shard_map/ppermute | solution.py:322
  31.4 59.3 %collective-permute-start.18 = (bf16[256,512]{1,0:T(8,128)(2,1)S(1)}, bf16[256,512]{1,0:T(8,128)(2,1)}, u32[]{:S(2)}, u32[]{:S(2)}) collective-permute-start(bf16[256,512]{1,0:T(8,128)(2,1)S(1)} %get-tuple-element.116), channel_id=1, source_target_pairs={{0,2},{1,3},{2,0},{3,1},{4,6},{5,7},{6,4},{7,5},{8,10},{9,11},{10,... | collective-permute-start | bytes 786440 | tf_op jit(solution)/shard_map/ppermute | solution.py:322
  32.9 58.5 %collective-permute-start.19 = (bf16[256,512]{1,0:T(8,128)(2,1)S(1)}, bf16[256,512]{1,0:T(8,128)(2,1)}, u32[]{:S(2)}, u32[]{:S(2)}) collective-permute-start(bf16[256,512]{1,0:T(8,128)(2,1)S(1)} %get-tuple-element.115), channel_id=1, source_target_pairs={{0,3},{1,2},{2,1},{3,0},{4,7},{5,6},{6,5},{7,4},{8,11},{9,10},{10,... | collective-permute-start | bytes 786440 | tf_op jit(solution)/shard_map/ppermute | solution.py:322
  40.2 12.2 %collective-permute-start.10 = (bf16[128,512]{1,0:T(8,128)(2,1)S(1)}, bf16[128,512]{1,0:T(8,128)(2,1)S(1)}, u32[]{:S(2)}, u32[]{:S(2)}) collective-permute-start(bf16[128,512]{1,0:T(8,128)(2,1)S(1)} %get-tuple-element.85), channel_id=1, source_target_pairs={{0,16},{4,20},{8,24},{12,28},{16,0},{20,4},{24,8},{28,12},{1,17},{... | collective-permute-start | bytes 393224 | tf_op jit(solution)/shard_map/ppermute | solution.py:322
  47.0 11.3 %collective-permute-start.11 = (bf16[128,512]{1,0:T(8,128)(2,1)S(1)}, bf16[128,512]{1,0:T(8,128)(2,1)S(1)}, u32[]{:S(2)}, u32[]{:S(2)}) collective-permute-start(bf16[128,512]{1,0:T(8,128)(2,1)S(1)} %get-tuple-element.85), channel_id=1, source_target_pairs={{0,20},{4,16},{8,28},{12,24},{16,4},{20,0},{24,12},{28,8},{1,21},{... | collective-permute-start | bytes 393224 | tf_op jit(solution)/shard_map/ppermute | solution.py:322
  60.9 32.0 %collective-permute-start.20 = (bf16[256,512]{1,0:T(8,128)(2,1)}, bf16[256,512]{1,0:T(8,128)(2,1)S(1)}, u32[]{:S(2)}, u32[]{:S(2)}) collective-permute-start(bf16[256,512]{1,0:T(8,128)(2,1)} %get-tuple-element.113), channel_id=1, source_target_pairs={{0,1},{1,0},{2,3},{3,2},{4,5},{5,4},{6,7},{7,6},{8,9},{9,8},{10,11... | collective-permute-start | bytes 786440 | tf_op jit(solution)/shard_map/ppermute | solution.py:322
  66.1 29.1 %collective-permute-start.21 = (bf16[256,512]{1,0:T(8,128)(2,1)}, bf16[256,512]{1,0:T(8,128)(2,1)S(1)}, u32[]{:S(2)}, u32[]{:S(2)}) collective-permute-start(bf16[256,512]{1,0:T(8,128)(2,1)} %get-tuple-element.112), channel_id=1, source_target_pairs={{0,2},{1,3},{2,0},{3,1},{4,6},{5,7},{6,4},{7,5},{8,10},{9,11},{10,... | collective-permute-start | bytes 786440 | tf_op jit(solution)/shard_map/ppermute | solution.py:322
  91.4 10.4 %collective-permute-start.15 = (bf16[256,512]{1,0:T(8,128)(2,1)S(1)}, bf16[256,512]{1,0:T(8,128)(2,1)S(1)}, u32[]{:S(2)}, u32[]{:S(2)}) collective-permute-start(bf16[256,512]{1,0:T(8,128)(2,1)S(1)} %get-tuple-element.120), channel_id=1, source_target_pairs={{0,2},{1,3},{2,0},{3,1},{4,6},{5,7},{6,4},{7,5},{8,10},{9,11},{10,... | collective-permute-start | bytes 786440 | tf_op jit(solution)/shard_map/ppermute | solution.py:322
  92.9 15.4 %collective-permute-start.16 = (bf16[256,512]{1,0:T(8,128)(2,1)S(1)}, bf16[256,512]{1,0:T(8,128)(2,1)S(1)}, u32[]{:S(2)}, u32[]{:S(2)}) collective-permute-start(bf16[256,512]{1,0:T(8,128)(2,1)S(1)} %get-tuple-element.119), channel_id=1, source_target_pairs={{0,3},{1,2},{2,1},{3,0},{4,7},{5,6},{6,5},{7,4},{8,11},{9,10},{10,... | collective-permute-start | bytes 786440 | tf_op jit(solution)/shard_map/ppermute | solution.py:322
  171.8 13.4 %collective-permute-start.26 = (bf16[256,512]{1,0:T(8,128)(2,1)S(1)}, bf16[256,512]{1,0:T(8,128)(2,1)S(1)}, u32[]{:S(2)}, u32[]{:S(2)}) collective-permute-start(bf16[256,512]{1,0:T(8,128)(2,1)S(1)} %get-tuple-element.105), channel_id=1, source_target_pairs={{0,1},{1,0},{2,3},{3,2},{4,5},{5,4},{6,7},{7,6},{8,9},{9,8},{10,11... | collective-permute-start | bytes 786440 | tf_op jit(solution)/shard_map/ppermute | solution.py:322
  171.9 13.4 %collective-permute-start.27 = (bf16[256,512]{1,0:T(8,128)(2,1)S(1)}, bf16[256,512]{1,0:T(8,128)(2,1)S(1)}, u32[]{:S(2)}, u32[]{:S(2)}) collective-permute-start(bf16[256,512]{1,0:T(8,128)(2,1)S(1)} %get-tuple-element.104), channel_id=1, source_target_pairs={{0,2},{1,3},{2,0},{3,1},{4,6},{5,7},{6,4},{7,5},{8,10},{9,11},{10,... | collective-permute-start | bytes 786440 | tf_op jit(solution)/shard_map/ppermute | solution.py:322
  173.4 12.4 %collective-permute-start.28 = (bf16[256,512]{1,0:T(8,128)(2,1)S(1)}, bf16[256,512]{1,0:T(8,128)(2,1)S(1)}, u32[]{:S(2)}, u32[]{:S(2)}) collective-permute-start(bf16[256,512]{1,0:T(8,128)(2,1)S(1)} %get-tuple-element.103), channel_id=1, source_target_pairs={{0,3},{1,2},{2,1},{3,0},{4,7},{5,6},{6,5},{7,4},{8,11},{9,10},{10,... | collective-permute-start | bytes 786440 | tf_op jit(solution)/shard_map/ppermute | solution.py:322
  173.9 49.1 %collective-permute-start.23 = (bf16[256,512]{1,0:T(8,128)(2,1)S(1)}, bf16[256,512]{1,0:T(8,128)(2,1)S(1)}, u32[]{:S(2)}, u32[]{:S(2)}) collective-permute-start(bf16[256,512]{1,0:T(8,128)(2,1)S(1)} %get-tuple-element.109), channel_id=1, source_target_pairs={{0,1},{1,0},{2,3},{3,2},{4,5},{5,4},{6,7},{7,6},{8,9},{9,8},{10,11... | collective-permute-start | bytes 786440 | tf_op jit(solution)/shard_map/ppermute | solution.py:322
  174.3 51.2 %collective-permute-start.24 = (bf16[256,512]{1,0:T(8,128)(2,1)S(1)}, bf16[256,512]{1,0:T(8,128)(2,1)S(1)}, u32[]{:S(2)}, u32[]{:S(2)}) collective-permute-start(bf16[256,512]{1,0:T(8,128)(2,1)S(1)} %get-tuple-element.108), channel_id=1, source_target_pairs={{0,2},{1,3},{2,0},{3,1},{4,6},{5,7},{6,4},{7,5},{8,10},{9,11},{10,... | collective-permute-start | bytes 786440 | tf_op jit(solution)/shard_map/ppermute | solution.py:322
  185.2 41.3 %collective-permute-start.25 = (bf16[256,512]{1,0:T(8,128)(2,1)S(1)}, bf16[256,512]{1,0:T(8,128)(2,1)S(1)}, u32[]{:S(2)}, u32[]{:S(2)}) collective-permute-start(bf16[256,512]{1,0:T(8,128)(2,1)S(1)} %get-tuple-element.107), channel_id=1, source_target_pairs={{0,3},{1,2},{2,1},{3,0},{4,7},{5,6},{6,5},{7,4},{8,11},{9,10},{10,... | collective-permute-start | bytes 786440 | tf_op jit(solution)/shard_map/ppermute | solution.py:322
  214.5 18.6 %collective-permute-start.43 = (f32[10240]{0:T(1024)S(1)}, f32[10240]{0:T(1024)S(1)}, u32[]{:S(2)}, u32[]{:S(2)}) collective-permute-start(f32[10240]{0:T(1024)S(1)} %pad_maximum_fusion.11), channel_id=1, source_target_pairs={{0,1},{1,0},{2,3},{3,2},{4,5},{5,4},{6,7},{7,6},{8,9},{9,8},{10,11... | collective-permute-start | bytes 122888 | tf_op jit(solution)/shard_map/ppermute | solution.py:322
  217.4 24.0 %collective-permute-start.29 = (bf16[128,512]{1,0:T(8,128)(2,1)}, bf16[128,512]{1,0:T(8,128)(2,1)}, u32[]{:S(2)}, u32[]{:S(2)}) collective-permute-start(bf16[128,512]{1,0:T(8,128)(2,1)} %get-tuple-element.95), channel_id=1, source_target_pairs={{0,4},{4,0},{8,12},{12,8},{16,20},{20,16},{24,28},{28,24},{1,5},{5... | collective-permute-start | bytes 393224 | tf_op jit(solution)/shard_map/ppermute | solution.py:322
  223.0 20.3 %collective-permute-start.30 = (bf16[128,512]{1,0:T(8,128)(2,1)}, bf16[128,512]{1,0:T(8,128)(2,1)S(1)}, u32[]{:S(2)}, u32[]{:S(2)}) collective-permute-start(bf16[128,512]{1,0:T(8,128)(2,1)} %get-tuple-element.101), channel_id=1, source_target_pairs={{0,8},{4,12},{8,0},{12,4},{16,24},{20,28},{24,16},{28,20},{1,9},{5... | collective-permute-start | bytes 393224 | tf_op jit(solution)/shard_map/ppermute | solution.py:322
  225.5 23.4 %collective-permute-start.31 = (bf16[128,512]{1,0:T(8,128)(2,1)}, bf16[128,512]{1,0:T(8,128)(2,1)S(1)}, u32[]{:S(2)}, u32[]{:S(2)}) collective-permute-start(bf16[128,512]{1,0:T(8,128)(2,1)} %get-tuple-element.100), channel_id=1, source_target_pairs={{0,12},{4,8},{8,4},{12,0},{16,28},{20,24},{24,20},{28,16},{1,13},{... | collective-permute-start | bytes 393224 | tf_op jit(solution)/shard_map/ppermute | solution.py:322
  226.5 22.5 %collective-permute-start.32 = (bf16[128,512]{1,0:T(8,128)(2,1)}, bf16[128,512]{1,0:T(8,128)(2,1)}, u32[]{:S(2)}, u32[]{:S(2)}) collective-permute-start(bf16[128,512]{1,0:T(8,128)(2,1)} %get-tuple-element.99), channel_id=1, source_target_pairs={{0,16},{4,20},{8,24},{12,28},{16,0},{20,4},{24,8},{28,12},{1,17},{... | collective-permute-start | bytes 393224 | tf_op jit(solution)/shard_map/ppermute | solution.py:322
  242.2 14.0 %collective-permute-start.33 = (bf16[128,512]{1,0:T(8,128)(2,1)S(1)}, bf16[128,512]{1,0:T(8,128)(2,1)S(1)}, u32[]{:S(2)}, u32[]{:S(2)}) collective-permute-start(bf16[128,512]{1,0:T(8,128)(2,1)S(1)} %copy-done.18), channel_id=1, source_target_pairs={{0,20},{4,16},{8,28},{12,24},{16,4},{20,0},{24,12},{28,8},{1,21},{... | collective-permute-start | bytes 393224 | tf_op jit(solution)/shard_map/ppermute | solution.py:322
  243.3 12.8 %collective-permute-start.34 = (bf16[128,512]{1,0:T(8,128)(2,1)S(1)}, bf16[128,512]{1,0:T(8,128)(2,1)S(1)}, u32[]{:S(2)}, u32[]{:S(2)}) collective-permute-start(bf16[128,512]{1,0:T(8,128)(2,1)S(1)} %copy-done.17), channel_id=1, source_target_pairs={{0,24},{4,28},{8,16},{12,20},{16,8},{20,12},{24,0},{28,4},{1,25},{... | collective-permute-start | bytes 393224 | tf_op jit(solution)/shard_map/ppermute | solution.py:322
  246.6 10.0 %collective-permute-start.35 = (bf16[128,512]{1,0:T(8,128)(2,1)S(1)}, bf16[128,512]{1,0:T(8,128)(2,1)S(1)}, u32[]{:S(2)}, u32[]{:S(2)}) collective-permute-start(bf16[128,512]{1,0:T(8,128)(2,1)S(1)} %copy-done.16), channel_id=1, source_target_pairs={{0,28},{4,24},{8,20},{12,16},{16,12},{20,8},{24,4},{28,0},{1,29},{... | collective-permute-start | bytes 393224 | tf_op jit(solution)/shard_map/ppermute | solution.py:322
  248.9 76.2 %collective-permute-start.69 = (bf16[8,128,512]{2,1,0:T(8,128)(2,1)}, bf16[8,128,512]{2,1,0:T(8,128)(2,1)}, u32[]{:S(2)}, u32[]{:S(2)}) collective-permute-start(bf16[8,128,512]{2,1,0:T(8,128)(2,1)} %dynamic-slice_bitcast_fusion), channel_id=1, source_target_pairs={{0,1},{1,0},{2,3},{3,2},{4,5},{5,4},{6,7},{7,6},{8,9},{9,8},{10,11... | collective-permute-start | bytes 3145736 | tf_op jit(solution)/shard_map/ppermute | solution.py:322
  249.0 80.0 %collective-permute-start.62 = (bf16[8,128,512]{2,1,0:T(8,128)(2,1)}, bf16[8,128,512]{2,1,0:T(8,128)(2,1)}, u32[]{:S(2)}, u32[]{:S(2)}) collective-permute-start(bf16[8,128,512]{2,1,0:T(8,128)(2,1)} %dynamic-slice_bitcast_fusion.1), channel_id=1, source_target_pairs={{0,1},{1,0},{2,3},{3,2},{4,5},{5,4},{6,7},{7,6},{8,9},{9,8},{10,11... | collective-permute-start | bytes 3145736 | tf_op jit(solution)/shard_map/ppermute | solution.py:322
  256.1 74.6 %collective-permute-start.55 = (bf16[8,128,512]{2,1,0:T(8,128)(2,1)}, bf16[8,128,512]{2,1,0:T(8,128)(2,1)}, u32[]{:S(2)}, u32[]{:S(2)}) collective-permute-start(bf16[8,128,512]{2,1,0:T(8,128)(2,1)} %dynamic-slice_bitcast_fusion.2), channel_id=1, source_target_pairs={{0,1},{1,0},{2,3},{3,2},{4,5},{5,4},{6,7},{7,6},{8,9},{9,8},{10,11... | collective-permute-start | bytes 3145736 | tf_op jit(solution)/shard_map/ppermute | solution.py:322
  256.2 78.2 %collective-permute-start.48 = (bf16[8,128,512]{2,1,0:T(8,128)(2,1)}, bf16[8,128,512]{2,1,0:T(8,128)(2,1)}, u32[]{:S(2)}, u32[]{:S(2)}) collective-permute-start(bf16[8,128,512]{2,1,0:T(8,128)(2,1)} %dynamic-slice_bitcast_fusion.3), channel_id=1, source_target_pairs={{0,1},{1,0},{2,3},{3,2},{4,5},{5,4},{6,7},{7,6},{8,9},{9,8},{10,11... | collective-permute-start | bytes 3145736 | tf_op jit(solution)/shard_map/ppermute | solution.py:322
  284.6 8.7 %collective-permute-start.39 = (bf16[128,512]{1,0:T(8,128)(2,1)S(1)}, bf16[128,512]{1,0:T(8,128)(2,1)S(1)}, u32[]{:S(2)}, u32[]{:S(2)}) collective-permute-start(bf16[128,512]{1,0:T(8,128)(2,1)S(1)} %get-tuple-element.83), channel_id=1, source_target_pairs={{0,16},{4,20},{8,24},{12,28},{16,0},{20,4},{24,8},{28,12},{1,17},{... | collective-permute-start | bytes 393224 | tf_op jit(solution)/shard_map/ppermute | solution.py:322
  326.9 15.0 %collective-permute-start.70 = (bf16[4,128,512]{2,1,0:T(8,128)(2,1)S(1)}, bf16[4,128,512]{2,1,0:T(8,128)(2,1)S(1)}, u32[]{:S(2)}, u32[]{:S(2)}) collective-permute-start(bf16[4,128,512]{2,1,0:T(8,128)(2,1)S(1)} %dynamic-slice_bitcast_fusion.4), channel_id=1, source_target_pairs={{0,4},{4,0},{8,12},{12,8},{16,20},{20,16},{24,28},{28,24},{1,5},{5... | collective-permute-start | bytes 1572872 | tf_op jit(solution)/shard_map/ppermute | solution.py:322
  330.6 21.4 %collective-permute-start.63 = (bf16[4,128,512]{2,1,0:T(8,128)(2,1)S(1)}, bf16[4,128,512]{2,1,0:T(8,128)(2,1)S(1)}, u32[]{:S(2)}, u32[]{:S(2)}) collective-permute-start(bf16[4,128,512]{2,1,0:T(8,128)(2,1)S(1)} %dynamic-slice_bitcast_fusion.5), channel_id=1, source_target_pairs={{0,4},{4,0},{8,12},{12,8},{16,20},{20,16},{24,28},{28,24},{1,5},{5... | collective-permute-start | bytes 1572872 | tf_op jit(solution)/shard_map/ppermute | solution.py:322
  332.5 25.1 %collective-permute-start.56 = (bf16[4,128,512]{2,1,0:T(8,128)(2,1)S(1)}, bf16[4,128,512]{2,1,0:T(8,128)(2,1)S(1)}, u32[]{:S(2)}, u32[]{:S(2)}) collective-permute-start(bf16[4,128,512]{2,1,0:T(8,128)(2,1)S(1)} %dynamic-slice_bitcast_fusion.6), channel_id=1, source_target_pairs={{0,4},{4,0},{8,12},{12,8},{16,20},{20,16},{24,28},{28,24},{1,5},{5... | collective-permute-start | bytes 1572872 | tf_op jit(solution)/shard_map/ppermute | solution.py:322
  335.9 46.4 %collective-permute-start.49 = (bf16[4,128,512]{2,1,0:T(8,128)(2,1)S(1)}, bf16[4,128,512]{2,1,0:T(8,128)(2,1)S(1)}, u32[]{:S(2)}, u32[]{:S(2)}) collective-permute-start(bf16[4,128,512]{2,1,0:T(8,128)(2,1)S(1)} %dynamic-slice_bitcast_fusion.7), channel_id=1, source_target_pairs={{0,4},{4,0},{8,12},{12,8},{16,20},{20,16},{24,28},{28,24},{1,5},{5... | collective-permute-start | bytes 1572872 | tf_op jit(solution)/shard_map/ppermute | solution.py:322
  342.0 18.5 %collective-permute-start.71 = (bf16[128,512]{1,0:T(8,128)(2,1)S(1)}, bf16[128,512]{1,0:T(8,128)(2,1)S(1)}, u32[]{:S(2)}, u32[]{:S(2)}) collective-permute-start(bf16[128,512]{1,0:T(8,128)(2,1)S(1)} %get-tuple-element.129), channel_id=1, source_target_pairs={{0,8},{4,12},{8,0},{12,4},{16,24},{20,28},{24,16},{28,20},{1,9},{5... | collective-permute-start | bytes 393224 | tf_op jit(solution)/shard_map/ppermute | solution.py:322
  342.1 20.0 %collective-permute-start.72 = (bf16[128,512]{1,0:T(8,128)(2,1)S(1)}, bf16[128,512]{1,0:T(8,128)(2,1)S(1)}, u32[]{:S(2)}, u32[]{:S(2)}) collective-permute-start(bf16[128,512]{1,0:T(8,128)(2,1)S(1)} %get-tuple-element.131), channel_id=1, source_target_pairs={{0,16},{4,20},{8,24},{12,28},{16,0},{20,4},{24,8},{28,12},{1,17},{... | collective-permute-start | bytes 393224 | tf_op jit(solution)/shard_map/ppermute | solution.py:322
  352.0 11.0 %collective-permute-start.73 = (bf16[128,512]{1,0:T(8,128)(2,1)S(1)}, bf16[128,512]{1,0:T(8,128)(2,1)S(1)}, u32[]{:S(2)}, u32[]{:S(2)}) collective-permute-start(bf16[128,512]{1,0:T(8,128)(2,1)S(1)} %get-tuple-element.130), channel_id=1, source_target_pairs={{0,24},{4,28},{8,16},{12,20},{16,8},{20,12},{24,0},{28,4},{1,25},{... | collective-permute-start | bytes 393224 | tf_op jit(solution)/shard_map/ppermute | solution.py:322
  360.6 9.5 %collective-permute-start.65 = (bf16[128,512]{1,0:T(8,128)(2,1)S(1)}, bf16[128,512]{1,0:T(8,128)(2,1)S(1)}, u32[]{:S(2)}, u32[]{:S(2)}) collective-permute-start(bf16[128,512]{1,0:T(8,128)(2,1)S(1)} %get-tuple-element.138), channel_id=1, source_target_pairs={{0,16},{4,20},{8,24},{12,28},{16,0},{20,4},{24,8},{28,12},{1,17},{... | collective-permute-start | bytes 393224 | tf_op jit(solution)/shard_map/ppermute | solution.py:322
  362.2 9.1 %collective-permute-start.66 = (bf16[128,512]{1,0:T(8,128)(2,1)S(1)}, bf16[128,512]{1,0:T(8,128)(2,1)S(1)}, u32[]{:S(2)}, u32[]{:S(2)}) collective-permute-start(bf16[128,512]{1,0:T(8,128)(2,1)S(1)} %get-tuple-element.137), channel_id=1, source_target_pairs={{0,24},{4,28},{8,16},{12,20},{16,8},{20,12},{24,0},{28,4},{1,25},{... | collective-permute-start | bytes 393224 | tf_op jit(solution)/shard_map/ppermute | solution.py:322
  363.0 10.4 %collective-permute-start.57 = (bf16[128,512]{1,0:T(8,128)(2,1)S(1)}, bf16[128,512]{1,0:T(8,128)(2,1)S(1)}, u32[]{:S(2)}, u32[]{:S(2)}) collective-permute-start(bf16[128,512]{1,0:T(8,128)(2,1)S(1)} %get-tuple-element.143), channel_id=1, source_target_pairs={{0,8},{4,12},{8,0},{12,4},{16,24},{20,28},{24,16},{28,20},{1,9},{5... | collective-permute-start | bytes 393224 | tf_op jit(solution)/shard_map/ppermute | solution.py:322
  364.4 9.8 %collective-permute-start.58 = (bf16[128,512]{1,0:T(8,128)(2,1)S(1)}, bf16[128,512]{1,0:T(8,128)(2,1)S(1)}, u32[]{:S(2)}, u32[]{:S(2)}) collective-permute-start(bf16[128,512]{1,0:T(8,128)(2,1)S(1)} %get-tuple-element.145), channel_id=1, source_target_pairs={{0,16},{4,20},{8,24},{12,28},{16,0},{20,4},{24,8},{28,12},{1,17},{... | collective-permute-start | bytes 393224 | tf_op jit(solution)/shard_map/ppermute | solution.py:322
  379.3 22.0 %collective-permute-start.75 = (bf16[128,512]{1,0:T(8,128)(2,1)S(1)}, bf16[128,512]{1,0:T(8,128)(2,1)S(1)}, u32[]{:S(2)}, u32[]{:S(2)}) collective-permute-start(bf16[128,512]{1,0:T(8,128)(2,1)S(1)} %add_convert_fusion), channel_id=1, source_target_pairs={{0,1},{1,0},{2,3},{3,2},{4,5},{5,4},{6,7},{7,6},{8,9},{9,8},{10,11... | collective-permute-start | bytes 393224 | tf_op jit(solution)/shard_map/ppermute | solution.py:322
  383.2 12.9 %collective-permute-start.51 = (bf16[128,512]{1,0:T(8,128)(2,1)S(1)}, bf16[128,512]{1,0:T(8,128)(2,1)S(1)}, u32[]{:S(2)}, u32[]{:S(2)}) collective-permute-start(bf16[128,512]{1,0:T(8,128)(2,1)S(1)} %get-tuple-element.152), channel_id=1, source_target_pairs={{0,16},{4,20},{8,24},{12,28},{16,0},{20,4},{24,8},{28,12},{1,17},{... | collective-permute-start | bytes 393224 | tf_op jit(solution)/shard_map/ppermute | solution.py:322
  384.3 11.8 %collective-permute-start.52 = (bf16[128,512]{1,0:T(8,128)(2,1)S(1)}, bf16[128,512]{1,0:T(8,128)(2,1)S(1)}, u32[]{:S(2)}, u32[]{:S(2)}) collective-permute-start(bf16[128,512]{1,0:T(8,128)(2,1)S(1)} %get-tuple-element.151), channel_id=1, source_target_pairs={{0,24},{4,28},{8,16},{12,20},{16,8},{20,12},{24,0},{28,4},{1,25},{... | collective-permute-start | bytes 393224 | tf_op jit(solution)/shard_map/ppermute | solution.py:322
  (61 other events, 397.1 us)

commit v2 on v1

--- a/solution.py
+++ b/solution.py
@@ -119,19 +119,38 @@
     return jnp.sum(values.astype(F32), axis=0, keepdims=True)
 
 
+THIRDS = (0, 336, 672)
+THIRD = 352
+HELD = (
+    (0, 0, 0), (6, 4, 5), (9, 5, 8), (8, 9, 7),
+    (1, 2, 3), (5, 2, 3), (6, 3, 9), (8, 9, 2),
+)
+
+
 def forward_one(
-    me_ref, x_ref, c_ref, allow_ref, gain_ref, shift_ref, w_ref, b_ref,
-    o_ref, q_ref, k_ref, v_ref, p_ref, o_scr,
+    me_ref, x_ref, y1, y2, y3, p1, p2, p3, m1, m2, m3,
+    allow_ref, gain_ref, shift_ref, w_ref, b_ref,
+    o_ref, c_ref, q_ref, k_ref, v_ref, p_ref, o_scr,
 ):
     me = me_ref[0]
+    got = (None, y1, y2, y3, p1, p2, p3, m1, m2, m3)
+    for position, held in enumerate(HELD):
+
+        @pl.when(me_ref[2] == position)
+        def _(held=held):
+            for start, index in zip(THIRDS, held):
+                rows = slice(start, start + THIRD)
+                c_ref[rows] = x_ref[rows] if index == 0 else got[index][...]
+
     gain, shift = gain_ref[...], shift_ref[...]
     matrix = swap_matrix(256)
     for d in range(4):
-        unit, _ = norm_parts(x_ref[d ^ me].astype(F32))
+        rows = slice(d * 256, (d + 1) * 256)
+        unit, _ = norm_parts(x_ref[rows].astype(F32))
         act = swap(matrix, (unit * gain + shift).astype(BF))
         q = (mm(act, w_ref[:, :512]) + b_ref[:, :512]).astype(BF) * SCALE
         q_ref[:, d] = q.astype(BF).reshape(16, 16, 512)
-        unit, _ = norm_parts(c_ref[d].astype(F32))
+        unit, _ = norm_parts(c_ref[rows].astype(F32))
         act = swap(matrix, (unit * gain + shift).astype(BF))
         kv = mm(act, w_ref[:, 512:])
         k_ref[:, d] = kv[:, :512].astype(BF).reshape(16, 16, 512)
@@ -150,7 +169,7 @@
 
     lax.fori_loop(0, 8, body, 0)
     for d in range(4):
-        o_ref[d] = swap(matrix, o_scr[:, d].reshape(256, 512))
+        o_ref[d] = swap(matrix, o_scr[:, d ^ me].reshape(256, 512))
 
 
 def middle(
@@ -243,16 +262,16 @@
 
 
 def backward_one(
-    me_ref, gb1_ref, x_ref, c_ref, q_ref, k_ref, v_ref, p_ref, gain_ref, shift_ref, w_ref, wm_ref,
-    base_ref, term_ref, act_ref, dq_ref, cact_ref, dkv_ref, vec_ref,
-    go_scr, dq_scr, dkv_scr,
+    me_ref, gb1_ref, c_ref, q_ref, k_ref, v_ref, p_ref, gain_ref, shift_ref, w_ref, wm_ref,
+    ta_ref, tb_ref, tc_ref, cact_ref, dkv_ref, dq_ref, vec_ref,
+    go_scr, dkv_scr, t_scr,
 ):
     me = me_ref[0]
     gain, shift = gain_ref[...], shift_ref[...]
     matrix = swap_matrix(256)
     masks, masks32 = head_masks(BF), head_masks(F32)
     for d in range(4):
-        go = mm(gb1_ref[d], wm_ref[...], 1, 1).astype(BF)
+        go = mm(gb1_ref[d ^ me], wm_ref[...], 1, 1).astype(BF)
         go_scr[:, d] = swap(matrix, go).reshape(16, 16, 512)
 
     def body(i, carry):
@@ -260,45 +279,138 @@
             f = i * 2 + j
             q, k, v, go = (r[f].reshape(64, 512) for r in (q_ref, k_ref, v_ref, go_scr))
             dq, dk, dv = attend_back(q, k, v, p_ref[f], go, masks, masks32)
-            dq_scr[f] = dq.reshape(4, 16, 512)
+            dq_ref[f] = dq.reshape(4, 16, 512)
             dkv_scr[f] = jnp.concatenate([dk, dv], axis=1).reshape(4, 16, 1024)
         return carry
 
     lax.fori_loop(0, 8, body, 0)
     gain_sum = jnp.zeros((1, 512), F32)
-    shift_sum, off_sum, q_sum, v_sum = gain_sum, gain_sum, gain_sum, gain_sum
+    shift_sum, v_sum = gain_sum, gain_sum
     for d in range(4):
-        unit, inverse = norm_parts(x_ref[d ^ me].astype(F32))
-        act_ref[d] = (unit * gain + shift).astype(BF)
-        dq = swap(matrix, dq_scr[:, d].reshape(256, 512))
-        dq_ref[d] = dq
-        back = mm(dq, w_ref[:, :512], 1, 1)
-        base_ref[d] = gb1_ref[d].astype(F32) + norm_back(back, unit, inverse, gain)
-        gain_sum += col_sum(back * unit)
-        shift_sum += col_sum(back)
-        off_sum += col_sum(gb1_ref[d])
-        q_sum += col_sum(dq)
-        unit, inverse = norm_parts(c_ref[d].astype(F32))
-        cact_ref[d] = (unit * gain + shift).astype(BF)
+        rows = slice(d * 256, (d + 1) * 256)
+        unit, inverse = norm_parts(c_ref[rows].astype(F32))
+        cact_ref[rows] = (unit * gain + shift).astype(BF)
         dkv = swap(matrix, dkv_scr[:, d].reshape(256, 1024))
-        dkv_ref[d] = dkv
+        dkv_ref[rows] = dkv
         back = mm(dkv, w_ref[:, 512:], 1, 1)
-        term_ref[d] = back.astype(BF)
+        t_scr[rows] = back.astype(BF)
         gain_sum += col_sum(back * unit)
         shift_sum += col_sum(back)
         v_sum += col_sum(dkv[:, 512:])
+    for ref, start in zip((ta_ref, tb_ref, tc_ref), THIRDS):
+        ref[...] = t_scr[start : start + THIRD]
+    zero = jnp.zeros((1, 512), F32)
+    vec_ref[...] = jnp.concatenate([gain_sum, shift_sum, v_sum] + [zero] * 5, axis=0)
+
+
+def backward_query(
+    me_ref, gb1_ref, x_ref, dq_ref, vecc_ref, gain_ref, shift_ref, w_ref,
+    base_ref, act_ref, dqn_ref, vec_ref,
+):
+    me = me_ref[0]
+    gain, shift = gain_ref[...], shift_ref[...]
+    matrix = swap_matrix(256)
+    gain_sum, shift_sum, v_sum = vecc_ref[0:1], vecc_ref[1:2], vecc_ref[2:3]
+    off_sum = jnp.zeros((1, 512), F32)
+    q_sum = off_sum
+    for d in range(4):
+        rows = slice(d * 256, (d + 1) * 256)
+        unit, inverse = norm_parts(x_ref[rows].astype(F32))
+        act_ref[rows] = (unit * gain + shift).astype(BF)
+        dq = swap(matrix, dq_ref[:, d].reshape(256, 512))
+        dqn_ref[rows] = dq
+        back = mm(dq, w_ref[:, :512], 1, 1)
+        gb1 = gb1_ref[d ^ me]
+        base_ref[rows] = gb1.astype(F32) + norm_back(back, unit, inverse, gain)
+        gain_sum += col_sum(back * unit)
+        shift_sum += col_sum(back)
+        off_sum += col_sum(gb1)
+        q_sum += col_sum(dq)
     zero = jnp.zeros((1, 512), F32)
     vec_ref[...] = jnp.concatenate(
         [gain_sum, shift_sum, off_sum, q_sum, v_sum, zero, zero, zero], axis=0
     )
 
 
-def finish(
-    me_ref, base_ref, sum_ref, x_ref, gain_ref, out_ref,
+def finish(me_ref, base_ref, a_ref, b_ref, c_ref, x_ref, gain_ref, out_ref):
+    owner = me_ref[1] == 1
+
+    @pl.when(owner)
+    def _():
+        for ref, start, rows in ((a_ref, 0, 336), (b_ref, 336, 336), (c_ref, 672, 352)):
+            at = slice(start, start + rows)
+            unit, inverse = norm_parts(x_ref[at].astype(F32))
+            extra = norm_back(ref[:rows], unit, inverse, gain_ref[...])
+            out_ref[at] = (base_ref[at] + extra).astype(BF)
+
+    @pl.when(jnp.logical_not(owner))
+    def _():
+        out_ref[...] = base_ref[...].astype(BF)
+
+
+def shard_of(me_ref, dy, d1, d3):
+    return ((me_ref[6] ^ d1 ^ (3 * d3)) * 2) + (me_ref[5] ^ dy)
+
+
+BITS = [(a, b, c) for a in range(2) for b in range(2) for c in range(2)]
+
+
+def grads_reduce(me_ref, hid_ref, gb3_ref, keep_ref, send_ref, scr):
+    core = me_ref[3]
+    for i in range(8):
+        scr[i * 256 : (i + 1) * 256] = mm(
+            hid_ref[:, i * 256 : (i + 1) * 256], gb3_ref[...], 0, 0
+        ).astype(BF)
+    for i, (d1, d3, dy) in enumerate(BITS):
+        start = shard_of(me_ref, dy, d1, d3) * 256
+        keep_ref[i] = scr[pl.ds(pl.multiple_of(start + core * 128, 128), 128)]
+        send_ref[i] = scr[pl.ds(pl.multiple_of(start + (1 - core) * 128, 128), 128)]
+
+
+def grads_expand(me_ref, act_ref, gu_ref, keep_ref, send_ref, scr):
+    core = me_ref[3]
+    for n in range(4):
+        scr[n] = mm(act_ref[...], gu_ref[:, n * 512 : (n + 1) * 512], 0, 0).astype(BF)
+    for i, (dy, d1, d3) in enumerate(BITS):
+        rows = pl.ds(pl.multiple_of(shard_of(me_ref, dy, d1, d3) * 64, 64), 64)
+        for u in range(2):
+            keep_ref[i, u] = scr[2 * core + u, rows]
+            send_ref[i, u] = scr[2 * (1 - core) + u, rows]
+
+
+def grads_feature(me_ref, act_ref, dqkv_ref, o_ref, gb_ref, keep_ref, send_ref, scr):
+    core, xx = me_ref[3], me_ref[4]
+    for n in range(3):
+        scr[n] = mm(act_ref[...], dqkv_ref[:, n * 512 : (n + 1) * 512], 0, 0).astype(BF)
+    scr[3] = mm(o_ref[...], gb_ref[...], 0, 0).astype(BF)
+    for i, (dy, d1, d3) in enumerate(BITS):
+        rows = pl.ds(pl.multiple_of(shard_of(me_ref, dy, d1, d3) * 64, 64), 64)
+        for dx in range(2):
+            keep_ref[dx, i] = scr[2 * core + (dx ^ xx), rows]
+            send_ref[dx, i] = scr[2 * (1 - core) + (dx ^ xx), rows]
+
+
+def grads_sample(
+    me_ref, act_ref, dq_ref, cact_ref, dkv_ref, o_ref, gb1_ref,
+    keepx_ref, sendx_ref, keepy_ref, sendy_ref, scr,
 ):
-    unit, inverse = norm_parts(x_ref[0].astype(F32))
-    extra = norm_back(sum_ref[0].astype(F32), unit, inverse, gain_ref[...])
-    out_ref[0] = (base_ref[0] + jnp.where(me_ref[1] == 1, extra, 0.0)).astype(BF)
+    core, xx = me_ref[3], me_ref[4]
+    scr[0] = mm(act_ref[...], dq_ref[...], 0, 0).astype(BF)
+    scr[1] = mm(cact_ref[...], dkv_ref[:, :512], 0, 0).astype(BF)
+    scr[2] = mm(cact_ref[...], dkv_ref[:, 512:], 0, 0).astype(BF)
+    total = jnp.zeros((512, 512), F32)
+    for d in range(4):
+        total += mm(o_ref[d], gb1_ref[d], 0, 0)
+    scr[3] = total.astype(BF)
+    for i, (dy, d1, d3) in enumerate(BITS):
+        start = shard_of(me_ref, dy, d1, d3) * 64
+        rows = pl.ds(pl.multiple_of(start, 64), 64)
+        keepy_ref[i] = scr[2 * core + 1, rows]
+        sendy_ref[i] = scr[2 * (1 - core) + 1, rows]
+        for dx in range(2):
+            rows = pl.ds(pl.multiple_of(start + (dx ^ xx) * 32, 32), 32)
+            keepx_ref[dx, i] = scr[2 * core, rows]
+            sendx_ref[dx, i] = scr[2 * (1 - core), rows]
 
 
 def spec(shape, index=None):
@@ -317,49 +429,110 @@
     return vector.reshape(1, -1)
 
 
-def shuffle(value, axis, mask, names=None):
+def whole(kernel, name, outs, scratch, *inputs):
+    return pl.pallas_call(
+        kernel,
+        out_shape=outs,
+        in_specs=[pl.BlockSpec(memory_space=pltpu.SMEM)] + [pl.BlockSpec()] * (len(inputs) - 1),
+        scratch_shapes=scratch,
+        compiler_params=params(),
+        name=name,
+    )(*inputs)
+
+
+def shuffle(value, axis, mask):
     size = lax.axis_size(axis)
     return lax.ppermute(value, axis, [(i, i ^ mask) for i in range(size)])
 
 
+CORE, X, Y, Z, Z3 = ("feat", 1), ("feat", 2), ("samp", 1), ("samp", 2), ("samp", 6)
+
+
+def turn(value, step):
+    return lax.ppermute(value, "samp", [(i, (i + 2 * step) % 8) for i in range(8)])
+
+
 def at(stacked, index, axis=0):
     return lax.dynamic_index_in_dim(stacked, index, axis, keepdims=False)
 
 
-def swap_blocks(blocks, me, axis):
+def swap_blocks(blocks, axis):
     return [blocks[0]] + [shuffle(blocks[d], axis, d) for d in range(1, len(blocks))]
 
 
-def reduce_rows(buffer, samp, core):
-    zz, yy = samp // 2, samp % 2
-    halves = buffer.reshape(8, 2, 128, 512)
-    got = shuffle(at(halves, 1 - core, 1), "feat", 1)
-    part = (at(halves, core, 1).astype(F32) + got.astype(F32)).astype(BF)
-    part = part.reshape(4, 2, 128, 512)
-    got = shuffle(at(part, 1 - yy, 1), "samp", 1)
-    part = (at(part, yy, 1).astype(F32) + got.astype(F32)).astype(BF)
-    total = at(part, zz).astype(F32)
-    for d in range(1, 4):
-        total = total + shuffle(at(part, zz ^ d), "samp", 2 * d).astype(F32)
-    mine = total.astype(BF)
-    total = mine.astype(F32) + shuffle(mine, "feat", 2).astype(F32)
-    mine = total.astype(BF)
-    other = shuffle(mine, "feat", 1)
-    first = jnp.where(core == 0, mine, other)
-    second = jnp.where(core == 0, other, mine)
-    return jnp.concatenate([first, second], axis=0).astype(F32)
+def plus(a, b):
+    return (a.astype(F32) + b.astype(F32)).astype(BF)
+
+
+def halve(keep, sent, where):
+    got = shuffle(sent, *where)
+    return plus(keep[0], got[0]), plus(keep[1], got[1])
+
+
+def join_two(mine, index, where):
+    other = shuffle(mine, *where)
+    return jnp.stack([jnp.where(index == 0, mine, other), jnp.where(index == 0, other, mine)])
+
+
+def chain(keep, sent, dims):
+    mine, out = halve(keep, sent, CORE)
+    for i, where in enumerate(dims):
+        if i == len(dims) - 1:
+            return plus(mine, shuffle(out, *where))
+        mine, out = halve(mine, out, where)
+
+
+def send_context(x, position):
+    dy, dz = position // 4, position % 4
+    owner = position == 0
+    a, b, c = (x[start : start + THIRD] for start in THIRDS)
+    y1, p1, m1 = shuffle(a, *Y), turn(b, 1), turn(c, -1)
+    pick = jnp.where
+    y2 = shuffle(pick(owner, b, pick(dz == 1, p1, m1)), *Y)
+    p2 = turn(pick(owner, c, pick(dy == 1, y1, p1)), 1)
+    m2 = turn(pick(owner, a, pick(dy == 1, y1, m1)), -1)
+    y3 = shuffle(pick(owner, c, p2), *Y)
+    p3 = turn(pick(owner, a, p2), 1)
+    m3 = turn(pick(owner, b, pick((dy == 0) & (dz == 3), m2, y2)), -1)
+    return y1, y2, y3, p1, p2, p3, m1, m2, m3
+
+
+def sum_context(a, b, c, position):
+    pick = jnp.where
+
+    def to(places):
+        hit = position == places[0]
+        for place in places[1:]:
+            hit = hit | (position == place)
+        return hit
+
+    def add(value, places, got):
+        return pick(to(places), plus(value, got), value)
+
+    y = shuffle(pick(to([6]), b, c), *Y)
+    m = turn(a, -1)
+    p = turn(pick(to([3, 7]), b, pick(to([2]), a, c)), 1)
+    a, b, c = (
+        add(add(a, [0, 5], m), [3], p),
+        add(add(b, [2], y), [0, 4], p),
+        add(add(c, [0, 1], y), [7], p),
+    )
+    y = shuffle(pick(to([7]), c, b), *Y)
+    m = turn(pick(to([1]), c, pick(to([5]), a, b)), -1)
+    p = turn(pick(to([2]), c, a), 1)
+    a, b, c = (
+        add(add(a, [4], m), [0, 4], p),
+        add(add(b, [0, 1], y), [1], m),
+        add(add(add(c, [3], y), [0], m), [3], p),
+    )
+    y, m, p = shuffle(a, *Y), turn(b, -1), turn(c, 1)
+    return tuple(u.astype(F32) + v.astype(F32) for u, v in ((a, y), (b, m), (c, p)))
 
 
 def sum_everywhere(value):
-    for axis, mask in (("feat", 1), ("feat", 2), ("samp", 1), ("samp", 2), ("samp", 4)):
-        value = value + shuffle(value, axis, mask)
+    for where in (CORE, X, Y, Z, Z3):
+        value = value + shuffle(value, *where)
     return value
-
-
-def rows_of(grad):
-    return jnp.concatenate(
-        [grad[:, c : c + 512].reshape(8, 64, 512) for c in range(0, grad.shape[1], 512)], axis=1
-    )
 
 
 def local_small(
@@ -369,46 +542,33 @@
     third_gain, third_shift, expand_weight, expand_bias, reduce_weight, reduce_bias, cotangent,
 ):
     samp, feat = lax.axis_index("samp"), lax.axis_index("feat")
-    core = feat % 2
+    core, xx = feat % 2, feat // 2
+    yy, zz = samp % 2, samp // 2
     flags = context_flags.reshape(8, 64)[:, 0]
-    root = jnp.argmax(flags).astype(jnp.int32)
-    me = jnp.stack([feat, (root == samp).astype(jnp.int32), samp, core]).astype(jnp.int32)
-
-    pieces = layer_input.reshape(8, 128, 512)
-    sent = [at(pieces, samp)] + [shuffle(at(pieces, samp ^ d), "samp", d) for d in range(1, 8)]
-    offset = samp ^ root
-    piece = sent[0]
-    for d in range(1, 8):
-        piece = jnp.where(offset == d, sent[d], piece)
-    context = jnp.concatenate(swap_blocks([piece] * 8, samp, "samp"), axis=0).reshape(4, 256, 512)
-    order = (samp ^ jnp.arange(8, dtype=jnp.int32)) * 8
-    order = (order[:, None] + jnp.arange(8, dtype=jnp.int32)[None, :]).reshape(64)
-    context_tasks = jnp.take(jnp.take(segment_ids.reshape(8, 64), root, axis=0), order)
-    blocks_of = (feat ^ jnp.arange(4, dtype=jnp.int32)) * 16
-    blocks_of = (blocks_of[:, None] + jnp.arange(16, dtype=jnp.int32)[None, :]).reshape(64)
-    own_tasks = jnp.take(lax.dynamic_slice_in_dim(segment_ids, samp * 64, 64), blocks_of)
-    allow = (own_tasks[:, None] == context_tasks[None, :]).astype(F32)
+    root = jnp.sum(jnp.where(flags == 1, jnp.arange(8, dtype=jnp.int32), 0))
+    position = ((yy ^ (root % 2)) * 4 + (zz - root // 2 + 4) % 4).astype(jnp.int32)
+    own = (position == 0).astype(jnp.int32)
+    me = jnp.stack([feat, own, position, core, xx, yy, zz]).astype(jnp.int32)
+
+    x = layer_input.reshape(1024, 512)
+    pieces = send_context(x, position)
+    tasks = segment_ids.reshape(8, 64)
+    allow = (at(tasks, samp)[:, None] == at(tasks, root)[None, :]).astype(F32)
     allow = jnp.concatenate([allow] * 4, axis=1)
 
-    x4 = layer_input.reshape(4, 256, 512)
-    cot4 = cotangent.reshape(4, 256, 512)
-    x_f = jnp.stack(swap_blocks([at(x4, feat ^ d) for d in range(4)], feat, "feat"))
-    cot_f = jnp.stack(swap_blocks([at(cot4, feat ^ d) for d in range(4)], feat, "feat"))
+    both = jnp.stack([layer_input.reshape(4, 256, 512), cotangent.reshape(4, 256, 512)], axis=1)
+    both = swap_blocks([at(both, feat ^ d) for d in range(4)], "feat")
+    x_f = jnp.stack([pair[0] for pair in both])
+    cot_f = jnp.stack([pair[1] for pair in both])
 
     heads = sds((16, 4, 16, 512))
-    smem = pl.BlockSpec(memory_space=pltpu.SMEM)
-    o1, q1, k1, v1, p1 = pl.pallas_call(
-        forward_one,
-        out_shape=(sds((4, 256, 512)), heads, heads, heads, sds((16, 64, 512), F32)),
-        in_specs=[smem] + [pl.BlockSpec()] * 7,
-        scratch_shapes=[pltpu.VMEM((16, 4, 16, 512), BF)],
-        compiler_params=params(),
-        name="forward_one",
-    )(
-        me, x4, context, allow, row(first_gain), row(first_shift), sample_weight,
-        row(sample_bias),
-    )
-    o1_f = jnp.stack(swap_blocks([o1[d] for d in range(4)], feat, "feat"))
+    o1, context, q1, k1, v1, p1 = whole(
+        forward_one, "forward_one",
+        (sds((4, 256, 512)), sds((1024, 512)), heads, heads, heads, sds((16, 64, 512), F32)),
+        [pltpu.VMEM((16, 4, 16, 512), BF)],
+        me, x, *pieces, allow, row(first_gain), row(first_shift), sample_weight, row(sample_bias),
+    )
+    o1_f = jnp.stack(swap_blocks([o1[d] for d in range(4)], "feat"))
 
     weights = [
         sample_mixer, row(sample_offset), row(second_gain), row(second_shift), feature_weight,
@@ -435,107 +595,92 @@
         name="middle",
     )(o1_f, x_f, cot_f, *weights)
 
-    out4 = jnp.stack(swap_blocks([out_f[d] for d in range(4)], feat, "feat"))
-    gb1 = jnp.stack(swap_blocks([gb1_f[d] for d in range(4)], feat, "feat"))
+    gb1 = jnp.stack(swap_blocks([gb1_f[d] for d in range(4)], "feat"))
+    out4 = jnp.stack(swap_blocks([out_f[d] for d in range(4)], "feat"))
     order4 = feat ^ jnp.arange(4, dtype=jnp.int32)
     layer_output = jnp.take(out4, order4, axis=0).reshape(64, 16, 512)
 
-    grad = lambda a, b: jnp.einsum("td,te->de", a, b, preferred_element_type=F32).astype(BF)
-    reduce_rows_grad = reduce_rows(grad(hidden, gb3).reshape(8, 256, 512), samp, core)
-    expand_rows = reduce_rows(rows_of(grad(act3, gu)), samp, core)
-    feature_rows = reduce_rows(
-        jnp.concatenate([rows_of(grad(act2, dqkv)), rows_of(grad(o2, gb2))], axis=1), samp, core
-    )
-
-    base, term, act1, dq1, cact, dkv, vec1 = pl.pallas_call(
-        backward_one,
-        out_shape=(
-            sds((4, 256, 512), F32), sds((4, 256, 512)), sds((4, 256, 512)), sds((4, 256, 512)),
-            sds((4, 256, 512)), sds((4, 256, 1024)), sds((8, 512), F32),
-        ),
-        in_specs=[smem] + [pl.BlockSpec()] * 11,
-        scratch_shapes=[
-            pltpu.VMEM((16, 4, 16, 512), BF),
+    rk, rs = whole(
+        grads_reduce, "grads_reduce", (sds((8, 128, 512)), sds((8, 128, 512))),
+        [pltpu.VMEM((2048, 512), BF)], me, hidden, gb3,
+    )
+    ek, es = whole(
+        grads_expand, "grads_expand", (sds((8, 2, 64, 512)), sds((8, 2, 64, 512))),
+        [pltpu.VMEM((4, 512, 512), BF)], me, act3, gu,
+    )
+    fk, fs = whole(
+        grads_feature, "grads_feature", (sds((2, 8, 64, 512)), sds((2, 8, 64, 512))),
+        [pltpu.VMEM((4, 512, 512), BF)], me, act2, dqkv, o2, gb2,
+    )
+    three = lambda a: a.reshape((2, 2, 2) + a.shape[1:])
+    four = lambda a: a.reshape((2, 2, 2, 2) + a.shape[2:])
+    r_part = chain(three(rk), three(rs), (Z, Z3, Y))
+    e_part = chain(three(ek), three(es), (Y, Z, Z3))
+    f_part = chain(four(fk), four(fs), (X, Y, Z, Z3))
+
+    third = sds((THIRD, 512))
+    ta, tb, tc, cact, dkv, dq_heads, vec_c = whole(
+        backward_one, "backward_one",
+        (third, third, third, sds((1024, 512)), sds((1024, 1024)), heads, sds((8, 512), F32)),
+        [
             pltpu.VMEM((16, 4, 16, 512), BF),
             pltpu.VMEM((16, 4, 16, 1024), BF),
+            pltpu.VMEM((1024, 512), BF),
         ],
-        compiler_params=params(),
-        name="backward_one",
-    )(
-        me, gb1, x4, context, q1, k1, v1, p1, row(first_gain), row(first_shift), sample_weight,
+        me, gb1, context, q1, k1, v1, p1, row(first_gain), row(first_shift), sample_weight,
         sample_mixer,
     )
-
-    terms = term.reshape(8, 128, 512)
-    total = terms[0].astype(F32)
-    for d in range(1, 8):
-        total = total + shuffle(terms[d], "samp", d).astype(F32)
-    summed = jnp.stack(swap_blocks([total.astype(BF)] * 8, samp, "samp"))
-    order8 = samp ^ jnp.arange(8, dtype=jnp.int32)
-    summed = jnp.take(summed, order8, axis=0).reshape(4, 256, 512)
-
-    flat = lambda a: a.reshape(1024, -1)
-    sample_rows = reduce_rows(
-        jnp.concatenate(
-            [
-                rows_of(grad(flat(act1), flat(dq1))),
-                rows_of(grad(flat(cact), flat(dkv))),
-                rows_of(grad(flat(o1), flat(gb1))),
-            ],
-            axis=1,
-        ),
-        samp,
-        core,
-    )
+    sums = sum_context(ta, tb, tc, position)
+    base, act1, dq1, vec1 = whole(
+        backward_query, "backward_query",
+        (sds((1024, 512), F32), sds((1024, 512)), sds((1024, 512)), sds((8, 512), F32)),
+        [],
+        me, gb1, x, dq_heads, vec_c, row(first_gain), row(first_shift), sample_weight,
+    )
+    sxk, sxs, syk, sys_ = whole(
+        grads_sample, "grads_sample",
+        (sds((2, 8, 32, 512)), sds((2, 8, 32, 512)), sds((8, 64, 512)), sds((8, 64, 512))),
+        [pltpu.VMEM((4, 512, 512), BF)],
+        me, act1, dq1, cact, dkv, o1, gb1,
+    )
+    sx_part = chain(four(sxk), four(sxs), (X, Y, Z, Z3))
+    sy_part = chain(three(syk), three(sys_), (Y, Z, Z3))
+
     vectors = sum_everywhere(
         jnp.concatenate([vec2.reshape(-1), bias2.reshape(-1), vec1.reshape(-1)])
     )
 
-    input_grad = pl.pallas_call(
-        finish,
-        grid_spec=pltpu.PrefetchScalarGridSpec(
-            num_scalar_prefetch=1,
-            grid=(4,),
-            in_specs=[
-                spec((1, 256, 512), lambda i, m: (i ^ m[0], 0, 0)),
-                spec((1, 256, 512), lambda i, m: (i, 0, 0)),
-                spec((1, 256, 512), lambda i, m: (i, 0, 0)),
-                spec((1, 512)),
-            ],
-            out_specs=spec((1, 256, 512), lambda i, m: (i, 0, 0)),
-        ),
-        out_shape=sds((4, 256, 512)),
-        compiler_params=params(),
-        name="finish",
-    )(me, base, summed, x4, row(first_gain)).reshape(64, 16, 512)
+    both_x = lambda part: plus(part, shuffle(part, *X))
+    reduce_grad = join_two(both_x(r_part), core, CORE).reshape(256, 512).astype(F32)
+    expand_blocks = join_two(both_x(e_part), core, CORE).reshape(4, 64, 512).astype(F32)
+    feature_blocks = join_two(join_two(f_part, xx, X), core, CORE).reshape(4, 64, 512).astype(F32)
+    sx = join_two(f_or_s(sx_part, xx), core, CORE).astype(F32)
+    sy = join_two(both_x(sy_part), core, CORE).astype(F32)
+
+    input_grad = whole(
+        finish, "finish", sds((1024, 512)), [], me, base, *sums, x, row(first_gain)
+    ).reshape(64, 16, 512)
 
     def vector(start, size):
         return lax.dynamic_slice_in_dim(vectors[start : start + size], samp * (size // 8), size // 8)
 
-    gain3, shift3, gain2, shift2, off2, bias_r, qs2, vs2 = (vector(i * 512, 512) for i in range(8))
+    gain3, shift3, gain2, shift2, off2, bias_r = (vector(i * 512, 512) for i in range(6))
     expand_b = vector(4096, 2048)
-    gain1, shift1, off1, qs1, vs1 = (vector(6144 + i * 512, 512) for i in range(5))
-
-    def joined(first, second):
-        both = jnp.concatenate([vectors[first : first + 512], vectors[second : second + 512]])
-        return lax.dynamic_slice_in_dim(both, samp * 128, 128)
-
-    columns = lambda rows, first, count: jnp.concatenate(
-        [rows[64 * (first + i) : 64 * (first + i + 1)] for i in range(count)], axis=1
-    )
-
-    def unmix(rows):
-        return rows
+    gain1, shift1, off1 = (vector(6144 + i * 512, 512) for i in range(3))
+    columns = lambda blocks: jnp.concatenate(blocks, axis=1)
 
     return (
         layer_output, input_grad,
-        gain1, shift1, columns(sample_rows, 0, 3), joined(6144 + 3 * 512, 6144 + 4 * 512),
-        columns(sample_rows, 3, 1), off1,
-        gain2, shift2, columns(feature_rows, 0, 3), joined(6 * 512, 7 * 512),
-        columns(feature_rows, 3, 1), off2,
-        gain3, shift3, columns(expand_rows, 0, 4), expand_b,
-        reduce_rows_grad, bias_r,
-    )
+        gain1, shift1, columns([sx[0], sy[0], sx[1]]), vector(6144 + 3 * 512, 1024), sy[1], off1,
+        gain2, shift2, columns([feature_blocks[i] for i in range(3)]), vector(6 * 512, 1024),
+        feature_blocks[3], off2,
+        gain3, shift3, columns([expand_blocks[i] for i in range(4)]), expand_b,
+        reduce_grad, bias_r,
+    )
+
+
+def f_or_s(half, xx):
+    return join_two(half, xx, X).reshape(64, 512)
 
 
 def spread_2(block, axis, owner):

time: 411 us -> 403 us (0.981)
  Pallas kernels: 104 us -> 132 us
  starting transfers between devices: 103 us -> 75.1 us
  waiting for transfers between devices: 109 us -> 131 us
  matrix products: 16.9 us -> 0 us
  local copies, waits for them, and re-layouts: 42 us -> 26.6 us
    ppermute x76 -> x55, starting transfers between devices: 103 us -> 50.6 us  [shuffle(): return lax.ppermute(value, axis, [(i, i ^ mask) for i in range(size)])]
    ppermute x0 -> x12, waiting for transfers between devices: none -> 37.7 us  [turn(): lax.ppermute(value, 'samp', [(i, (i + 2 * step) % 8) for i in range(8)])]
    pallas_call x3 -> x8, Pallas kernels: 51.6 us -> 80.7 us  [whole(): pl.pallas_call(kernel, out_shape=outs, in_specs=[pl.BlockSpec(memory_spac...]
    ppermute x0 -> x12, starting transfers between devices: none -> 24.4 us  [turn(): lax.ppermute(value, 'samp', [(i, (i + 2 * step) % 8) for i in range(8)])]
    dot_general x7 -> x0, matrix products: 16.9 us -> none  [local_small(): jnp.einsum('td,te->de', a, b, preferred_element_type=F32).astype(BF)]
    ppermute x76 -> x55, waiting for transfers between devices: 109 us -> 93.7 us  [shuffle(): return lax.ppermute(value, axis, [(i, i ^ mask) for i in range(size)])]
    slice x10 -> x13, local copies, waits for them, and re-layouts: 3.3 us -> 14.8 us  [the longest x5 7.9 us: halve(): return (plus(keep[0], got[0]), plus(keep[1], got[1]))]
    unnamed x80 -> x68, local copies, waits for them, and re-layouts: 12.4 us -> 1.66 us
  transfers between devices with their start and end apart: 76 -> 67, of which waited for: 34 -> 31; matrix products, arithmetic and copies ran while one was open for 16% -> 12% of each run, Pallas kernels for 13% -> 19%
where the time goes in v2:
time: 403 us; the launch traced here: 397 us
  Pallas kernels  132 us (33%)
  waiting for transfers between devices  131 us (33%)
  starting transfers between devices  75.1 us (19%)
  local copies, waits for them, and re-layouts  26.6 us (7%)
  other arithmetic  25.8 us (6%)
  between operations  5.77 us (1%)
    ppermute x55, waiting for transfers between devices, shuffle(): return lax.ppermute(value, axis, [(i, i ^ mask) for i in range(size)])  93.7 us
    pallas_call x8, Pallas kernels, whole(): pl.pallas_call(kernel, out_shape=outs, in_specs=[pl.BlockSpec(memory_spac...  80.7 us
    pallas_call x1, Pallas kernels, local_small(): pl.pallas_call(middle, grid=(4,), out_shape=(sds((4, 256, 512)), sds((4,...  51.7 us
    ppermute x55, starting transfers between devices, shuffle(): return lax.ppermute(value, axis, [(i, i ^ mask) for i in range(size)])  50.6 us
    ppermute x12, waiting for transfers between devices, turn(): lax.ppermute(value, 'samp', [(i, (i + 2 * step) % 8) for i in range(8)])  37.7 us
    ppermute x12, starting transfers between devices, turn(): lax.ppermute(value, 'samp', [(i, (i + 2 * step) % 8) for i in range(8)])  24.4 us
  transfers between devices with their start and end apart: 67, of which 31 were waited for; matrix products, arithmetic and copies ran while one was open for 12% of the time, Pallas kernels for 19%

profile of v2, /device:TPU:0, one launch (start us, length us, event | category | flops | bytes accessed | tf_op | source)
XLA Modules:
  0.0 397.0 jit_solution(3769475018669489690)
XLA Ops:
  2.0 3.1 collective-permute-start.1
  6.6 2.4 fusion.33
  15.8 2.3 collective-permute-start.2
  19.2 7.7 %collective-permute-done.2.m1 = bf16[352,512]{1,0:T(8,128)(2,1)S(1)} collective-permute-done((bf16[352,512]{1,0:T(8,128)(2,1)S(1)}, bf16[352,512]{1,0:T(8,128)(2,1)S(1)}, u32[]{:S(2)}, u32[]{:S(2)}) %collective-permute-start.2) | collective-permute-done | bytes 360480 | tf_op jit(solution)/shard_map/ppermute | solution.py:452
  26.9 9.3 %collective-permute-done.4.p2 = bf16[352,512]{1,0:T(8,128)(2,1)S(1)} collective-permute-done((bf16[352,512]{1,0:T(8,128)(2,1)S(1)}, bf16[352,512]{1,0:T(8,128)(2,1)S(1)}, u32[]{:S(2)}, u32[]{:S(2)}) %collective-permute-start.4) | collective-permute-done | bytes 360480 | tf_op jit(solution)/shard_map/ppermute | solution.py:452
  41.3 6.0 %collective-permute-done.3.y2 = bf16[352,512]{1,0:T(8,128)(2,1)S(1)} collective-permute-done((bf16[352,512]{1,0:T(8,128)(2,1)}, bf16[352,512]{1,0:T(8,128)(2,1)S(1)}, u32[]{:S(2)}, u32[]{:S(2)}) %collective-permute-start.3) | collective-permute-done | bytes 360480 | tf_op jit(solution)/shard_map/ppermute | solution.py:445
  48.3 4.2 %collective-permute-start.8 = (bf16[352,512]{1,0:T(8,128)(2,1)S(1)}, bf16[352,512]{1,0:T(8,128)(2,1)S(1)}, u32[]{:S(2)}, u32[]{:S(2)}) collective-permute-start(bf16[352,512]{1,0:T(8,128)(2,1)S(1)} %select_select_fusion.2), channel_id=1, source_target_pairs={{0,24},{4,28},{8,0},{12,4},{16,8},{20,12},{24,16},{28,20},{1,25},{... | collective-permute-start | bytes 1081352 | tf_op jit(solution)/shard_map/ppermute | solution.py:452
  56.2 5.5 %collective-permute-done.6.p3 = bf16[352,512]{1,0:T(8,128)(2,1)S(1)} collective-permute-done((bf16[352,512]{1,0:T(8,128)(2,1)S(1)}, bf16[352,512]{1,0:T(8,128)(2,1)S(1)}, u32[]{:S(2)}, u32[]{:S(2)}) %collective-permute-start.6) | collective-permute-done | bytes 360480 | tf_op jit(solution)/shard_map/ppermute | solution.py:452
  61.7 3.2 collective-permute-done.8.m3
  65.6 22.5 %forward_one.1 = (bf16[4,256,512]{2,1,0:T(8,128)(2,1)}, bf16[1024,512]{1,0:T(8,128)(2,1)}, bf16[16,4,16,512]{3,2,1,0:T(8,128)(2,1)}, bf16[16,4,16,512]{3,2,1,0:T...) custom-call(s32[7]{0:T(128)} %stack.143.me_ref, bf16[1024,512]{1,0:T(8,128)(2,1)} %bitcast.339, ...), custom_call_target="tpu_custom_call" | custom-call | tf_op jit(solution)/shard_map/forward_one/pallas_call | solution.py:433
  94.2 4.6 %collective-permute-done.10 = bf16[256,512]{1,0:T(8,128)(2,1)S(1)} collective-permute-done((bf16[256,512]{1,0:T(8,128)(2,1)S(1)}, bf16[256,512]{1,0:T(8,128)(2,1)S(1)}, u32[]{:S(2)}, u32[]{:S(2)}) %collective-permute-start.10) | collective-permute-done | bytes 262176 | tf_op jit(solution)/shard_map/ppermute | solution.py:445
  98.8 4.7 %collective-permute-done.11 = bf16[256,512]{1,0:T(8,128)(2,1)S(1)} collective-permute-done((bf16[256,512]{1,0:T(8,128)(2,1)S(1)}, bf16[256,512]{1,0:T(8,128)(2,1)S(1)}, u32[]{:S(2)}, u32[]{:S(2)}) %collective-permute-start.11) | collective-permute-done | bytes 262176 | tf_op jit(solution)/shard_map/ppermute | solution.py:445
  104.6 51.7 %middle.1 = (bf16[4,256,512]{2,1,0:T(8,128)(2,1)}, bf16[4,256,512]{2,1,0:T(8,128)(2,1)}, bf16[1024,512]{1,0:T(8,128)(2,1)}, bf16[1024,1536]{1,0:T(8,128)(2,1)}, ...) custom-call(bf16[4,256,512]{2,1,0:T(8,128)(2,1)} %pad_maximum_fusion, ...), custom_call_target="tpu_custom_call" | custom-call | tf_op jit(solution)/shard_map/middle/pallas_call | solution.py:580
  156.3 6.3 %grads_reduce.1 = (bf16[8,128,512]{2,1,0:T(8,128)(2,1)}, bf16[8,128,512]{2,1,0:T(8,128)(2,1)}) custom-call(s32[7]{0:T(128)} %stack.143.me_ref, bf16[1024,2048]{1,0:T(8,128)(2,1)} %get-tuple-element.94.hid_ref, bf16[1024,512]{1,0:T(8,128)(2,1)} %get-tuple-element.95.gb3_ref), custom_call_target="tpu_custom_call" | custom-call | tf_op jit(solution)/shard_map/grads_reduce/pallas_call | solution.py:433
  162.8 2.3 fusion.86
  165.1 6.3 %grads_expand.1 = (bf16[8,2,64,512]{3,2,1,0:T(8,128)(2,1)}, bf16[8,2,64,512]{3,2,1,0:T(8,128)(2,1)}) custom-call(s32[7]{0:T(128)} %stack.143.me_ref, bf16[1024,512]{1,0:T(8,128)(2,1)} %get-tuple-element.90.act_ref, bf16[1024,2048]{1,0:T(8,128)(2,1)} %get-tuple-element.91.gu_ref), custom_call_target="tpu_custom_call" | custom-call | tf_op jit(solution)/shard_map/grads_expand/pallas_call | solution.py:433
  175.7 6.7 %grads_feature.1 = (bf16[2,8,64,512]{3,2,1,0:T(8,128)(2,1)}, bf16[2,8,64,512]{3,2,1,0:T(8,128)(2,1)}) custom-call(s32[7]{0:T(128)} %stack.143.me_ref, bf16[1024,512]{1,0:T(8,128)(2,1)} %get-tuple-element.84.act_ref, bf16[1024,1536]{1,0:T(8,128)(2,1)} %get-tuple-element.85.dqkv_ref, bf16[1024,512]{1,0:T(8,128)(2,1)} %get-tuple-element.86.o_ref, ...), custom_call_target="tpu_custom_call" | custom-call | tf_op jit(solution)/shard_map/grads_feature/pallas_call | solution.py:433
  182.4 2.3 fusion.88
  187.9 21.9 %backward_one.1 = (bf16[352,512]{1,0:T(8,128)(2,1)}, bf16[352,512]{1,0:T(8,128)(2,1)}, bf16[352,512]{1,0:T(8,128)(2,1)}, bf16[1024,512]{1,0:T(8,128)(2,1)}, bf16...) custom-call(s32[7]{0:T(128)} %stack.143.me_ref, ...), custom_call_target="tpu_custom_call" | custom-call | tf_op jit(solution)/shard_map/backward_one/pallas_call | solution.py:433
  209.9 6.6 %backward_query.1 = (f32[1024,512]{1,0:T(8,128)}, bf16[1024,512]{1,0:T(8,128)(2,1)}, bf16[1024,512]{1,0:T(8,128)(2,1)}, f32[8,512]{1,0:T(8,128)}) custom-call(s32[7]{0:T(128)} %stack.143.me_ref, bf16[4,256,512]{2,1,0:T(8,128)(2,1)} %pad_maximum_fusion.4.gb1_ref, bf16[1024,512]{1,0:T(8,128)(2,1)} %bitcast.340, ...), custom_call_target="tpu_custom_call" | custom-call | tf_op jit(solution)/shard_map/backward_query/pallas_call | solution.py:433
  218.8 6.8 %grads_sample.1 = (bf16[2,8,32,512]{3,2,1,0:T(8,128)(2,1)}, bf16[2,8,32,512]{3,2,1,0:T(8,128)(2,1)}, bf16[8,64,512]{2,1,0:T(8,128)(2,1)}, bf16[8,64,512]{2,1,0:T(8,128)(2,1)}) custom-call(s32[7]{0:T(128)} %stack.143.me_ref, bf16[1024,512]{1,0:T(8,128)(2,1)} %get-tuple-element.76.act_ref, bf16[1024,512]{1,0:T(8,128)(2,1)} %get-tuple-element.77.dq_ref, ...), custom_call_target="tpu_custom_call" | custom-call | tf_op jit(solution)/shard_map/grads_sample/pallas_call | solution.py:433
  229.7 3.7 collective-permute-start.21
  241.3 7.7 %collective-permute-done.33 = f32[10240]{0:T(1024)S(1)} collective-permute-done((f32[10240]{0:T(1024)S(1)}, f32[10240]{0:T(1024)S(1)}, u32[]{:S(2)}, u32[]{:S(2)}) %collective-permute-start.33) | collective-permute-done | bytes 40992 | tf_op jit(solution)/shard_map/ppermute | solution.py:445
  249.1 4.2 %collective-permute-start.34 = (f32[10240]{0:T(1024)S(1)}, f32[10240]{0:T(1024)S(1)}, u32[]{:S(2)}, u32[]{:S(2)}) collective-permute-start(f32[10240]{0:T(1024)S(1)} %add.326), channel_id=1, source_target_pairs={{0,24},{4,28},{8,16},{12,20},{16,8},{20,12},{24,0},{28,4},{1,25},{... | collective-permute-start | bytes 122888 | tf_op jit(solution)/shard_map/ppermute | solution.py:445
  253.4 2.0 collective-permute-done.34
  267.0 3.8 collective-permute-start.24
  273.5 6.7 %collective-permute-done.25 = bf16[352,512]{1,0:T(8,128)(2,1)S(1)} collective-permute-done((bf16[352,512]{1,0:T(8,128)(2,1)S(1)}, bf16[352,512]{1,0:T(8,128)(2,1)S(1)}, u32[]{:S(2)}, u32[]{:S(2)}) %collective-permute-start.25) | collective-permute-done | bytes 360480 | tf_op jit(solution)/shard_map/ppermute | solution.py:452
  280.2 4.9 %collective-permute-done.24 = bf16[352,512]{1,0:T(8,128)(2,1)S(1)} collective-permute-done((bf16[352,512]{1,0:T(8,128)(2,1)S(1)}, bf16[352,512]{1,0:T(8,128)(2,1)S(1)}, u32[]{:S(2)}, u32[]{:S(2)}) %collective-permute-start.24) | collective-permute-done | bytes 360480 | tf_op jit(solution)/shard_map/ppermute | solution.py:452
  287.5 4.8 %collective-permute-done.43 = bf16[2,2,64,512]{3,2,1,0:T(8,128)(2,1)S(1)} collective-permute-done((bf16[2,2,64,512]{3,2,1,0:T(8,128)(2,1)S(1)}, bf16[2,2,64,512]{3,2,1,0:T(8,128)(2,1)S(1)}, u32[]{:S(2)}, u32[]{:S(2)}) %collective-permute-start.43) | collective-permute-done | bytes 262176 | tf_op jit(solution)/shard_map/ppermute | solution.py:445
  292.3 3.1 collective-permute-start.29
  295.5 2.2 collective-permute-start.28
  301.8 8.3 %collective-permute-done.37 = bf16[2,2,32,512]{3,2,1,0:T(8,128)(2,1)S(1)} collective-permute-done((bf16[2,2,32,512]{3,2,1,0:T(8,128)(2,1)S(1)}, bf16[2,2,32,512]{3,2,1,0:T(8,128)(2,1)S(1)}, u32[]{:S(2)}, u32[]{:S(2)}) %collective-permute-start.37) | collective-permute-done | bytes 131104 | tf_op jit(solution)/shard_map/ppermute | solution.py:445
  310.2 2.1 collective-permute-start.38
  312.6 4.3 %collective-permute-done.38 = bf16[2,32,512]{2,1,0:T(8,128)(2,1)S(1)} collective-permute-done((bf16[2,32,512]{2,1,0:T(8,128)(2,1)S(1)}, bf16[2,32,512]{2,1,0:T(8,128)(2,1)S(1)}, u32[]{:S(2)}, u32[]{:S(2)}) %collective-permute-start.38) | collective-permute-done | bytes 65568 | tf_op jit(solution)/shard_map/ppermute | solution.py:445
  317.0 2.4 collective-permute-start.39
  319.4 11.6 %collective-permute-done.39 = bf16[32,512]{1,0:T(8,128)(2,1)S(1)} collective-permute-done((bf16[32,512]{1,0:T(8,128)(2,1)S(1)}, bf16[32,512]{1,0:T(8,128)(2,1)S(1)}, u32[]{:S(2)}, u32[]{:S(2)}) %collective-permute-start.39) | collective-permute-done | bytes 32800 | tf_op jit(solution)/shard_map/ppermute | solution.py:445
  332.8 4.3 %collective-permute-done.45 = bf16[64,512]{1,0:T(8,128)(2,1)S(1)} collective-permute-done((bf16[64,512]{1,0:T(8,128)(2,1)S(1)}, bf16[64,512]{1,0:T(8,128)(2,1)S(1)}, u32[]{:S(2)}, u32[]{:S(2)}) %collective-permute-start.45) | collective-permute-done | bytes 65568 | tf_op jit(solution)/shard_map/ppermute | solution.py:445
  338.5 2.5 collective-permute-done.40
  342.4 3.5 collective-permute-done.46
  351.6 3.6 finish.1
  356.9 2.4 collective-permute-start.63
  360.6 7.3 %collective-permute-done.63 = bf16[2,128,512]{2,1,0:T(8,128)(2,1)S(1)} collective-permute-done((bf16[2,128,512]{2,1,0:T(8,128)(2,1)S(1)}, bf16[2,128,512]{2,1,0:T(8,128)(2,1)S(1)}, u32[]{:S(2)}, u32[]{:S(2)}) %collective-permute-start.63) | collective-permute-done | bytes 262176 | tf_op jit(solution)/shard_map/ppermute | solution.py:445
  369.5 3.1 collective-permute-done.57
  372.6 2.0 collective-permute-start.58
  375.7 6.6 %collective-permute-done.51 = bf16[2,64,512]{2,1,0:T(8,128)(2,1)S(1)} collective-permute-done((bf16[2,64,512]{2,1,0:T(8,128)(2,1)S(1)}, bf16[2,64,512]{2,1,0:T(8,128)(2,1)S(1)}, u32[]{:S(2)}, u32[]{:S(2)}) %collective-permute-start.51) | collective-permute-done | bytes 131104 | tf_op jit(solution)/shard_map/ppermute | solution.py:445
  382.3 2.1 collective-permute-start.52
  385.5 3.0 collective-permute-done.52
  390.2 2.6 collective-permute-done.53
  (277 shorter events, 89.8 us)
Async XLA Ops:
  2.0 13.8 %collective-permute-start.1 = (bf16[352,512]{1,0:T(8,128)(2,1)S(1)}, bf16[352,512]{1,0:T(8,128)(2,1)S(1)}, u32[]{:S(2)}, u32[]{:S(2)}) collective-permute-start(bf16[352,512]{1,0:T(8,128)(2,1)S(1)} %bitcast.344), channel_id=1, source_target_pairs={{0,8},{4,12},{8,16},{12,20},{16,24},{20,28},{24,0},{28,4},{1,9},{5... | collective-permute-start | bytes 1081352 | tf_op jit(solution)/shard_map/ppermute | solution.py:452
  5.1 13.0 %collective-permute-start = (bf16[352,512]{1,0:T(8,128)(2,1)S(1)}, bf16[352,512]{1,0:T(8,128)(2,1)S(1)}, u32[]{:S(2)}, u32[]{:S(2)}) collective-permute-start(bf16[352,512]{1,0:T(8,128)(2,1)S(1)} %bitcast.352), channel_id=1, source_target_pairs={{0,4},{4,0},{8,12},{12,8},{16,20},{20,16},{24,28},{28,24},{1,5},{5... | collective-permute-start | bytes 1081352 | tf_op jit(solution)/shard_map/ppermute | solution.py:445
  9.0 39.3 %collective-permute-start.12 = (bf16[2,256,512]{2,1,0:T(8,128)(2,1)}, bf16[2,256,512]{2,1,0:T(8,128)(2,1)}, u32[]{:S(2)}, u32[]{:S(2)}) collective-permute-start(bf16[2,256,512]{2,1,0:T(8,128)(2,1)} %get-tuple-element.104), channel_id=1, source_target_pairs={{0,1},{1,0},{2,3},{3,2},{4,5},{5,4},{6,7},{7,6},{8,9},{9,8},{10,11... | collective-permute-start | bytes 1572872 | tf_op jit(solution)/shard_map/ppermute | solution.py:445
  9.0 44.6 %collective-permute-start.13 = (bf16[2,256,512]{2,1,0:T(8,128)(2,1)}, bf16[2,256,512]{2,1,0:T(8,128)(2,1)}, u32[]{:S(2)}, u32[]{:S(2)}) collective-permute-start(bf16[2,256,512]{2,1,0:T(8,128)(2,1)} %get-tuple-element.105), channel_id=1, source_target_pairs={{0,2},{1,3},{2,0},{3,1},{4,6},{5,7},{6,4},{7,5},{8,10},{9,11},{10,... | collective-permute-start | bytes 1572872 | tf_op jit(solution)/shard_map/ppermute | solution.py:445
  10.5 80.9 %collective-permute-start.14 = (bf16[2,256,512]{2,1,0:T(8,128)(2,1)}, bf16[2,256,512]{2,1,0:T(8,128)(2,1)}, u32[]{:S(2)}, u32[]{:S(2)}) collective-permute-start(bf16[2,256,512]{2,1,0:T(8,128)(2,1)} %get-tuple-element.106), channel_id=1, source_target_pairs={{0,3},{1,2},{2,1},{3,0},{4,7},{5,6},{6,5},{7,4},{8,11},{9,10},{10,... | collective-permute-start | bytes 1572872 | tf_op jit(solution)/shard_map/ppermute | solution.py:445
  15.8 11.1 %collective-permute-start.2 = (bf16[352,512]{1,0:T(8,128)(2,1)S(1)}, bf16[352,512]{1,0:T(8,128)(2,1)S(1)}, u32[]{:S(2)}, u32[]{:S(2)}) collective-permute-start(bf16[352,512]{1,0:T(8,128)(2,1)S(1)} %bitcast.345), channel_id=1, source_target_pairs={{0,24},{4,28},{8,0},{12,4},{16,8},{20,12},{24,16},{28,20},{1,25},{... | collective-permute-start | bytes 1081352 | tf_op jit(solution)/shard_map/ppermute | solution.py:452
  18.2 18.0 %collective-permute-start.4 = (bf16[352,512]{1,0:T(8,128)(2,1)S(1)}, bf16[352,512]{1,0:T(8,128)(2,1)S(1)}, u32[]{:S(2)}, u32[]{:S(2)}) collective-permute-start(bf16[352,512]{1,0:T(8,128)(2,1)S(1)} %select_select_fusion.4), channel_id=1, source_target_pairs={{0,8},{4,12},{8,16},{12,20},{16,24},{20,28},{24,0},{28,4},{1,9},{5... | collective-permute-start | bytes 1081352 | tf_op jit(solution)/shard_map/ppermute | solution.py:452
  37.3 10.0 %collective-permute-start.3 = (bf16[352,512]{1,0:T(8,128)(2,1)}, bf16[352,512]{1,0:T(8,128)(2,1)S(1)}, u32[]{:S(2)}, u32[]{:S(2)}) collective-permute-start(bf16[352,512]{1,0:T(8,128)(2,1)} %get-tuple-element.178), channel_id=1, source_target_pairs={{0,4},{4,0},{8,12},{12,8},{16,20},{20,16},{24,28},{28,24},{1,5},{5... | collective-permute-start | bytes 1081352 | tf_op jit(solution)/shard_map/ppermute | solution.py:445
  37.8 10.4 %collective-permute-start.7 = (bf16[352,512]{1,0:T(8,128)(2,1)}, bf16[352,512]{1,0:T(8,128)(2,1)S(1)}, u32[]{:S(2)}, u32[]{:S(2)}) collective-permute-start(bf16[352,512]{1,0:T(8,128)(2,1)} %get-tuple-element.175), channel_id=1, source_target_pairs={{0,24},{4,28},{8,0},{12,4},{16,8},{20,12},{24,16},{28,20},{1,25},{... | collective-permute-start | bytes 1081352 | tf_op jit(solution)/shard_map/ppermute | solution.py:452
  47.3 8.9 %collective-permute-start.5 = (bf16[352,512]{1,0:T(8,128)(2,1)S(1)}, bf16[352,512]{1,0:T(8,128)(2,1)S(1)}, u32[]{:S(2)}, u32[]{:S(2)}) collective-permute-start(bf16[352,512]{1,0:T(8,128)(2,1)S(1)} %get-tuple-element.177), channel_id=1, source_target_pairs={{0,4},{4,0},{8,12},{12,8},{16,20},{20,16},{24,28},{28,24},{1,5},{5... | collective-permute-start | bytes 1081352 | tf_op jit(solution)/shard_map/ppermute | solution.py:445
  48.2 13.5 %collective-permute-start.6 = (bf16[352,512]{1,0:T(8,128)(2,1)S(1)}, bf16[352,512]{1,0:T(8,128)(2,1)S(1)}, u32[]{:S(2)}, u32[]{:S(2)}) collective-permute-start(bf16[352,512]{1,0:T(8,128)(2,1)S(1)} %get-tuple-element.176), channel_id=1, source_target_pairs={{0,8},{4,12},{8,16},{12,20},{16,24},{20,28},{24,0},{28,4},{1,9},{5... | collective-permute-start | bytes 1081352 | tf_op jit(solution)/shard_map/ppermute | solution.py:452
  48.3 16.6 %collective-permute-start.8 = (bf16[352,512]{1,0:T(8,128)(2,1)S(1)}, bf16[352,512]{1,0:T(8,128)(2,1)S(1)}, u32[]{:S(2)}, u32[]{:S(2)}) collective-permute-start(bf16[352,512]{1,0:T(8,128)(2,1)S(1)} %select_select_fusion.2), channel_id=1, source_target_pairs={{0,24},{4,28},{8,0},{12,4},{16,8},{20,12},{24,16},{28,20},{1,25},{... | collective-permute-start | bytes 1081352 | tf_op jit(solution)/shard_map/ppermute | solution.py:452
  89.6 9.2 %collective-permute-start.10 = (bf16[256,512]{1,0:T(8,128)(2,1)S(1)}, bf16[256,512]{1,0:T(8,128)(2,1)S(1)}, u32[]{:S(2)}, u32[]{:S(2)}) collective-permute-start(bf16[256,512]{1,0:T(8,128)(2,1)S(1)} %get-tuple-element.135), channel_id=1, source_target_pairs={{0,2},{1,3},{2,0},{3,1},{4,6},{5,7},{6,4},{7,5},{8,10},{9,11},{10,... | collective-permute-start | bytes 786440 | tf_op jit(solution)/shard_map/ppermute | solution.py:445
  90.9 12.6 %collective-permute-start.11 = (bf16[256,512]{1,0:T(8,128)(2,1)S(1)}, bf16[256,512]{1,0:T(8,128)(2,1)S(1)}, u32[]{:S(2)}, u32[]{:S(2)}) collective-permute-start(bf16[256,512]{1,0:T(8,128)(2,1)S(1)} %get-tuple-element.134), channel_id=1, source_target_pairs={{0,3},{1,2},{2,1},{3,0},{4,7},{5,6},{6,5},{7,4},{8,11},{9,10},{10,... | collective-permute-start | bytes 786440 | tf_op jit(solution)/shard_map/ppermute | solution.py:445
  162.5 135.2 %collective-permute-start.61 = (bf16[2,2,2,128,512]{4,3,2,1,0:T(8,128)(2,1)}, bf16[2,2,2,128,512]{4,3,2,1,0:T(8,128)(2,1)}, u32[]{:S(2)}, u32[]{:S(2)}) collective-permute-start(bf16[2,2,2,128,512]{4,3,2,1,0:T(8,128)(2,1)} %bitcast.395), channel_id=1, source_target_pairs={{0,1},{1,0},{2,3},{3,2},{4,5},{5,4},{6,7},{7,6},{8,9},{9,8},{10,11... | collective-permute-start | bytes 3145736 | tf_op jit(solution)/shard_map/ppermute | solution.py:445
  173.1 11.6 %collective-permute-start.18 = (bf16[256,512]{1,0:T(8,128)(2,1)S(1)}, bf16[256,512]{1,0:T(8,128)(2,1)S(1)}, u32[]{:S(2)}, u32[]{:S(2)}) collective-permute-start(bf16[256,512]{1,0:T(8,128)(2,1)S(1)} %get-tuple-element.128), channel_id=1, source_target_pairs={{0,1},{1,0},{2,3},{3,2},{4,5},{5,4},{6,7},{7,6},{8,9},{9,8},{10,11... | collective-permute-start | bytes 786440 | tf_op jit(solution)/shard_map/ppermute | solution.py:445
  173.4 12.5 %collective-permute-start.19 = (bf16[256,512]{1,0:T(8,128)(2,1)S(1)}, bf16[256,512]{1,0:T(8,128)(2,1)S(1)}, u32[]{:S(2)}, u32[]{:S(2)}) collective-permute-start(bf16[256,512]{1,0:T(8,128)(2,1)S(1)} %get-tuple-element.127), channel_id=1, source_target_pairs={{0,2},{1,3},{2,0},{3,1},{4,6},{5,7},{6,4},{7,5},{8,10},{9,11},{10,... | collective-permute-start | bytes 786440 | tf_op jit(solution)/shard_map/ppermute | solution.py:445
  174.6 12.2 %collective-permute-start.20 = (bf16[256,512]{1,0:T(8,128)(2,1)S(1)}, bf16[256,512]{1,0:T(8,128)(2,1)S(1)}, u32[]{:S(2)}, u32[]{:S(2)}) collective-permute-start(bf16[256,512]{1,0:T(8,128)(2,1)S(1)} %get-tuple-element.126), channel_id=1, source_target_pairs={{0,3},{1,2},{2,1},{3,0},{4,7},{5,6},{6,5},{7,4},{8,11},{9,10},{10,... | collective-permute-start | bytes 786440 | tf_op jit(solution)/shard_map/ppermute | solution.py:445
  175.1 58.3 %collective-permute-start.15 = (bf16[256,512]{1,0:T(8,128)(2,1)S(1)}, bf16[256,512]{1,0:T(8,128)(2,1)S(1)}, u32[]{:S(2)}, u32[]{:S(2)}) collective-permute-start(bf16[256,512]{1,0:T(8,128)(2,1)S(1)} %get-tuple-element.132), channel_id=1, source_target_pairs={{0,1},{1,0},{2,3},{3,2},{4,5},{5,4},{6,7},{7,6},{8,9},{9,8},{10,11... | collective-permute-start | bytes 786440 | tf_op jit(solution)/shard_map/ppermute | solution.py:445
  184.6 48.9 %collective-permute-start.16 = (bf16[256,512]{1,0:T(8,128)(2,1)S(1)}, bf16[256,512]{1,0:T(8,128)(2,1)S(1)}, u32[]{:S(2)}, u32[]{:S(2)}) collective-permute-start(bf16[256,512]{1,0:T(8,128)(2,1)S(1)} %get-tuple-element.131), channel_id=1, source_target_pairs={{0,2},{1,3},{2,0},{3,1},{4,6},{5,7},{6,4},{7,5},{8,10},{9,11},{10,... | collective-permute-start | bytes 786440 | tf_op jit(solution)/shard_map/ppermute | solution.py:445
  185.9 47.8 %collective-permute-start.17 = (bf16[256,512]{1,0:T(8,128)(2,1)S(1)}, bf16[256,512]{1,0:T(8,128)(2,1)S(1)}, u32[]{:S(2)}, u32[]{:S(2)}) collective-permute-start(bf16[256,512]{1,0:T(8,128)(2,1)S(1)} %get-tuple-element.130), channel_id=1, source_target_pairs={{0,3},{1,2},{2,1},{3,0},{4,7},{5,6},{6,5},{7,4},{8,11},{9,10},{10,... | collective-permute-start | bytes 786440 | tf_op jit(solution)/shard_map/ppermute | solution.py:445
  217.2 8.5 %collective-permute-start.30 = (f32[10240]{0:T(1024)S(1)}, f32[10240]{0:T(1024)S(1)}, u32[]{:S(2)}, u32[]{:S(2)}) collective-permute-start(f32[10240]{0:T(1024)S(1)} %pad_maximum_fusion.13), channel_id=1, source_target_pairs={{0,1},{1,0},{2,3},{3,2},{4,5},{5,4},{6,7},{7,6},{8,9},{9,8},{10,11... | collective-permute-start | bytes 122888 | tf_op jit(solution)/shard_map/ppermute | solution.py:445
  229.7 35.5 %collective-permute-start.21 = (bf16[352,512]{1,0:T(8,128)(2,1)}, bf16[352,512]{1,0:T(8,128)(2,1)}, u32[]{:S(2)}, u32[]{:S(2)}) collective-permute-start(bf16[352,512]{1,0:T(8,128)(2,1)} %get-tuple-element.70), channel_id=1, source_target_pairs={{0,24},{4,28},{8,0},{12,4},{16,8},{20,12},{24,16},{28,20},{1,25},{... | collective-permute-start | bytes 1081352 | tf_op jit(solution)/shard_map/ppermute | solution.py:452
  233.5 37.4 %collective-permute-start.42 = (bf16[2,2,2,64,512]{4,3,2,1,0:T(8,128)(2,1)}, bf16[2,2,2,64,512]{4,3,2,1,0:T(8,128)(2,1)}, u32[]{:S(2)}, u32[]{:S(2)}) collective-permute-start(bf16[2,2,2,64,512]{4,3,2,1,0:T(8,128)(2,1)} %bitcast.398), channel_id=1, source_target_pairs={{0,1},{1,0},{2,3},{3,2},{4,5},{5,4},{6,7},{7,6},{8,9},{9,8},{10,11... | collective-permute-start | bytes 1572872 | tf_op jit(solution)/shard_map/ppermute | solution.py:445
  233.5 30.4 %collective-permute-start.22 = (bf16[352,512]{1,0:T(8,128)(2,1)}, bf16[352,512]{1,0:T(8,128)(2,1)S(1)}, u32[]{:S(2)}, u32[]{:S(2)}) collective-permute-start(bf16[352,512]{1,0:T(8,128)(2,1)} %get-tuple-element.144), channel_id=1, source_target_pairs={{0,8},{4,12},{8,16},{12,20},{16,24},{20,28},{24,0},{28,4},{1,9},{5... | collective-permute-start | bytes 1081352 | tf_op jit(solution)/shard_map/ppermute | solution.py:452
  238.6 10.5 %collective-permute-start.33 = (f32[10240]{0:T(1024)S(1)}, f32[10240]{0:T(1024)S(1)}, u32[]{:S(2)}, u32[]{:S(2)}) collective-permute-start(f32[10240]{0:T(1024)S(1)} %add.325), channel_id=1, source_target_pairs={{0,8},{4,12},{8,0},{12,4},{16,24},{20,28},{24,16},{28,20},{1,9},{5... | collective-permute-start | bytes 122888 | tf_op jit(solution)/shard_map/ppermute | solution.py:445
  255.4 9.5 %collective-permute-start.23 = (bf16[352,512]{1,0:T(8,128)(2,1)S(1)}, bf16[352,512]{1,0:T(8,128)(2,1)S(1)}, u32[]{:S(2)}, u32[]{:S(2)}) collective-permute-start(bf16[352,512]{1,0:T(8,128)(2,1)S(1)} %copy-done.25), channel_id=1, source_target_pairs={{0,4},{4,0},{8,12},{12,8},{16,20},{20,16},{24,28},{28,24},{1,5},{5... | collective-permute-start | bytes 1081352 | tf_op jit(solution)/shard_map/ppermute | solution.py:445
  263.9 9.3 %collective-permute-start.35 = (bf16[2,2,2,2,32,512]{5,4,3,2,1,0:T(8,128)(2,1)S(1)}, bf16[2,2,2,2,32,512]{5,4,3,2,1,0:T(8,128)(2,1)S(1)}, u32[]{:S(2)}, u32[]{:S(2)}) collective-permute-start(bf16[2,2,2,2,32,512]{5,4,3,2,1,0:T(8,128)(2,1)S(1)} %bitcast.397), channel_id=1, source_target_pairs={{0,1},{1,0},{2,3},{3,2},{4,5},{5,4},{6,7},{7,6},{8,9},{9,8},{10,11... | collective-permute-start | bytes 1572872 | tf_op jit(solution)/shard_map/ppermute | solution.py:445
  267.0 13.2 %collective-permute-start.25 = (bf16[352,512]{1,0:T(8,128)(2,1)S(1)}, bf16[352,512]{1,0:T(8,128)(2,1)S(1)}, u32[]{:S(2)}, u32[]{:S(2)}) collective-permute-start(bf16[352,512]{1,0:T(8,128)(2,1)S(1)} %broadcast_select_fusion.3), channel_id=1, source_target_pairs={{0,8},{4,12},{8,16},{12,20},{16,24},{20,28},{24,0},{28,4},{1,9},{5... | collective-permute-start | bytes 1081352 | tf_op jit(solution)/shard_map/ppermute | solution.py:452
  267.0 18.0 %collective-permute-start.24 = (bf16[352,512]{1,0:T(8,128)(2,1)S(1)}, bf16[352,512]{1,0:T(8,128)(2,1)S(1)}, u32[]{:S(2)}, u32[]{:S(2)}) collective-permute-start(bf16[352,512]{1,0:T(8,128)(2,1)S(1)} %get-tuple-element.101), channel_id=1, source_target_pairs={{0,24},{4,28},{8,0},{12,4},{16,8},{20,12},{24,16},{28,20},{1,25},{... | collective-permute-start | bytes 1081352 | tf_op jit(solution)/shard_map/ppermute | solution.py:452
  270.9 14.9 %collective-permute-start.27 = (bf16[352,512]{1,0:T(8,128)(2,1)S(1)}, bf16[352,512]{1,0:T(8,128)(2,1)S(1)}, u32[]{:S(2)}, u32[]{:S(2)}) collective-permute-start(bf16[352,512]{1,0:T(8,128)(2,1)S(1)} %get-tuple-element.98), channel_id=1, source_target_pairs={{0,4},{4,0},{8,12},{12,8},{16,20},{20,16},{24,28},{28,24},{1,5},{5... | collective-permute-start | bytes 1081352 | tf_op jit(solution)/shard_map/ppermute | solution.py:445
  273.2 27.5 %collective-permute-start.55 = (bf16[2,2,2,2,64,512]{5,4,3,2,1,0:T(8,128)(2,1)S(1)}, bf16[2,2,2,2,64,512]{5,4,3,2,1,0:T(8,128)(2,1)S(1)}, u32[]{:S(2)}, u32[]{:S(2)}) collective-permute-start(bf16[2,2,2,2,64,512]{5,4,3,2,1,0:T(8,128)(2,1)S(1)} %bitcast.394), channel_id=1, source_target_pairs={{0,1},{1,0},{2,3},{3,2},{4,5},{5,4},{6,7},{7,6},{8,9},{9,8},{10,11... | collective-permute-start | bytes 3145736 | tf_op jit(solution)/shard_map/ppermute | solution.py:445
  280.2 30.0 %collective-permute-start.48 = (bf16[2,2,2,2,64,512]{5,4,3,2,1,0:T(8,128)(2,1)S(1)}, bf16[2,2,2,2,64,512]{5,4,3,2,1,0:T(8,128)(2,1)S(1)}, u32[]{:S(2)}, u32[]{:S(2)}) collective-permute-start(bf16[2,2,2,2,64,512]{5,4,3,2,1,0:T(8,128)(2,1)S(1)} %bitcast.396), channel_id=1, source_target_pairs={{0,1},{1,0},{2,3},{3,2},{4,5},{5,4},{6,7},{7,6},{8,9},{9,8},{10,11... | collective-permute-start | bytes 3145736 | tf_op jit(solution)/shard_map/ppermute | solution.py:445
  285.7 9.7 %collective-permute-start.36 = (bf16[2,2,2,32,512]{4,3,2,1,0:T(8,128)(2,1)S(1)}, bf16[2,2,2,32,512]{4,3,2,1,0:T(8,128)(2,1)S(1)}, u32[]{:S(2)}, u32[]{:S(2)}) collective-permute-start(bf16[2,2,2,32,512]{4,3,2,1,0:T(8,128)(2,1)S(1)} %get-tuple-element.164), channel_id=1, source_target_pairs={{0,2},{1,3},{2,0},{3,1},{4,6},{5,7},{6,4},{7,5},{8,10},{9,11},{10,... | collective-permute-start | bytes 786440 | tf_op jit(solution)/shard_map/ppermute | solution.py:445
  292.3 54.4 %collective-permute-start.29 = (bf16[352,512]{1,0:T(8,128)(2,1)S(1)}, bf16[352,512]{1,0:T(8,128)(2,1)S(1)}, u32[]{:S(2)}, u32[]{:S(2)}) collective-permute-start(bf16[352,512]{1,0:T(8,128)(2,1)S(1)} %get-tuple-element.140), channel_id=1, source_target_pairs={{0,8},{4,12},{8,16},{12,20},{16,24},{20,28},{24,0},{28,4},{1,9},{5... | collective-permute-start | bytes 1081352 | tf_op jit(solution)/shard_map/ppermute | solution.py:452
  295.5 53.6 %collective-permute-start.28 = (bf16[352,512]{1,0:T(8,128)(2,1)S(1)}, bf16[352,512]{1,0:T(8,128)(2,1)S(1)}, u32[]{:S(2)}, u32[]{:S(2)}) collective-permute-start(bf16[352,512]{1,0:T(8,128)(2,1)S(1)} %get-tuple-element.141), channel_id=1, source_target_pairs={{0,24},{4,28},{8,0},{12,4},{16,8},{20,12},{24,16},{28,20},{1,25},{... | collective-permute-start | bytes 1081352 | tf_op jit(solution)/shard_map/ppermute | solution.py:452
  297.8 52.3 %collective-permute-start.26 = (bf16[352,512]{1,0:T(8,128)(2,1)S(1)}, bf16[352,512]{1,0:T(8,128)(2,1)S(1)}, u32[]{:S(2)}, u32[]{:S(2)}) collective-permute-start(bf16[352,512]{1,0:T(8,128)(2,1)S(1)} %get-tuple-element.142), channel_id=1, source_target_pairs={{0,4},{4,0},{8,12},{12,8},{16,20},{20,16},{24,28},{28,24},{1,5},{5... | collective-permute-start | bytes 1081352 | tf_op jit(solution)/shard_map/ppermute | solution.py:445
  300.7 9.4 %collective-permute-start.37 = (bf16[2,2,32,512]{3,2,1,0:T(8,128)(2,1)S(1)}, bf16[2,2,32,512]{3,2,1,0:T(8,128)(2,1)S(1)}, u32[]{:S(2)}, u32[]{:S(2)}) collective-permute-start(bf16[2,2,32,512]{3,2,1,0:T(8,128)(2,1)S(1)} %get-tuple-element.162), channel_id=1, source_target_pairs={{0,4},{4,0},{8,12},{12,8},{16,20},{20,16},{24,28},{28,24},{1,5},{5... | collective-permute-start | bytes 393224 | tf_op jit(solution)/shard_map/ppermute | solution.py:445
  316.9 39.8 %collective-permute-start.62 = (bf16[2,2,128,512]{3,2,1,0:T(8,128)(2,1)S(1)}, bf16[2,2,128,512]{3,2,1,0:T(8,128)(2,1)S(1)}, u32[]{:S(2)}, u32[]{:S(2)}) collective-permute-start(bf16[2,2,128,512]{3,2,1,0:T(8,128)(2,1)S(1)} %get-tuple-element.110), channel_id=1, source_target_pairs={{0,8},{4,12},{8,0},{12,4},{16,24},{20,28},{24,16},{28,20},{1,9},{5... | collective-permute-start | bytes 1572872 | tf_op jit(solution)/shard_map/ppermute | solution.py:445
  317.0 14.0 %collective-permute-start.39 = (bf16[32,512]{1,0:T(8,128)(2,1)S(1)}, bf16[32,512]{1,0:T(8,128)(2,1)S(1)}, u32[]{:S(2)}, u32[]{:S(2)}) collective-permute-start(bf16[32,512]{1,0:T(8,128)(2,1)S(1)} %fusion.77), channel_id=1, source_target_pairs={{0,24},{4,28},{8,16},{12,20},{16,8},{20,12},{24,0},{28,4},{1,25},{... | collective-permute-start | bytes 98312 | tf_op jit(solution)/shard_map/ppermute | solution.py:445
  346.0 13.4 %collective-permute-start.56 = (bf16[2,2,2,64,512]{4,3,2,1,0:T(8,128)(2,1)S(1)}, bf16[2,2,2,64,512]{4,3,2,1,0:T(8,128)(2,1)S(1)}, u32[]{:S(2)}, u32[]{:S(2)}) collective-permute-start(bf16[2,2,2,64,512]{4,3,2,1,0:T(8,128)(2,1)S(1)} %get-tuple-element.116), channel_id=1, source_target_pairs={{0,4},{4,0},{8,12},{12,8},{16,20},{20,16},{24,28},{28,24},{1,5},{5... | collective-permute-start | bytes 1572872 | tf_op jit(solution)/shard_map/ppermute | solution.py:445
  346.8 12.8 %collective-permute-start.49 = (bf16[2,2,2,64,512]{4,3,2,1,0:T(8,128)(2,1)S(1)}, bf16[2,2,2,64,512]{4,3,2,1,0:T(8,128)(2,1)S(1)}, u32[]{:S(2)}, u32[]{:S(2)}) collective-permute-start(bf16[2,2,2,64,512]{4,3,2,1,0:T(8,128)(2,1)S(1)} %get-tuple-element.122), channel_id=1, source_target_pairs={{0,2},{1,3},{2,0},{3,1},{4,6},{5,7},{6,4},{7,5},{8,10},{9,11},{10,... | collective-permute-start | bytes 1572872 | tf_op jit(solution)/shard_map/ppermute | solution.py:445
  356.9 11.0 %collective-permute-start.63 = (bf16[2,128,512]{2,1,0:T(8,128)(2,1)S(1)}, bf16[2,128,512]{2,1,0:T(8,128)(2,1)S(1)}, u32[]{:S(2)}, u32[]{:S(2)}) collective-permute-start(bf16[2,128,512]{2,1,0:T(8,128)(2,1)S(1)} %get-tuple-element.108), channel_id=1, source_target_pairs={{0,24},{4,28},{8,16},{12,20},{16,8},{20,12},{24,0},{28,4},{1,25},{... | collective-permute-start | bytes 786440 | tf_op jit(solution)/shard_map/ppermute | solution.py:445
  359.5 13.1 %collective-permute-start.57 = (bf16[2,2,64,512]{3,2,1,0:T(8,128)(2,1)S(1)}, bf16[2,2,64,512]{3,2,1,0:T(8,128)(2,1)S(1)}, u32[]{:S(2)}, u32[]{:S(2)}) collective-permute-start(bf16[2,2,64,512]{3,2,1,0:T(8,128)(2,1)S(1)} %get-tuple-element.114), channel_id=1, source_target_pairs={{0,8},{4,12},{8,0},{12,4},{16,24},{20,28},{24,16},{28,20},{1,9},{5... | collective-permute-start | bytes 786440 | tf_op jit(solution)/shard_map/ppermute | solution.py:445
  359.7 15.0 %collective-permute-start.50 = (bf16[2,2,64,512]{3,2,1,0:T(8,128)(2,1)S(1)}, bf16[2,2,64,512]{3,2,1,0:T(8,128)(2,1)S(1)}, u32[]{:S(2)}, u32[]{:S(2)}) collective-permute-start(bf16[2,2,64,512]{3,2,1,0:T(8,128)(2,1)S(1)} %get-tuple-element.120), channel_id=1, source_target_pairs={{0,4},{4,0},{8,12},{12,8},{16,20},{20,16},{24,28},{28,24},{1,5},{5... | collective-permute-start | bytes 786440 | tf_op jit(solution)/shard_map/ppermute | solution.py:445
  372.6 11.8 %collective-permute-start.58 = (bf16[2,64,512]{2,1,0:T(8,128)(2,1)S(1)}, bf16[2,64,512]{2,1,0:T(8,128)(2,1)S(1)}, u32[]{:S(2)}, u32[]{:S(2)}) collective-permute-start(bf16[2,64,512]{2,1,0:T(8,128)(2,1)S(1)} %fusion.57), channel_id=1, source_target_pairs={{0,24},{4,28},{8,16},{12,20},{16,8},{20,12},{24,0},{28,4},{1,25},{... | collective-permute-start | bytes 393224 | tf_op jit(solution)/shard_map/ppermute | solution.py:445
  374.7 7.6 %collective-permute-start.51 = (bf16[2,64,512]{2,1,0:T(8,128)(2,1)S(1)}, bf16[2,64,512]{2,1,0:T(8,128)(2,1)S(1)}, u32[]{:S(2)}, u32[]{:S(2)}) collective-permute-start(bf16[2,64,512]{2,1,0:T(8,128)(2,1)S(1)} %get-tuple-element.154), channel_id=1, source_target_pairs={{0,8},{4,12},{8,0},{12,4},{16,24},{20,28},{24,16},{28,20},{1,9},{5... | collective-permute-start | bytes 393224 | tf_op jit(solution)/shard_map/ppermute | solution.py:445
  374.9 14.6 %collective-permute-start.65 = (bf16[128,512]{1,0:T(8,128)(2,1)S(1)}, bf16[128,512]{1,0:T(8,128)(2,1)S(1)}, u32[]{:S(2)}, u32[]{:S(2)}) collective-permute-start(bf16[128,512]{1,0:T(8,128)(2,1)S(1)} %fusion.46), channel_id=1, source_target_pairs={{0,2},{1,3},{2,0},{3,1},{4,6},{5,7},{6,4},{7,5},{8,10},{9,11},{10,... | collective-permute-start | bytes 393224 | tf_op jit(solution)/shard_map/ppermute | solution.py:445
  (52 other events, 490.2 us)

commit v3 on v2

--- a/solution.py
+++ b/solution.py
@@ -15,7 +15,6 @@
 QUAD = 4 * HEAD_DIM
 BF = jnp.bfloat16
 F32 = jnp.float32
-VMEM_LIMIT = 56 << 20
 
 
 def mm(a, b, ca=1, cb=0):
@@ -130,7 +129,7 @@
 def forward_one(
     me_ref, x_ref, y1, y2, y3, p1, p2, p3, m1, m2, m3,
     allow_ref, gain_ref, shift_ref, w_ref, b_ref,
-    o_ref, c_ref, q_ref, k_ref, v_ref, p_ref, o_scr,
+    o0, o1, o2, o3, on_ref, c_ref, q_ref, k_ref, v_ref, p_ref, o_scr,
 ):
     me = me_ref[0]
     got = (None, y1, y2, y3, p1, p2, p3, m1, m2, m3)
@@ -168,34 +167,36 @@
         return carry
 
     lax.fori_loop(0, 8, body, 0)
-    for d in range(4):
-        o_ref[d] = swap(matrix, o_scr[:, d ^ me].reshape(256, 512))
+    for d, ref in enumerate((o0, o1, o2, o3)):
+        value = swap(matrix, o_scr[:, d ^ me].reshape(256, 512))
+        ref[...] = value
+        on_ref[d ^ me] = value
 
 
 def middle(
-    o1_ref, x_ref, cot_ref,
+    me_ref, o0, o1, o2_, o3, x0, x1, x2, x3, c0, c1, c2, c3,
     wm1_ref, off1_ref, g2_ref, s2_ref, wf_ref, bf_ref, wm2_ref, off2_ref,
     g3_ref, s3_ref, we_ref, be_ref, wr_ref, br_ref,
-    out_ref, gb1_ref, a2_ref, dqkv_ref, o2_ref, gb2_ref, a3_ref, gu_ref, hid_ref, gb3_ref,
-    vec_ref, bias_ref,
+    out0, out2, out13, gb10, gb11, gb12, gb13,
+    a2_ref, dqkv_ref, o2_ref, gb2_ref, a3_ref, gu_ref, hid_ref, gb3_ref, vec_ref, bias_ref,
 ):
     samples = 4
 
-    def gather(ref):
+    def gather(*refs):
         return jnp.concatenate(
-            [ref[d, s * 16 : (s + 1) * 16] for s in range(samples) for d in range(4)], axis=0
+            [ref[s * 16 : (s + 1) * 16] for s in range(samples) for ref in refs], axis=0
         )
 
-    def scatter(ref, values):
+    def scatter(values, *refs):
         for s in range(samples):
-            for d in range(4):
+            for d, ref in enumerate(refs):
                 at = (s * 4 + d) * 16
-                ref[d, s * 16 : (s + 1) * 16] = values[at : at + 16]
+                ref[s * 16 : (s + 1) * 16] = values[at : at + 16]
 
     masks, masks32 = head_masks(BF), head_masks(F32)
-    o1, cot = gather(o1_ref), gather(cot_ref)
+    attended, cot = gather(o0, o1, o2_, o3), gather(c0, c1, c2, c3)
     gb3_ref[...] = cot
-    r1 = gather(x_ref).astype(F32) + mm(o1, wm1_ref[...]) + off1_ref[...]
+    r1 = gather(x0, x1, x2, x3).astype(F32) + mm(attended, wm1_ref[...]) + off1_ref[...]
     unit2, inv2 = norm_parts(r1)
     act2 = (unit2 * g2_ref[...] + s2_ref[...]).astype(BF)
     a2_ref[...] = act2
@@ -229,7 +230,7 @@
         bias.append(col_sum(gu))
         term = mm(gu, we_ref[:, cols], 1, 1)
         back = term if back is None else back + term
-    scatter(out_ref, out.astype(BF))
+    scatter(out.astype(BF), out0, out13.at[0], out2, out13.at[1])
     vecs = [col_sum(back * unit3), col_sum(back)]
     gr2 = cot.astype(F32) + norm_back(back, unit3, inv3, g3_ref[...])
     gb2 = gr2.astype(BF)
@@ -249,7 +250,7 @@
     back = mm(dqkv, wf_ref[...], 1, 1)
     vecs += [col_sum(back * unit2), col_sum(back)]
     gr1 = gr2 + norm_back(back, unit2, inv2, g2_ref[...])
-    scatter(gb1_ref, gr1.astype(BF))
+    scatter(gr1.astype(BF), gb10, gb11, gb12, gb13)
     vecs += [col_sum(gb2), col_sum(cot), col_sum(dqkv[:, :512]), col_sum(dqkv[:, 1024:])]
 
     @pl.when(pl.program_id(0) == 0)
@@ -261,36 +262,56 @@
     bias_ref[...] += jnp.concatenate(bias, axis=1)
 
 
-def backward_one(
-    me_ref, gb1_ref, c_ref, q_ref, k_ref, v_ref, p_ref, gain_ref, shift_ref, w_ref, wm_ref,
-    ta_ref, tb_ref, tc_ref, cact_ref, dkv_ref, dq_ref, vec_ref,
-    go_scr, dkv_scr, t_scr,
-):
-    me = me_ref[0]
-    gain, shift = gain_ref[...], shift_ref[...]
-    matrix = swap_matrix(256)
+def attend_half(q_ref, k_ref, v_ref, p_ref, go_ref, half, dq_ref, dkv_ref):
     masks, masks32 = head_masks(BF), head_masks(F32)
-    for d in range(4):
-        go = mm(gb1_ref[d ^ me], wm_ref[...], 1, 1).astype(BF)
-        go_scr[:, d] = swap(matrix, go).reshape(16, 16, 512)
 
     def body(i, carry):
         for j in range(2):
             f = i * 2 + j
-            q, k, v, go = (r[f].reshape(64, 512) for r in (q_ref, k_ref, v_ref, go_scr))
+            q, k, v, go = (
+                r.reshape(64, 512)
+                for r in (q_ref[f], k_ref[f], v_ref[f], go_ref[half * 8 + f])
+            )
             dq, dk, dv = attend_back(q, k, v, p_ref[f], go, masks, masks32)
             dq_ref[f] = dq.reshape(4, 16, 512)
-            dkv_scr[f] = jnp.concatenate([dk, dv], axis=1).reshape(4, 16, 1024)
+            dkv_ref[f] = jnp.concatenate([dk, dv], axis=1).reshape(4, 16, 1024)
         return carry
 
-    lax.fori_loop(0, 8, body, 0)
+    lax.fori_loop(0, 4, body, 0)
+
+
+def backward_first(
+    me_ref, g0, g1, g2, g3, q_ref, k_ref, v_ref, p_ref, wm_ref,
+    gb1_ref, go_ref, dq_ref, dkv_ref,
+):
+    me = me_ref[0]
+    matrix = swap_matrix(256)
+    for d, ref in enumerate((g0, g1, g2, g3)):
+        value = ref[...]
+        gb1_ref[d ^ me] = value
+        go = mm(value, wm_ref[...], 1, 1).astype(BF)
+        go_ref[:, d ^ me] = swap(matrix, go).reshape(16, 16, 512)
+    attend_half(q_ref, k_ref, v_ref, p_ref, go_ref, 0, dq_ref, dkv_ref)
+
+
+def backward_second(
+    me_ref, go_ref, q_ref, k_ref, v_ref, p_ref, dkva_ref, c_ref, gain_ref, shift_ref, w_ref,
+    ta_ref, tb_ref, tc_ref, cact_ref, dkv_ref, dq_ref, vec_ref,
+    dkv_scr, t_scr,
+):
+    attend_half(q_ref, k_ref, v_ref, p_ref, go_ref, 1, dq_ref, dkv_scr)
+    gain, shift = gain_ref[...], shift_ref[...]
+    matrix = swap_matrix(256)
     gain_sum = jnp.zeros((1, 512), F32)
     shift_sum, v_sum = gain_sum, gain_sum
     for d in range(4):
         rows = slice(d * 256, (d + 1) * 256)
         unit, inverse = norm_parts(c_ref[rows].astype(F32))
         cact_ref[rows] = (unit * gain + shift).astype(BF)
-        dkv = swap(matrix, dkv_scr[:, d].reshape(256, 1024))
+        heads = jnp.concatenate(
+            [r[:, d].reshape(128, 1024) for r in (dkva_ref, dkv_scr)], axis=0
+        )
+        dkv = swap(matrix, heads)
         dkv_ref[rows] = dkv
         back = mm(dkv, w_ref[:, 512:], 1, 1)
         t_scr[rows] = back.astype(BF)
@@ -304,10 +325,9 @@
 
 
 def backward_query(
-    me_ref, gb1_ref, x_ref, dq_ref, vecc_ref, gain_ref, shift_ref, w_ref,
+    me_ref, gb1_ref, x_ref, dqa_ref, dqb_ref, vecc_ref, gain_ref, shift_ref, w_ref,
     base_ref, act_ref, dqn_ref, vec_ref,
 ):
-    me = me_ref[0]
     gain, shift = gain_ref[...], shift_ref[...]
     matrix = swap_matrix(256)
     gain_sum, shift_sum, v_sum = vecc_ref[0:1], vecc_ref[1:2], vecc_ref[2:3]
@@ -317,10 +337,11 @@
         rows = slice(d * 256, (d + 1) * 256)
         unit, inverse = norm_parts(x_ref[rows].astype(F32))
         act_ref[rows] = (unit * gain + shift).astype(BF)
-        dq = swap(matrix, dq_ref[:, d].reshape(256, 512))
+        heads = jnp.concatenate([r[:, d].reshape(128, 512) for r in (dqa_ref, dqb_ref)], axis=0)
+        dq = swap(matrix, heads)
         dqn_ref[rows] = dq
         back = mm(dq, w_ref[:, :512], 1, 1)
-        gb1 = gb1_ref[d ^ me]
+        gb1 = gb1_ref[d]
         base_ref[rows] = gb1.astype(F32) + norm_back(back, unit, inverse, gain)
         gain_sum += col_sum(back * unit)
         shift_sum += col_sum(back)
@@ -332,20 +353,30 @@
     )
 
 
-def finish(me_ref, base_ref, a_ref, b_ref, c_ref, x_ref, gain_ref, out_ref):
+def finish(
+    me_ref, base_ref, a_ref, ag_ref, b_ref, bg_ref, c_ref, cg_ref, x_ref, gain_ref, out_ref
+):
     owner = me_ref[1] == 1
 
     @pl.when(owner)
     def _():
-        for ref, start, rows in ((a_ref, 0, 336), (b_ref, 336, 336), (c_ref, 672, 352)):
+        for ref, got, start, rows in (
+            (a_ref, ag_ref, 0, 336), (b_ref, bg_ref, 336, 336), (c_ref, cg_ref, 672, 352)
+        ):
             at = slice(start, start + rows)
             unit, inverse = norm_parts(x_ref[at].astype(F32))
-            extra = norm_back(ref[:rows], unit, inverse, gain_ref[...])
+            total = ref[:rows].astype(F32) + got[:rows].astype(F32)
+            extra = norm_back(total, unit, inverse, gain_ref[...])
             out_ref[at] = (base_ref[at] + extra).astype(BF)
 
     @pl.when(jnp.logical_not(owner))
     def _():
         out_ref[...] = base_ref[...].astype(BF)
+
+
+def place(me_ref, b0, b1, b2, b3, out_ref):
+    for d, ref in enumerate((b0, b1, b2, b3)):
+        out_ref[d ^ me_ref[0]] = ref[...]
 
 
 def shard_of(me_ref, dy, d1, d3):
@@ -421,23 +452,33 @@
     return jax.ShapeDtypeStruct(shape, dtype)
 
 
-def params():
-    return pltpu.CompilerParams(vmem_limit_bytes=VMEM_LIMIT)
+def params(limit):
+    return pltpu.CompilerParams(vmem_limit_bytes=limit << 20)
 
 
 def row(vector):
     return vector.reshape(1, -1)
 
 
-def whole(kernel, name, outs, scratch, *inputs):
+def whole(kernel, name, limit, outs, scratch, *inputs):
+    arrays, specs = [inputs[0]], [pl.BlockSpec(memory_space=pltpu.SMEM)]
+    for entry in inputs[1:]:
+        array, block, index = entry if isinstance(entry, tuple) else (entry, None, None)
+        arrays.append(array)
+        block = array.shape if block is None else block
+        index = (0,) * array.ndim if index is None else index
+        specs.append(pl.BlockSpec(block, lambda i, index=index: index))
+    single = not isinstance(outs, tuple)
     return pl.pallas_call(
         kernel,
+        grid=(1,),
         out_shape=outs,
-        in_specs=[pl.BlockSpec(memory_space=pltpu.SMEM)] + [pl.BlockSpec()] * (len(inputs) - 1),
+        in_specs=specs,
+        out_specs=jax.tree.map(lambda o: pl.BlockSpec(o.shape, lambda i: (0,) * len(o.shape)), outs),
         scratch_shapes=scratch,
-        compiler_params=params(),
+        compiler_params=params(limit),
         name=name,
-    )(*inputs)
+    )(*arrays)
 
 
 def shuffle(value, axis, mask):
@@ -456,45 +497,76 @@
     return lax.dynamic_index_in_dim(stacked, index, axis, keepdims=False)
 
 
-def swap_blocks(blocks, axis):
-    return [blocks[0]] + [shuffle(blocks[d], axis, d) for d in range(1, len(blocks))]
+def fence(tree):
+    return lax.optimization_barrier(tree)
 
 
 def plus(a, b):
     return (a.astype(F32) + b.astype(F32)).astype(BF)
 
 
-def halve(keep, sent, where):
-    got = shuffle(sent, *where)
-    return plus(keep[0], got[0]), plus(keep[1], got[1])
-
-
-def join_two(mine, index, where):
-    other = shuffle(mine, *where)
-    return jnp.stack([jnp.where(index == 0, mine, other), jnp.where(index == 0, other, mine)])
-
-
-def chain(keep, sent, dims):
-    mine, out = halve(keep, sent, CORE)
-    for i, where in enumerate(dims):
-        if i == len(dims) - 1:
-            return plus(mine, shuffle(out, *where))
-        mine, out = halve(mine, out, where)
+class Chain:
+    def __init__(self, keep, sent, dims):
+        self.keep, self.sent, self.dims = keep, sent, (CORE,) + dims
+
+    def start(self):
+        return shuffle(self.sent, *self.dims[0])
+
+    def take(self, got):
+        self.dims = self.dims[1:]
+        if self.dims:
+            self.keep, self.sent = plus(self.keep[0], got[0]), plus(self.keep[1], got[1])
+        else:
+            self.keep = plus(self.keep, got)
+
+
+def together(chains, make=lambda: ()):
+    got = [chain.start() for chain in chains]
+    got, other = fence((got, make()))
+    for chain, value in zip(chains, got):
+        chain.take(value)
+    return other
+
+
+def last_round(parts):
+    joined = jnp.concatenate([part.reshape(-1, 512) for part in parts], axis=0)
+    return joined, [shuffle(joined, "feat", mask) for mask in (1, 2, 3)]
+
+
+def pick_sum(rows, core):
+    own, sibling, partner, other = (r.astype(F32) for r in rows)
+    mine, theirs = own + partner, sibling + other
+    return jnp.stack([jnp.where(core == 0, mine, theirs), jnp.where(core == 0, theirs, mine)])
+
+
+def pick_join(rows, core, xx):
+    place = core * 2 + xx
+    outs = []
+    for target in range(4):
+        value = rows[0]
+        for mask, index in ((1, 2), (2, 1), (3, 3)):
+            value = jnp.where((place ^ target) == index, rows[mask], value)
+        outs.append(value.astype(F32))
+    return jnp.stack(outs)
 
 
 def send_context(x, position):
     dy, dz = position // 4, position % 4
     owner = position == 0
     a, b, c = (x[start : start + THIRD] for start in THIRDS)
-    y1, p1, m1 = shuffle(a, *Y), turn(b, 1), turn(c, -1)
     pick = jnp.where
-    y2 = shuffle(pick(owner, b, pick(dz == 1, p1, m1)), *Y)
-    p2 = turn(pick(owner, c, pick(dy == 1, y1, p1)), 1)
-    m2 = turn(pick(owner, a, pick(dy == 1, y1, m1)), -1)
-    y3 = shuffle(pick(owner, c, p2), *Y)
-    p3 = turn(pick(owner, a, p2), 1)
-    m3 = turn(pick(owner, b, pick((dy == 0) & (dz == 3), m2, y2)), -1)
-    return y1, y2, y3, p1, p2, p3, m1, m2, m3
+    y1, p1, m1 = yield shuffle(a, *Y), turn(b, 1), turn(c, -1)
+    y2, p2, m2 = yield (
+        shuffle(pick(owner, b, pick(dz == 1, p1, m1)), *Y),
+        turn(pick(owner, c, pick(dy == 1, y1, p1)), 1),
+        turn(pick(owner, a, pick(dy == 1, y1, m1)), -1),
+    )
+    y3, p3, m3 = yield (
+        shuffle(pick(owner, c, p2), *Y),
+        turn(pick(owner, a, p2), 1),
+        turn(pick(owner, b, pick((dy == 0) & (dz == 3), m2, y2)), -1),
+    )
+    yield y1, y2, y3, p1, p2, p3, m1, m2, m3
 
 
 def sum_context(a, b, c, position):
@@ -506,33 +578,34 @@
             hit = hit | (position == place)
         return hit
 
-    def add(value, places, got):
-        return pick(to(places), plus(value, got), value)
-
-    y = shuffle(pick(to([6]), b, c), *Y)
-    m = turn(a, -1)
-    p = turn(pick(to([3, 7]), b, pick(to([2]), a, c)), 1)
+    def add(value, *terms):
+        total = value.astype(F32)
+        for places, got in terms:
+            total = total + pick(to(places), got.astype(F32), 0.0)
+        return total.astype(BF)
+
+    y, m, p = yield (
+        shuffle(pick(to([6]), b, c), *Y),
+        turn(a, -1),
+        turn(pick(to([3, 7]), b, pick(to([2]), a, c)), 1),
+    )
     a, b, c = (
-        add(add(a, [0, 5], m), [3], p),
-        add(add(b, [2], y), [0, 4], p),
-        add(add(c, [0, 1], y), [7], p),
-    )
-    y = shuffle(pick(to([7]), c, b), *Y)
-    m = turn(pick(to([1]), c, pick(to([5]), a, b)), -1)
-    p = turn(pick(to([2]), c, a), 1)
+        add(a, ([0, 5], m), ([3], p)),
+        add(b, ([2], y), ([0, 4], p)),
+        add(c, ([0, 1], y), ([7], p)),
+    )
+    y, m, p = yield (
+        shuffle(pick(to([7]), c, b), *Y),
+        turn(pick(to([1]), c, pick(to([5]), a, b)), -1),
+        turn(pick(to([2]), c, a), 1),
+    )
     a, b, c = (
-        add(add(a, [4], m), [0, 4], p),
-        add(add(b, [0, 1], y), [1], m),
-        add(add(add(c, [3], y), [0], m), [3], p),
-    )
-    y, m, p = shuffle(a, *Y), turn(b, -1), turn(c, 1)
-    return tuple(u.astype(F32) + v.astype(F32) for u, v in ((a, y), (b, m), (c, p)))
-
-
-def sum_everywhere(value):
-    for where in (CORE, X, Y, Z, Z3):
-        value = value + shuffle(value, *where)
-    return value
+        add(a, ([4], m), ([0, 4], p)),
+        add(b, ([0, 1], y), ([1], m)),
+        add(c, ([3], y), ([0], m), ([3], p)),
+    )
+    y, m, p = yield shuffle(a, *Y), turn(b, -1), turn(c, 1)
+    yield tuple((u, v) for u, v in ((a, y), (b, m), (c, p)))
 
 
 def local_small(
@@ -551,115 +624,184 @@
     me = jnp.stack([feat, own, position, core, xx, yy, zz]).astype(jnp.int32)
 
     x = layer_input.reshape(1024, 512)
-    pieces = send_context(x, position)
+    x4, cot4 = layer_input.reshape(4, 256, 512), cotangent.reshape(4, 256, 512)
     tasks = segment_ids.reshape(8, 64)
     allow = (at(tasks, samp)[:, None] == at(tasks, root)[None, :]).astype(F32)
     allow = jnp.concatenate([allow] * 4, axis=1)
 
-    both = jnp.stack([layer_input.reshape(4, 256, 512), cotangent.reshape(4, 256, 512)], axis=1)
-    both = swap_blocks([at(both, feat ^ d) for d in range(4)], "feat")
-    x_f = jnp.stack([pair[0] for pair in both])
-    cot_f = jnp.stack([pair[1] for pair in both])
+    steps = send_context(x, position)
+    block = lambda value, d: at(value, feat ^ d)
+    to_core = jnp.stack([block(x4, 1), block(cot4, 1), block(x4, 3), block(cot4, 3)])
+    got, from_core = fence((next(steps), shuffle(to_core, *CORE)))
+    to_x = jnp.stack([block(x4, 2), from_core[2]])
+    got, x_far = fence((steps.send(got), shuffle(to_x, *X)))
+    to_x = jnp.stack([block(cot4, 2), from_core[3]])
+    got, cot_far, allow = fence((steps.send(got), shuffle(to_x, *X), allow))
+    pieces = steps.send(got)
 
     heads = sds((16, 4, 16, 512))
-    o1, context, q1, k1, v1, p1 = whole(
-        forward_one, "forward_one",
-        (sds((4, 256, 512)), sds((1024, 512)), heads, heads, heads, sds((16, 64, 512), F32)),
+    quarter = sds((256, 512))
+    *o_blocks, o1, context, q1, k1, v1, p1 = whole(
+        forward_one, "forward_one", 32,
+        (quarter,) * 4
+        + (sds((4, 256, 512)), sds((1024, 512)), heads, heads, heads, sds((16, 64, 512), F32)),
         [pltpu.VMEM((16, 4, 16, 512), BF)],
         me, x, *pieces, allow, row(first_gain), row(first_shift), sample_weight, row(sample_bias),
     )
-    o1_f = jnp.stack(swap_blocks([o1[d] for d in range(4)], "feat"))
+    o_blocks[1:] = fence([shuffle(o_blocks[d], "feat", d) for d in range(1, 4)])
 
     weights = [
         sample_mixer, row(sample_offset), row(second_gain), row(second_shift), feature_weight,
         row(feature_bias), feature_mixer, row(feature_offset), row(third_gain), row(third_shift),
         expand_weight, row(expand_bias), reduce_weight, row(reduce_bias),
     ]
-    blocked = spec((4, 64, 512), lambda i: (0, i, 0))
-    wide = lambda n: spec((256, n), lambda i: (i, 0))
-    out_f, gb1_f, act2, dqkv, o2, gb2, act3, gu, hidden, gb3, vec2, bias2 = pl.pallas_call(
+    flat = spec((64, 512), lambda i, m: (i, 0))
+    own = spec((None, 64, 512), lambda i, m: (m[0], i, 0))
+    part = lambda n: spec((None, 64, 512), lambda i, m: (n, i, 0))
+    wide = lambda n: spec((256, n), lambda i, m: (i, 0))
+    still = lambda shape: spec(shape, lambda i, m: (0, 0))
+    (
+        out0, out2, out13, g0, g1, g2, g3,
+        act2, dqkv, o2, gb2, act3, gu, hidden, gb3, vec2, bias2,
+    ) = pl.pallas_call(
         middle,
-        grid=(4,),
+        grid_spec=pltpu.PrefetchScalarGridSpec(
+            num_scalar_prefetch=1,
+            grid=(4,),
+            in_specs=[flat] * 4
+            + [own, part(0), part(0), part(1), own, part(1), part(0), part(1)]
+            + [
+                pl.BlockSpec(w.shape, lambda i, m: (0, 0), pipeline_mode=pl.Buffered(1))
+                for w in weights
+            ],
+            out_specs=[
+                flat, flat, spec((2, 64, 512), lambda i, m: (0, i, 0)), flat, flat, flat, flat,
+                wide(512), wide(1536), wide(512), wide(512), wide(512), wide(2048), wide(2048),
+                wide(512), still((8, 512)), still((1, 2048)),
+            ],
+        ),
         out_shape=(
-            sds((4, 256, 512)), sds((4, 256, 512)), sds((1024, 512)), sds((1024, 1536)),
-            sds((1024, 512)), sds((1024, 512)), sds((1024, 512)), sds((1024, 2048)),
-            sds((1024, 2048)), sds((1024, 512)), sds((8, 512), F32), sds((1, 2048), F32),
+            quarter, quarter, sds((2, 256, 512)), quarter, quarter, quarter, quarter,
+            sds((1024, 512)), sds((1024, 1536)), sds((1024, 512)), sds((1024, 512)),
+            sds((1024, 512)), sds((1024, 2048)), sds((1024, 2048)), sds((1024, 512)),
+            sds((8, 512), F32), sds((1, 2048), F32),
         ),
-        in_specs=[blocked] * 3
-        + [pl.BlockSpec(w.shape, lambda i: (0, 0), pipeline_mode=pl.Buffered(1)) for w in weights],
-        out_specs=[
-            blocked, blocked, wide(512), wide(1536), wide(512), wide(512), wide(512), wide(2048),
-            wide(2048), wide(512), spec((8, 512)), spec((1, 2048)),
-        ],
-        compiler_params=params(),
+        compiler_params=params(44),
         name="middle",
-    )(o1_f, x_f, cot_f, *weights)
-
-    gb1 = jnp.stack(swap_blocks([gb1_f[d] for d in range(4)], "feat"))
-    out4 = jnp.stack(swap_blocks([out_f[d] for d in range(4)], "feat"))
-    order4 = feat ^ jnp.arange(4, dtype=jnp.int32)
-    layer_output = jnp.take(out4, order4, axis=0).reshape(64, 16, 512)
+    )(me, *o_blocks, x4, from_core, x_far, x_far, cot4, from_core, cot_far, cot_far, *weights)
 
     rk, rs = whole(
-        grads_reduce, "grads_reduce", (sds((8, 128, 512)), sds((8, 128, 512))),
+        grads_reduce, "grads_reduce", 16, (sds((8, 128, 512)), sds((8, 128, 512))),
         [pltpu.VMEM((2048, 512), BF)], me, hidden, gb3,
     )
     ek, es = whole(
-        grads_expand, "grads_expand", (sds((8, 2, 64, 512)), sds((8, 2, 64, 512))),
+        grads_expand, "grads_expand", 16, (sds((8, 2, 64, 512)), sds((8, 2, 64, 512))),
         [pltpu.VMEM((4, 512, 512), BF)], me, act3, gu,
     )
     fk, fs = whole(
-        grads_feature, "grads_feature", (sds((2, 8, 64, 512)), sds((2, 8, 64, 512))),
+        grads_feature, "grads_feature", 16, (sds((2, 8, 64, 512)), sds((2, 8, 64, 512))),
         [pltpu.VMEM((4, 512, 512), BF)], me, act2, dqkv, o2, gb2,
     )
     three = lambda a: a.reshape((2, 2, 2) + a.shape[1:])
     four = lambda a: a.reshape((2, 2, 2, 2) + a.shape[2:])
-    r_part = chain(three(rk), three(rs), (Z, Z3, Y))
-    e_part = chain(three(ek), three(es), (Y, Z, Z3))
-    f_part = chain(four(fk), four(fs), (X, Y, Z, Z3))
+    r_chain = Chain(three(rk), three(rs), (Z, Z3, Y))
+    e_chain = Chain(three(ek), three(es), (Y, Z, Z3))
+    f_chain = Chain(four(fk), four(fs), (X, Y, Z, Z3))
+    g1, g2, g3 = together(
+        [r_chain, e_chain, f_chain],
+        lambda: [shuffle(g, "feat", d) for d, g in ((1, g1), (2, g2), (3, g3))],
+    )
+
+    half_of = lambda a, i: (a, (8,) + a.shape[1:], (i,) + (0,) * (a.ndim - 1))
+    half_heads = sds((8, 4, 16, 512))
+    gb1, go, dqa, dkva = together(
+        [r_chain, e_chain, f_chain],
+        lambda: whole(
+            backward_first, "backward_first", 24,
+            (sds((4, 256, 512)), heads, half_heads, sds((8, 4, 16, 1024))), [],
+            me, g0, g1, g2, g3, *(half_of(a, 0) for a in (q1, k1, v1, p1)), sample_mixer,
+        ),
+    )
 
     third = sds((THIRD, 512))
-    ta, tb, tc, cact, dkv, dq_heads, vec_c = whole(
-        backward_one, "backward_one",
-        (third, third, third, sds((1024, 512)), sds((1024, 1024)), heads, sds((8, 512), F32)),
-        [
-            pltpu.VMEM((16, 4, 16, 512), BF),
-            pltpu.VMEM((16, 4, 16, 1024), BF),
-            pltpu.VMEM((1024, 512), BF),
-        ],
-        me, gb1, context, q1, k1, v1, p1, row(first_gain), row(first_shift), sample_weight,
-        sample_mixer,
-    )
-    sums = sum_context(ta, tb, tc, position)
-    base, act1, dq1, vec1 = whole(
-        backward_query, "backward_query",
-        (sds((1024, 512), F32), sds((1024, 512)), sds((1024, 512)), sds((8, 512), F32)),
-        [],
-        me, gb1, x, dq_heads, vec_c, row(first_gain), row(first_shift), sample_weight,
-    )
-    sxk, sxs, syk, sys_ = whole(
-        grads_sample, "grads_sample",
-        (sds((2, 8, 32, 512)), sds((2, 8, 32, 512)), sds((8, 64, 512)), sds((8, 64, 512))),
-        [pltpu.VMEM((4, 512, 512), BF)],
-        me, act1, dq1, cact, dkv, o1, gb1,
-    )
-    sx_part = chain(four(sxk), four(sxs), (X, Y, Z, Z3))
-    sy_part = chain(three(syk), three(sys_), (Y, Z, Z3))
-
-    vectors = sum_everywhere(
-        jnp.concatenate([vec2.reshape(-1), bias2.reshape(-1), vec1.reshape(-1)])
-    )
-
-    both_x = lambda part: plus(part, shuffle(part, *X))
-    reduce_grad = join_two(both_x(r_part), core, CORE).reshape(256, 512).astype(F32)
-    expand_blocks = join_two(both_x(e_part), core, CORE).reshape(4, 64, 512).astype(F32)
-    feature_blocks = join_two(join_two(f_part, xx, X), core, CORE).reshape(4, 64, 512).astype(F32)
-    sx = join_two(f_or_s(sx_part, xx), core, CORE).astype(F32)
-    sy = join_two(both_x(sy_part), core, CORE).astype(F32)
-
+    (ta, tb, tc, cact, dkv, dqb, vec_c), near = together(
+        [r_chain, e_chain, f_chain],
+        lambda: (
+            whole(
+                backward_second, "backward_second", 32,
+                (
+                    third, third, third, sds((1024, 512)), sds((1024, 1024)), half_heads,
+                    sds((8, 512), F32),
+                ),
+                [pltpu.VMEM((8, 4, 16, 1024), BF), pltpu.VMEM((1024, 512), BF)],
+                me, go, *(half_of(a, 1) for a in (q1, k1, v1, p1)), dkva, context,
+                row(first_gain), row(first_shift), sample_weight,
+            ),
+            shuffle(out13, *CORE),
+        ),
+    )
+
+    steps = sum_context(ta, tb, tc, position)
+
+    def rest():
+        base, act1, dq1, vec1 = whole(
+            backward_query, "backward_query", 24,
+            (sds((1024, 512), F32), sds((1024, 512)), sds((1024, 512)), sds((8, 512), F32)), [],
+            me, gb1, x, dqa, dqb, vec_c, row(first_gain), row(first_shift), sample_weight,
+        )
+        grads = whole(
+            grads_sample, "grads_sample", 16,
+            (sds((2, 8, 32, 512)), sds((2, 8, 32, 512)), sds((8, 64, 512)), sds((8, 64, 512))),
+            [pltpu.VMEM((4, 512, 512), BF)],
+            me, act1, dq1, cact, dkv, o1, gb1,
+        )
+        far = shuffle(jnp.stack([out2, near[1]]), *X)
+        return next(steps), base, vec1, grads, far
+
+    got, base, vec1, (sxk, sxs, syk, sys_), far = together([r_chain, e_chain], rest)
+    vectors = jnp.concatenate([vec2.reshape(-1), bias2.reshape(-1), vec1.reshape(-1)])
+    vector_dims = [CORE, X, Y, Z, Z3]
+
+    def add_vectors():
+        return shuffle(vectors, *vector_dims.pop(0))
+
+    sx_chain = Chain(four(sxk), four(sxs), (X, Y, Z, Z3))
+    sy_chain = Chain(three(syk), three(sys_), (Y, Z, Z3))
+    layer_output = whole(
+        place, "place", 16, sds((4, 256, 512)), [], me, out0,
+        (near, (None, 256, 512), (0, 0, 0)), (far, (None, 256, 512), (0, 0, 0)),
+        (far, (None, 256, 512), (1, 0, 0)),
+    ).reshape(64, 16, 512)
+    rows_a, others = last_round([r_chain.keep, e_chain.keep])
+    got, others, v, layer_output = together(
+        [sx_chain, sy_chain, f_chain],
+        lambda: (steps.send(got), others, add_vectors(), layer_output),
+    )
+    rows_a = [rows_a] + others
+    vectors = vectors + v
+    got, v = together(
+        [sx_chain, sy_chain, f_chain], lambda: (steps.send(got), add_vectors())
+    )
+    vectors = vectors + v
     input_grad = whole(
-        finish, "finish", sds((1024, 512)), [], me, base, *sums, x, row(first_gain)
+        finish, "finish", 24, sds((1024, 512)), [],
+        me, base, *(v for pair in steps.send(got) for v in pair), x, row(first_gain),
     ).reshape(64, 16, 512)
+    v, input_grad = together([sx_chain, sy_chain], lambda: (add_vectors(), input_grad))
+    vectors = vectors + v
+    (v,) = together([sx_chain, sy_chain], lambda: (add_vectors(),))
+    vectors = vectors + v
+    (v,) = together([sx_chain], lambda: (add_vectors(),))
+    vectors = vectors + v
+    rows_b, others = last_round([f_chain.keep, sx_chain.keep, sy_chain.keep])
+    rows_b = [rows_b] + others
+
+    cut = lambda rows, start, count: [r[start : start + count] for r in rows]
+    reduce_grad = pick_sum(cut(rows_a, 0, 128), core).reshape(256, 512)
+    expand = pick_sum(cut(rows_a, 128, 128), core).reshape(4, 64, 512)
+    feature = pick_join(cut(rows_b, 0, 64), core, xx)
+    sx = pick_join(cut(rows_b, 64, 32), core, xx).reshape(2, 64, 512)
+    sy = pick_sum(cut(rows_b, 96, 64), core)
 
     def vector(start, size):
         return lax.dynamic_slice_in_dim(vectors[start : start + size], samp * (size // 8), size // 8)
@@ -672,15 +814,11 @@
     return (
         layer_output, input_grad,
         gain1, shift1, columns([sx[0], sy[0], sx[1]]), vector(6144 + 3 * 512, 1024), sy[1], off1,
-        gain2, shift2, columns([feature_blocks[i] for i in range(3)]), vector(6 * 512, 1024),
-        feature_blocks[3], off2,
-        gain3, shift3, columns([expand_blocks[i] for i in range(4)]), expand_b,
+        gain2, shift2, columns([feature[i] for i in range(3)]), vector(6 * 512, 1024),
+        feature[3], off2,
+        gain3, shift3, columns([expand[i] for i in range(4)]), expand_b,
         reduce_grad, bias_r,
     )
-
-
-def f_or_s(half, xx):
-    return join_two(half, xx, X).reshape(64, 512)
 
 
 def spread_2(block, axis, owner):

time: 403 us -> 358 us (0.89)
  Pallas kernels: 132 us -> 108 us
  waiting for transfers between devices: 131 us -> 114 us
    pallas_call x9 -> x11, Pallas kernels: 132 us -> 108 us  [the longest x10 56.7 us: whole(): pl.pallas_call(kernel, grid=(1,), out_shape=outs, in_specs=specs, out_spe...]
    ppermute x55 -> x50, waiting for transfers between devices: 93.7 us -> 69.6 us  [shuffle(): return lax.ppermute(value, axis, [(i, i ^ mask) for i in range(size)])]
    unnamed x68 -> x116, local copies, waits for them, and re-layouts: 1.66 us -> 15 us
    slice x12 -> x7, local copies, waits for them, and re-layouts: 13.4 us -> 1.18 us  [the longest x1 0.86 us: local_small(): to_x = jnp.stack([block(cot4, 2), from_core[3]])]
    ppermute x12, waiting for transfers between devices: 37.7 us -> 44.2 us  [turn(): lax.ppermute(value, 'samp', [(i, (i + 2 * step) % 8) for i in range(8)])]
    ppermute x12, starting transfers between devices: 24.4 us -> 18.7 us  [turn(): lax.ppermute(value, 'samp', [(i, (i + 2 * step) % 8) for i in range(8)])]
    convert_element_type x25 -> x22, other arithmetic: 4.49 us -> 9.28 us  [plus(): return (a.astype(F32) + b.astype(F32)).astype(BF)]
    ppermute x55 -> x50, starting transfers between devices: 50.6 us -> 54.9 us  [shuffle(): return lax.ppermute(value, axis, [(i, i ^ mask) for i in range(size)])]
  transfers between devices with their start and end apart: 67 -> 62, of which waited for: 31 -> 27; matrix products, arithmetic and copies ran while one was open for 12% -> 8% of each run, Pallas kernels for 19% -> 10%
where the time goes in v3:
time: 358 us; the launch traced here: 355 us
  waiting for transfers between devices  114 us (32%)
  Pallas kernels  108 us (30%)
  starting transfers between devices  73.6 us (21%)
  other arithmetic  26.7 us (7%)
  local copies, waits for them, and re-layouts  26.5 us (7%)
  between operations  5.81 us (2%)
    ppermute x50, waiting for transfers between devices, shuffle(): return lax.ppermute(value, axis, [(i, i ^ mask) for i in range(size)])  69.6 us
    pallas_call x10, Pallas kernels, whole(): pl.pallas_call(kernel, grid=(1,), out_shape=outs, in_specs=specs, out_spe...  56.7 us
    ppermute x50, starting transfers between devices, shuffle(): return lax.ppermute(value, axis, [(i, i ^ mask) for i in range(size)])  54.9 us
    pallas_call x1, Pallas kernels, local_small(): pl.pallas_call(middle, grid_spec=pltpu.PrefetchScalarGridSpec(num_scalar_...  51.4 us
    ppermute x12, waiting for transfers between devices, turn(): lax.ppermute(value, 'samp', [(i, (i + 2 * step) % 8) for i in range(8)])  44.2 us
    ppermute x12, starting transfers between devices, turn(): lax.ppermute(value, 'samp', [(i, (i + 2 * step) % 8) for i in range(8)])  18.7 us
    unnamed x116, local copies, waits for them, and re-layouts  15 us
    convert_element_type x22, other arithmetic, plus(): return (a.astype(F32) + b.astype(F32)).astype(BF)  9.28 us
  transfers between devices with their start and end apart: 62, of which 27 were waited for; matrix products, arithmetic and copies ran while one was open for 8% of the time, Pallas kernels for 10%

profile of v3, /device:TPU:0, one launch (start us, length us, event | category | flops | bytes accessed | tf_op | source)
XLA Modules:
  0.0 354.6 jit_solution(7372895826605688561)
XLA Ops:
  0.7 2.0 constant_dynamic-slice_fusion.2
  5.3 2.5 collective-permute-start
  9.4 2.2 collective-permute-start.2
  15.2 1.9 collective-permute-done.y1
  17.1 4.0 %collective-permute-done.1.p1 = bf16[352,512]{1,0:T(8,128)(2,1)S(1)} collective-permute-done((bf16[352,512]{1,0:T(8,128)(2,1)}, bf16[352,512]{1,0:T(8,128)(2,1)S(1)}, u32[]{:S(2)}, u32[]{:S(2)}) %collective-permute-start.1) | collective-permute-done | bytes 360480 | tf_op jit(solution)/shard_map/ppermute | solution.py:493
  21.1 6.5 %collective-permute-done.2.m1 = bf16[352,512]{1,0:T(8,128)(2,1)S(1)} collective-permute-done((bf16[352,512]{1,0:T(8,128)(2,1)}, bf16[352,512]{1,0:T(8,128)(2,1)S(1)}, u32[]{:S(2)}, u32[]{:S(2)}) %collective-permute-start.2) | collective-permute-done | bytes 360480 | tf_op jit(solution)/shard_map/ppermute | solution.py:493
  31.0 2.2 select_select_fusion.3
  34.9 2.7 collective-permute-start.6
  39.0 2.0 pad_maximum_fusion.2
  43.0 4.2 %collective-permute-done.5.p2 = bf16[352,512]{1,0:T(8,128)(2,1)} collective-permute-done((bf16[352,512]{1,0:T(8,128)(2,1)}, bf16[352,512]{1,0:T(8,128)(2,1)}, u32[]{:S(2)}, u32[]{:S(2)}) %collective-permute-start.5) | collective-permute-done | bytes 360480 | tf_op jit(solution)/shard_map/ppermute | solution.py:493
  47.2 5.2 %collective-permute-done.6.m2 = bf16[352,512]{1,0:T(8,128)(2,1)} collective-permute-done((bf16[352,512]{1,0:T(8,128)(2,1)}, bf16[352,512]{1,0:T(8,128)(2,1)}, u32[]{:S(2)}, u32[]{:S(2)}) %collective-permute-start.6) | collective-permute-done | bytes 360480 | tf_op jit(solution)/shard_map/ppermute | solution.py:493
  52.4 1.9 select_select_fusion.2
  54.3 2.1 collective-permute-start.10
  56.4 2.1 broadcast_select_fusion.3
  60.3 11.8 %collective-permute-done.10.m3 = bf16[352,512]{1,0:T(8,128)(2,1)} collective-permute-done((bf16[352,512]{1,0:T(8,128)(2,1)}, bf16[352,512]{1,0:T(8,128)(2,1)}, u32[]{:S(2)}, u32[]{:S(2)}) %collective-permute-start.10) | collective-permute-done | bytes 360480 | tf_op jit(solution)/shard_map/ppermute | solution.py:493
  74.3 19.6 %forward_one.1 = (bf16[256,512]{1,0:T(8,128)(2,1)S(1)}, bf16[256,512]{1,0:T(8,128)(2,1)S(1)}, bf16[256,512]{1,0:T(8,128)(2,1)S(1)}, bf16[256,512]{1,0:T(8,128)(2...) custom-call(s32[7]{0:T(128)S(1)} %stack.95.me_ref, ...), custom_call_target="tpu_custom_call" | custom-call | tf_op jit(solution)/shard_map/forward_one/pallas_call | solution.py:472
  97.8 7.3 %collective-permute-done.13.o2_ = bf16[256,512]{1,0:T(8,128)(2,1)S(1)} collective-permute-done((bf16[256,512]{1,0:T(8,128)(2,1)S(1)}, bf16[256,512]{1,0:T(8,128)(2,1)S(1)}, u32[]{:S(2)}, u32[]{:S(2)}) %collective-permute-start.13) | collective-permute-done | bytes 262176 | tf_op jit(solution)/shard_map/ppermute | solution.py:486
  105.1 4.7 %collective-permute-done.14.o3 = bf16[256,512]{1,0:T(8,128)(2,1)S(1)} collective-permute-done((bf16[256,512]{1,0:T(8,128)(2,1)S(1)}, bf16[256,512]{1,0:T(8,128)(2,1)S(1)}, u32[]{:S(2)}, u32[]{:S(2)}) %collective-permute-start.14) | collective-permute-done | bytes 262176 | tf_op jit(solution)/shard_map/ppermute | solution.py:486
  109.9 51.4 %middle.1 = (bf16[256,512]{1,0:T(8,128)(2,1)S(1)}, bf16[256,512]{1,0:T(8,128)(2,1)S(1)}, bf16[2,256,512]{2,1,0:T(8,128)(2,1)}, bf16[256,512]{1,0:T(8,128)(2,1)S(...) custom-call(s32[7]{0:T(128)S(1)} %stack.95.me_ref, ...), custom_call_target="tpu_custom_call" | custom-call | tf_op jit(solution)/shard_map/middle/pallas_call | solution.py:666
  162.3 2.0 copy-done.17
  164.3 3.0 grads_feature.1
  167.7 3.0 grads_expand.1
  171.1 3.1 grads_reduce.1
  177.7 6.1 %collective-permute-done.19.g2 = bf16[256,512]{1,0:T(8,128)(2,1)S(1)} collective-permute-done((bf16[256,512]{1,0:T(8,128)(2,1)S(1)}, bf16[256,512]{1,0:T(8,128)(2,1)S(1)}, u32[]{:S(2)}, u32[]{:S(2)}) %collective-permute-start.19) | collective-permute-done | bytes 262176 | tf_op jit(solution)/shard_map/ppermute | solution.py:486
  183.8 4.3 %collective-permute-done.20.g3 = bf16[256,512]{1,0:T(8,128)(2,1)S(1)} collective-permute-done((bf16[256,512]{1,0:T(8,128)(2,1)S(1)}, bf16[256,512]{1,0:T(8,128)(2,1)S(1)}, u32[]{:S(2)}, u32[]{:S(2)}) %collective-permute-start.20) | collective-permute-done | bytes 262176 | tf_op jit(solution)/shard_map/ppermute | solution.py:486
  192.6 8.3 %backward_first.1 = (bf16[4,256,512]{2,1,0:T(8,128)(2,1)S(1)}, bf16[16,4,16,512]{3,2,1,0:T(8,128)(2,1)S(1)}, bf16[8,4,16,512]{3,2,1,0:T(8,128)(2,1)S(1)}, bf16[8,4,16,1024]{3,2,1,0:T(8,128)(2,1)S(1)}) custom-call(s32[7]{0:T(128)S(1)} %stack.95.me_ref, bf16[256,512]{1,0:T(8,128)(2,1)S(1)} %get-tuple-element.191.g0, ...), custom_call_target="tpu_custom_call" | custom-call | tf_op jit(solution)/shard_map/backward_first/pallas_call | solution.py:472
  201.0 1.9 collective-permute-done.23
  209.7 2.4 collective-permute-start.24
  219.8 9.1 %backward_second.1 = (bf16[352,512]{1,0:T(8,128)(2,1)S(1)}, bf16[352,512]{1,0:T(8,128)(2,1)S(1)}, bf16[352,512]{1,0:T(8,128)(2,1)S(1)}, bf16[1024,512]{1,0:T(8,1...) custom-call(s32[7]{0:T(128)S(1)} %stack.95.me_ref, ...), custom_call_target="tpu_custom_call" | custom-call | tf_op jit(solution)/shard_map/backward_second/pallas_call | solution.py:472
  235.3 3.4 collective-permute-start.29
  238.7 2.9 backward_query.1
  241.6 3.0 grads_sample.1
  245.6 3.9 %collective-permute-done.29 = bf16[2,64,512]{2,1,0:T(8,128)(2,1)S(1)} collective-permute-done((bf16[2,64,512]{2,1,0:T(8,128)(2,1)S(1)}, bf16[2,64,512]{2,1,0:T(8,128)(2,1)S(1)}, u32[]{:S(2)}, u32[]{:S(2)}) %collective-permute-start.29) | collective-permute-done | bytes 131104 | tf_op jit(solution)/shard_map/ppermute | solution.py:486
  252.0 2.4 collective-permute-done.28
  254.4 3.8 %collective-permute-start.36 = (bf16[2,64,512]{2,1,0:T(8,128)(2,1)S(1)}, bf16[2,64,512]{2,1,0:T(8,128)(2,1)S(1)}, u32[]{:S(2)}, u32[]{:S(2)}) collective-permute-start(bf16[2,64,512]{2,1,0:T(8,128)(2,1)S(1)} %get-tuple-element.348), channel_id=1, source_target_pairs={{0,8},{4,12},{8,0},{12,4},{16,24},{20,28},{24,16},{28,20},{1,9},{5... | collective-permute-start | bytes 393224 | tf_op jit(solution)/shard_map/ppermute | solution.py:486
  265.1 4.3 %collective-permute-done.41 = bf16[256,512]{1,0:T(8,128)(2,1)S(1)} collective-permute-done((bf16[256,512]{1,0:T(8,128)(2,1)S(1)}, bf16[256,512]{1,0:T(8,128)(2,1)S(1)}, u32[]{:S(2)}, u32[]{:S(2)}) %collective-permute-start.41) | collective-permute-done | bytes 262176 | tf_op jit(solution)/shard_map/ppermute | solution.py:486
  269.4 3.4 collective-permute-start.38
  275.8 5.9 %collective-permute-done.38 = bf16[352,512]{1,0:T(8,128)(2,1)S(1)} collective-permute-done((bf16[352,512]{1,0:T(8,128)(2,1)S(1)}, bf16[352,512]{1,0:T(8,128)(2,1)S(1)}, u32[]{:S(2)}, u32[]{:S(2)}) %collective-permute-start.38) | collective-permute-done | bytes 360480 | tf_op jit(solution)/shard_map/ppermute | solution.py:493
  281.7 6.6 %collective-permute-done.39 = bf16[352,512]{1,0:T(8,128)(2,1)S(1)} collective-permute-done((bf16[352,512]{1,0:T(8,128)(2,1)S(1)}, bf16[352,512]{1,0:T(8,128)(2,1)S(1)}, u32[]{:S(2)}, u32[]{:S(2)}) %collective-permute-start.39) | collective-permute-done | bytes 360480 | tf_op jit(solution)/shard_map/ppermute | solution.py:493
  290.4 3.6 %collective-permute-start.48 = (bf16[352,512]{1,0:T(8,128)(2,1)S(1)}, bf16[352,512]{1,0:T(8,128)(2,1)S(1)}, u32[]{:S(2)}, u32[]{:S(2)}) collective-permute-start(bf16[352,512]{1,0:T(8,128)(2,1)S(1)} %get-tuple-element.323.b_ref), channel_id=1, source_target_pairs={{0,24},{4,28},{8,0},{12,4},{16,8},{20,12},{24,16},{28,20},{1,25},{... | collective-permute-start | bytes 1081352 | tf_op jit(solution)/shard_map/ppermute | solution.py:493
  294.0 3.9 %collective-permute-start.46 = (bf16[64,512]{1,0:T(8,128)(2,1)S(1)}, bf16[64,512]{1,0:T(8,128)(2,1)S(1)}, u32[]{:S(2)}, u32[]{:S(2)}) collective-permute-start(bf16[64,512]{1,0:T(8,128)(2,1)S(1)} %fusion.56), channel_id=1, source_target_pairs={{0,24},{4,28},{8,16},{12,20},{16,8},{20,12},{24,0},{28,4},{1,25},{... | collective-permute-start | bytes 196616 | tf_op jit(solution)/shard_map/ppermute | solution.py:486
  299.6 11.9 %collective-permute-done.46 = bf16[64,512]{1,0:T(8,128)(2,1)S(1)} collective-permute-done((bf16[64,512]{1,0:T(8,128)(2,1)S(1)}, bf16[64,512]{1,0:T(8,128)(2,1)S(1)}, u32[]{:S(2)}, u32[]{:S(2)}) %collective-permute-start.46) | collective-permute-done | bytes 65568 | tf_op jit(solution)/shard_map/ppermute | solution.py:486
  313.1 5.2 %collective-permute-done.44 = bf16[2,2,2,32,512]{4,3,2,1,0:T(8,128)(2,1)S(1)} collective-permute-done((bf16[2,2,2,32,512]{4,3,2,1,0:T(8,128)(2,1)S(1)}, bf16[2,2,2,32,512]{4,3,2,1,0:T(8,128)(2,1)S(1)}, u32[]{:S(2)}, u32[]{:S(2)}) %collective-permute-start.44) | collective-permute-done | bytes 262176 | tf_op jit(solution)/shard_map/ppermute | solution.py:486
  322.6 3.1 finish.1
  325.7 2.0 collective-permute-start.55
  329.9 3.5 collective-permute-done.56
  333.4 2.1 collective-permute-start.57
  339.1 2.1 collective-permute-done.58
  (293 shorter events, 92.3 us)
Async XLA Ops:
  3.8 23.8 %collective-permute-start.3 = (bf16[4,256,512]{2,1,0:T(8,128)(2,1)}, bf16[4,256,512]{2,1,0:T(8,128)(2,1)S(1)}, u32[]{:S(2)}, u32[]{:S(2)}) collective-permute-start(bf16[4,256,512]{2,1,0:T(8,128)(2,1)} %pad_maximum_fusion), channel_id=1, source_target_pairs={{0,1},{1,0},{2,3},{3,2},{4,5},{5,4},{6,7},{7,6},{8,9},{9,8},{10,11... | collective-permute-start | bytes 3145736 | tf_op jit(solution)/shard_map/ppermute | solution.py:486
  5.3 11.8 %collective-permute-start = (bf16[352,512]{1,0:T(8,128)(2,1)}, bf16[352,512]{1,0:T(8,128)(2,1)S(1)}, u32[]{:S(2)}, u32[]{:S(2)}) collective-permute-start(bf16[352,512]{1,0:T(8,128)(2,1)} %bitcast.8), channel_id=1, source_target_pairs={{0,4},{4,0},{8,12},{12,8},{16,20},{20,16},{24,28},{28,24},{1,5},{5... | collective-permute-start | bytes 1081352 | tf_op jit(solution)/shard_map/ppermute | solution.py:486
  7.8 13.3 %collective-permute-start.1 = (bf16[352,512]{1,0:T(8,128)(2,1)}, bf16[352,512]{1,0:T(8,128)(2,1)S(1)}, u32[]{:S(2)}, u32[]{:S(2)}) collective-permute-start(bf16[352,512]{1,0:T(8,128)(2,1)} %bitcast.9), channel_id=1, source_target_pairs={{0,8},{4,12},{8,16},{12,20},{16,24},{20,28},{24,0},{28,4},{1,9},{5... | collective-permute-start | bytes 1081352 | tf_op jit(solution)/shard_map/ppermute | solution.py:493
  9.4 18.2 %collective-permute-start.2 = (bf16[352,512]{1,0:T(8,128)(2,1)}, bf16[352,512]{1,0:T(8,128)(2,1)S(1)}, u32[]{:S(2)}, u32[]{:S(2)}) collective-permute-start(bf16[352,512]{1,0:T(8,128)(2,1)} %bitcast.10), channel_id=1, source_target_pairs={{0,24},{4,28},{8,0},{12,4},{16,8},{20,12},{24,16},{28,20},{1,25},{... | collective-permute-start | bytes 1081352 | tf_op jit(solution)/shard_map/ppermute | solution.py:493
  29.5 22.9 %collective-permute-start.7 = (bf16[2,256,512]{2,1,0:T(8,128)(2,1)}, bf16[2,256,512]{2,1,0:T(8,128)(2,1)S(1)}, u32[]{:S(2)}, u32[]{:S(2)}) collective-permute-start(bf16[2,256,512]{2,1,0:T(8,128)(2,1)} %pad_maximum_fusion.1), channel_id=1, source_target_pairs={{0,2},{1,3},{2,0},{3,1},{4,6},{5,7},{6,4},{7,5},{8,10},{9,11},{10,... | collective-permute-start | bytes 1572872 | tf_op jit(solution)/shard_map/ppermute | solution.py:486
  33.2 9.8 %collective-permute-start.4 = (bf16[352,512]{1,0:T(8,128)(2,1)}, bf16[352,512]{1,0:T(8,128)(2,1)}, u32[]{:S(2)}, u32[]{:S(2)}) collective-permute-start(bf16[352,512]{1,0:T(8,128)(2,1)} %get-tuple-element.356), channel_id=1, source_target_pairs={{0,4},{4,0},{8,12},{12,8},{16,20},{20,16},{24,28},{28,24},{1,5},{5... | collective-permute-start | bytes 1081352 | tf_op jit(solution)/shard_map/ppermute | solution.py:486
  33.7 13.5 %collective-permute-start.5 = (bf16[352,512]{1,0:T(8,128)(2,1)}, bf16[352,512]{1,0:T(8,128)(2,1)}, u32[]{:S(2)}, u32[]{:S(2)}) collective-permute-start(bf16[352,512]{1,0:T(8,128)(2,1)} %get-tuple-element.357), channel_id=1, source_target_pairs={{0,8},{4,12},{8,16},{12,20},{16,24},{20,28},{24,0},{28,4},{1,9},{5... | collective-permute-start | bytes 1081352 | tf_op jit(solution)/shard_map/ppermute | solution.py:493
  34.9 17.5 %collective-permute-start.6 = (bf16[352,512]{1,0:T(8,128)(2,1)}, bf16[352,512]{1,0:T(8,128)(2,1)}, u32[]{:S(2)}, u32[]{:S(2)}) collective-permute-start(bf16[352,512]{1,0:T(8,128)(2,1)} %get-tuple-element.355), channel_id=1, source_target_pairs={{0,24},{4,28},{8,0},{12,4},{16,8},{20,12},{24,16},{28,20},{1,25},{... | collective-permute-start | bytes 1081352 | tf_op jit(solution)/shard_map/ppermute | solution.py:493
  41.0 19.4 %collective-permute-start.11 = (bf16[2,256,512]{2,1,0:T(8,128)(2,1)}, bf16[2,256,512]{2,1,0:T(8,128)(2,1)}, u32[]{:S(2)}, u32[]{:S(2)}) collective-permute-start(bf16[2,256,512]{2,1,0:T(8,128)(2,1)} %pad_maximum_fusion.2), channel_id=1, source_target_pairs={{0,2},{1,3},{2,0},{3,1},{4,6},{5,7},{6,4},{7,5},{8,10},{9,11},{10,... | collective-permute-start | bytes 1572872 | tf_op jit(solution)/shard_map/ppermute | solution.py:486
  54.3 17.9 %collective-permute-start.10 = (bf16[352,512]{1,0:T(8,128)(2,1)}, bf16[352,512]{1,0:T(8,128)(2,1)}, u32[]{:S(2)}, u32[]{:S(2)}) collective-permute-start(bf16[352,512]{1,0:T(8,128)(2,1)} %select_select_fusion.2), channel_id=1, source_target_pairs={{0,24},{4,28},{8,0},{12,4},{16,8},{20,12},{24,16},{28,20},{1,25},{... | collective-permute-start | bytes 1081352 | tf_op jit(solution)/shard_map/ppermute | solution.py:493
  58.5 13.7 %collective-permute-start.8 = (bf16[352,512]{1,0:T(8,128)(2,1)}, bf16[352,512]{1,0:T(8,128)(2,1)}, u32[]{:S(2)}, u32[]{:S(2)}) collective-permute-start(bf16[352,512]{1,0:T(8,128)(2,1)} %get-tuple-element.354), channel_id=1, source_target_pairs={{0,4},{4,0},{8,12},{12,8},{16,20},{20,16},{24,28},{28,24},{1,5},{5... | collective-permute-start | bytes 1081352 | tf_op jit(solution)/shard_map/ppermute | solution.py:486
  60.0 12.2 %collective-permute-start.9 = (bf16[352,512]{1,0:T(8,128)(2,1)}, bf16[352,512]{1,0:T(8,128)(2,1)}, u32[]{:S(2)}, u32[]{:S(2)}) collective-permute-start(bf16[352,512]{1,0:T(8,128)(2,1)} %get-tuple-element.353), channel_id=1, source_target_pairs={{0,8},{4,12},{8,16},{12,20},{16,24},{20,28},{24,0},{28,4},{1,9},{5... | collective-permute-start | bytes 1081352 | tf_op jit(solution)/shard_map/ppermute | solution.py:493
  95.9 9.2 %collective-permute-start.13 = (bf16[256,512]{1,0:T(8,128)(2,1)S(1)}, bf16[256,512]{1,0:T(8,128)(2,1)S(1)}, u32[]{:S(2)}, u32[]{:S(2)}) collective-permute-start(bf16[256,512]{1,0:T(8,128)(2,1)S(1)} %get-tuple-element.164), channel_id=1, source_target_pairs={{0,2},{1,3},{2,0},{3,1},{4,6},{5,7},{6,4},{7,5},{8,10},{9,11},{10,... | collective-permute-start | bytes 786440 | tf_op jit(solution)/shard_map/ppermute | solution.py:486
  96.5 13.3 %collective-permute-start.14 = (bf16[256,512]{1,0:T(8,128)(2,1)S(1)}, bf16[256,512]{1,0:T(8,128)(2,1)S(1)}, u32[]{:S(2)}, u32[]{:S(2)}) collective-permute-start(bf16[256,512]{1,0:T(8,128)(2,1)S(1)} %get-tuple-element.165), channel_id=1, source_target_pairs={{0,3},{1,2},{2,1},{3,0},{4,7},{5,6},{6,5},{7,4},{8,11},{9,10},{10,... | collective-permute-start | bytes 786440 | tf_op jit(solution)/shard_map/ppermute | solution.py:486
  167.4 20.8 %collective-permute-start.17 = (bf16[2,2,2,2,64,512]{5,4,3,2,1,0:T(8,128)(2,1)S(1)}, bf16[2,2,2,2,64,512]{5,4,3,2,1,0:T(8,128)(2,1)S(1)}, u32[]{:S(2)}, u32[]{:S(2)}) collective-permute-start(bf16[2,2,2,2,64,512]{5,4,3,2,1,0:T(8,128)(2,1)S(1)} %bitcast.279), channel_id=1, source_target_pairs={{0,1},{1,0},{2,3},{3,2},{4,5},{5,4},{6,7},{7,6},{8,9},{9,8},{10,11... | collective-permute-start | bytes 3145736 | tf_op jit(solution)/shard_map/ppermute | solution.py:486
  170.8 17.4 %collective-permute-start.16 = (bf16[2,2,2,2,64,512]{5,4,3,2,1,0:T(8,128)(2,1)S(1)}, bf16[2,2,2,2,64,512]{5,4,3,2,1,0:T(8,128)(2,1)S(1)}, u32[]{:S(2)}, u32[]{:S(2)}) collective-permute-start(bf16[2,2,2,2,64,512]{5,4,3,2,1,0:T(8,128)(2,1)S(1)} %bitcast.280), channel_id=1, source_target_pairs={{0,1},{1,0},{2,3},{3,2},{4,5},{5,4},{6,7},{7,6},{8,9},{9,8},{10,11... | collective-permute-start | bytes 3145736 | tf_op jit(solution)/shard_map/ppermute | solution.py:486
  174.1 14.0 %collective-permute-start.15 = (bf16[2,2,2,128,512]{4,3,2,1,0:T(8,128)(2,1)S(1)}, bf16[2,2,2,128,512]{4,3,2,1,0:T(8,128)(2,1)S(1)}, u32[]{:S(2)}, u32[]{:S(2)}) collective-permute-start(bf16[2,2,2,128,512]{4,3,2,1,0:T(8,128)(2,1)S(1)} %bitcast.281), channel_id=1, source_target_pairs={{0,1},{1,0},{2,3},{3,2},{4,5},{5,4},{6,7},{7,6},{8,9},{9,8},{10,11... | collective-permute-start | bytes 3145736 | tf_op jit(solution)/shard_map/ppermute | solution.py:486
  174.7 9.1 %collective-permute-start.19 = (bf16[256,512]{1,0:T(8,128)(2,1)S(1)}, bf16[256,512]{1,0:T(8,128)(2,1)S(1)}, u32[]{:S(2)}, u32[]{:S(2)}) collective-permute-start(bf16[256,512]{1,0:T(8,128)(2,1)S(1)} %get-tuple-element.184), channel_id=1, source_target_pairs={{0,2},{1,3},{2,0},{3,1},{4,6},{5,7},{6,4},{7,5},{8,10},{9,11},{10,... | collective-permute-start | bytes 786440 | tf_op jit(solution)/shard_map/ppermute | solution.py:486
  177.2 10.9 %collective-permute-start.20 = (bf16[256,512]{1,0:T(8,128)(2,1)S(1)}, bf16[256,512]{1,0:T(8,128)(2,1)S(1)}, u32[]{:S(2)}, u32[]{:S(2)}) collective-permute-start(bf16[256,512]{1,0:T(8,128)(2,1)S(1)} %get-tuple-element.185), channel_id=1, source_target_pairs={{0,3},{1,2},{2,1},{3,0},{4,7},{5,6},{6,5},{7,4},{8,11},{9,10},{10,... | collective-permute-start | bytes 786440 | tf_op jit(solution)/shard_map/ppermute | solution.py:486
  188.5 14.4 %collective-permute-start.23 = (bf16[2,2,2,64,512]{4,3,2,1,0:T(8,128)(2,1)S(1)}, bf16[2,2,2,64,512]{4,3,2,1,0:T(8,128)(2,1)S(1)}, u32[]{:S(2)}, u32[]{:S(2)}) collective-permute-start(bf16[2,2,2,64,512]{4,3,2,1,0:T(8,128)(2,1)S(1)} %get-tuple-element.292), channel_id=1, source_target_pairs={{0,2},{1,3},{2,0},{3,1},{4,6},{5,7},{6,4},{7,5},{8,10},{9,11},{10,... | collective-permute-start | bytes 1572872 | tf_op jit(solution)/shard_map/ppermute | solution.py:486
  189.5 14.1 %collective-permute-start.22 = (bf16[2,2,2,64,512]{4,3,2,1,0:T(8,128)(2,1)S(1)}, bf16[2,2,2,64,512]{4,3,2,1,0:T(8,128)(2,1)S(1)}, u32[]{:S(2)}, u32[]{:S(2)}) collective-permute-start(bf16[2,2,2,64,512]{4,3,2,1,0:T(8,128)(2,1)S(1)} %get-tuple-element.296), channel_id=1, source_target_pairs={{0,4},{4,0},{8,12},{12,8},{16,20},{20,16},{24,28},{28,24},{1,5},{5... | collective-permute-start | bytes 1572872 | tf_op jit(solution)/shard_map/ppermute | solution.py:486
  191.4 13.8 %collective-permute-start.21 = (bf16[2,2,128,512]{3,2,1,0:T(8,128)(2,1)S(1)}, bf16[2,2,128,512]{3,2,1,0:T(8,128)(2,1)S(1)}, u32[]{:S(2)}, u32[]{:S(2)}) collective-permute-start(bf16[2,2,128,512]{3,2,1,0:T(8,128)(2,1)S(1)} %get-tuple-element.301), channel_id=1, source_target_pairs={{0,8},{4,12},{8,0},{12,4},{16,24},{20,28},{24,16},{28,20},{1,9},{5... | collective-permute-start | bytes 1572872 | tf_op jit(solution)/shard_map/ppermute | solution.py:486
  192.6 36.4 %collective-permute-start.27 = (bf16[2,256,512]{2,1,0:T(8,128)(2,1)}, bf16[2,256,512]{2,1,0:T(8,128)(2,1)S(1)}, u32[]{:S(2)}, u32[]{:S(2)}) collective-permute-start(bf16[2,256,512]{2,1,0:T(8,128)(2,1)} %get-tuple-element.216), channel_id=1, source_target_pairs={{0,1},{1,0},{2,3},{3,2},{4,5},{5,4},{6,7},{7,6},{8,9},{9,8},{10,11... | collective-permute-start | bytes 1572872 | tf_op jit(solution)/shard_map/ppermute | solution.py:486
  206.1 22.9 %collective-permute-start.26 = (bf16[2,2,64,512]{3,2,1,0:T(8,128)(2,1)}, bf16[2,2,64,512]{3,2,1,0:T(8,128)(2,1)}, u32[]{:S(2)}, u32[]{:S(2)}) collective-permute-start(bf16[2,2,64,512]{3,2,1,0:T(8,128)(2,1)} %get-tuple-element.288), channel_id=1, source_target_pairs={{0,4},{4,0},{8,12},{12,8},{16,20},{20,16},{24,28},{28,24},{1,5},{5... | collective-permute-start | bytes 786440 | tf_op jit(solution)/shard_map/ppermute | solution.py:486
  207.6 21.4 %collective-permute-start.25 = (bf16[2,2,64,512]{3,2,1,0:T(8,128)(2,1)}, bf16[2,2,64,512]{3,2,1,0:T(8,128)(2,1)}, u32[]{:S(2)}, u32[]{:S(2)}) collective-permute-start(bf16[2,2,64,512]{3,2,1,0:T(8,128)(2,1)} %get-tuple-element.290), channel_id=1, source_target_pairs={{0,8},{4,12},{8,0},{12,4},{16,24},{20,28},{24,16},{28,20},{1,9},{5... | collective-permute-start | bytes 786440 | tf_op jit(solution)/shard_map/ppermute | solution.py:486
  209.7 19.3 %collective-permute-start.24 = (bf16[2,128,512]{2,1,0:T(8,128)(2,1)}, bf16[2,128,512]{2,1,0:T(8,128)(2,1)}, u32[]{:S(2)}, u32[]{:S(2)}) collective-permute-start(bf16[2,128,512]{2,1,0:T(8,128)(2,1)} %get-tuple-element.299), channel_id=1, source_target_pairs={{0,24},{4,28},{8,16},{12,20},{16,8},{20,12},{24,0},{28,4},{1,25},{... | collective-permute-start | bytes 786440 | tf_op jit(solution)/shard_map/ppermute | solution.py:486
  229.1 29.1 %collective-permute-start.33 = (bf16[2,256,512]{2,1,0:T(8,128)(2,1)S(1)}, bf16[2,256,512]{2,1,0:T(8,128)(2,1)S(1)}, u32[]{:S(2)}, u32[]{:S(2)}) collective-permute-start(bf16[2,256,512]{2,1,0:T(8,128)(2,1)S(1)} %pad_maximum_fusion.3), channel_id=1, source_target_pairs={{0,2},{1,3},{2,0},{3,1},{4,6},{5,7},{6,4},{7,5},{8,10},{9,11},{10,... | collective-permute-start | bytes 1572872 | tf_op jit(solution)/shard_map/ppermute | solution.py:486
  230.7 27.5 %collective-permute-start.31 = (bf16[352,512]{1,0:T(8,128)(2,1)S(1)}, bf16[352,512]{1,0:T(8,128)(2,1)S(1)}, u32[]{:S(2)}, u32[]{:S(2)}) collective-permute-start(bf16[352,512]{1,0:T(8,128)(2,1)S(1)} %get-tuple-element.221), channel_id=1, source_target_pairs={{0,24},{4,28},{8,0},{12,4},{16,8},{20,12},{24,16},{28,20},{1,25},{... | collective-permute-start | bytes 1081352 | tf_op jit(solution)/shard_map/ppermute | solution.py:493
  232.3 25.9 %collective-permute-start.30 = (bf16[352,512]{1,0:T(8,128)(2,1)S(1)}, bf16[352,512]{1,0:T(8,128)(2,1)S(1)}, u32[]{:S(2)}, u32[]{:S(2)}) collective-permute-start(bf16[352,512]{1,0:T(8,128)(2,1)S(1)} %get-tuple-element.326), channel_id=1, source_target_pairs={{0,4},{4,0},{8,12},{12,8},{16,20},{20,16},{24,28},{28,24},{1,5},{5... | collective-permute-start | bytes 1081352 | tf_op jit(solution)/shard_map/ppermute | solution.py:486
  233.9 24.3 %collective-permute-start.32 = (bf16[352,512]{1,0:T(8,128)(2,1)S(1)}, bf16[352,512]{1,0:T(8,128)(2,1)S(1)}, u32[]{:S(2)}, u32[]{:S(2)}) collective-permute-start(bf16[352,512]{1,0:T(8,128)(2,1)S(1)} %get-tuple-element.325), channel_id=1, source_target_pairs={{0,8},{4,12},{8,16},{12,20},{16,24},{20,28},{24,0},{28,4},{1,9},{5... | collective-permute-start | bytes 1081352 | tf_op jit(solution)/shard_map/ppermute | solution.py:493
  235.3 14.1 %collective-permute-start.29 = (bf16[2,64,512]{2,1,0:T(8,128)(2,1)S(1)}, bf16[2,64,512]{2,1,0:T(8,128)(2,1)S(1)}, u32[]{:S(2)}, u32[]{:S(2)}) collective-permute-start(bf16[2,64,512]{2,1,0:T(8,128)(2,1)S(1)} %fusion.42), channel_id=1, source_target_pairs={{0,24},{4,28},{8,16},{12,20},{16,8},{20,12},{24,0},{28,4},{1,25},{... | collective-permute-start | bytes 393224 | tf_op jit(solution)/shard_map/ppermute | solution.py:486
  254.4 8.8 %collective-permute-start.36 = (bf16[2,64,512]{2,1,0:T(8,128)(2,1)S(1)}, bf16[2,64,512]{2,1,0:T(8,128)(2,1)S(1)}, u32[]{:S(2)}, u32[]{:S(2)}) collective-permute-start(bf16[2,64,512]{2,1,0:T(8,128)(2,1)S(1)} %get-tuple-element.348), channel_id=1, source_target_pairs={{0,8},{4,12},{8,0},{12,4},{16,24},{20,28},{24,16},{28,20},{1,9},{5... | collective-permute-start | bytes 393224 | tf_op jit(solution)/shard_map/ppermute | solution.py:486
  260.2 9.2 %collective-permute-start.41 = (bf16[256,512]{1,0:T(8,128)(2,1)S(1)}, bf16[256,512]{1,0:T(8,128)(2,1)S(1)}, u32[]{:S(2)}, u32[]{:S(2)}) collective-permute-start(bf16[256,512]{1,0:T(8,128)(2,1)S(1)} %pad_maximum_fusion.8), channel_id=1, source_target_pairs={{0,2},{1,3},{2,0},{3,1},{4,6},{5,7},{6,4},{7,5},{8,10},{9,11},{10,... | collective-permute-start | bytes 786440 | tf_op jit(solution)/shard_map/ppermute | solution.py:486
  260.8 13.3 %collective-permute-start.42 = (bf16[256,512]{1,0:T(8,128)(2,1)S(1)}, bf16[256,512]{1,0:T(8,128)(2,1)S(1)}, u32[]{:S(2)}, u32[]{:S(2)}) collective-permute-start(bf16[256,512]{1,0:T(8,128)(2,1)S(1)} %pad_maximum_fusion.8), channel_id=1, source_target_pairs={{0,3},{1,2},{2,1},{3,0},{4,7},{5,6},{6,5},{7,4},{8,11},{9,10},{10,... | collective-permute-start | bytes 786440 | tf_op jit(solution)/shard_map/ppermute | solution.py:486
  263.2 25.1 %collective-permute-start.34 = (bf16[2,2,2,2,32,512]{5,4,3,2,1,0:T(8,128)(2,1)S(1)}, bf16[2,2,2,2,32,512]{5,4,3,2,1,0:T(8,128)(2,1)S(1)}, u32[]{:S(2)}, u32[]{:S(2)}) collective-permute-start(bf16[2,2,2,2,32,512]{5,4,3,2,1,0:T(8,128)(2,1)S(1)} %bitcast.283), channel_id=1, source_target_pairs={{0,1},{1,0},{2,3},{3,2},{4,5},{5,4},{6,7},{7,6},{8,9},{9,8},{10,11... | collective-permute-start | bytes 1572872 | tf_op jit(solution)/shard_map/ppermute | solution.py:486
  263.5 24.8 %collective-permute-start.35 = (bf16[2,2,2,64,512]{4,3,2,1,0:T(8,128)(2,1)S(1)}, bf16[2,2,2,64,512]{4,3,2,1,0:T(8,128)(2,1)S(1)}, u32[]{:S(2)}, u32[]{:S(2)}) collective-permute-start(bf16[2,2,2,64,512]{4,3,2,1,0:T(8,128)(2,1)S(1)} %bitcast.282), channel_id=1, source_target_pairs={{0,1},{1,0},{2,3},{3,2},{4,5},{5,4},{6,7},{7,6},{8,9},{9,8},{10,11... | collective-permute-start | bytes 1572872 | tf_op jit(solution)/shard_map/ppermute | solution.py:486
  263.9 11.9 %collective-permute-start.37 = (bf16[352,512]{1,0:T(8,128)(2,1)S(1)}, bf16[352,512]{1,0:T(8,128)(2,1)S(1)}, u32[]{:S(2)}, u32[]{:S(2)}) collective-permute-start(bf16[352,512]{1,0:T(8,128)(2,1)S(1)} %broadcast_select_fusion), channel_id=1, source_target_pairs={{0,4},{4,0},{8,12},{12,8},{16,20},{20,16},{24,28},{28,24},{1,5},{5... | collective-permute-start | bytes 1081352 | tf_op jit(solution)/shard_map/ppermute | solution.py:486
  269.4 12.3 %collective-permute-start.38 = (bf16[352,512]{1,0:T(8,128)(2,1)S(1)}, bf16[352,512]{1,0:T(8,128)(2,1)S(1)}, u32[]{:S(2)}, u32[]{:S(2)}) collective-permute-start(bf16[352,512]{1,0:T(8,128)(2,1)S(1)} %get-tuple-element.285), channel_id=1, source_target_pairs={{0,24},{4,28},{8,0},{12,4},{16,8},{20,12},{24,16},{28,20},{1,25},{... | collective-permute-start | bytes 1081352 | tf_op jit(solution)/shard_map/ppermute | solution.py:493
  274.1 14.2 %collective-permute-start.39 = (bf16[352,512]{1,0:T(8,128)(2,1)S(1)}, bf16[352,512]{1,0:T(8,128)(2,1)S(1)}, u32[]{:S(2)}, u32[]{:S(2)}) collective-permute-start(bf16[352,512]{1,0:T(8,128)(2,1)S(1)} %get-tuple-element.282), channel_id=1, source_target_pairs={{0,8},{4,12},{8,16},{12,20},{16,24},{20,28},{24,0},{28,4},{1,9},{5... | collective-permute-start | bytes 1081352 | tf_op jit(solution)/shard_map/ppermute | solution.py:493
  288.3 10.0 %collective-permute-start.50 = (f32[10240]{0:T(1024)S(1)}, f32[10240]{0:T(1024)S(1)}, u32[]{:S(2)}, u32[]{:S(2)}) collective-permute-start(f32[10240]{0:T(1024)S(1)} %fusion.69), channel_id=1, source_target_pairs={{0,2},{1,3},{2,0},{3,1},{4,6},{5,7},{6,4},{7,5},{8,10},{9,11},{10,... | collective-permute-start | bytes 122888 | tf_op jit(solution)/shard_map/ppermute | solution.py:486
  289.4 28.8 %collective-permute-start.47 = (bf16[352,512]{1,0:T(8,128)(2,1)S(1)}, bf16[352,512]{1,0:T(8,128)(2,1)S(1)}, u32[]{:S(2)}, u32[]{:S(2)}) collective-permute-start(bf16[352,512]{1,0:T(8,128)(2,1)S(1)} %get-tuple-element.324.a_ref), channel_id=1, source_target_pairs={{0,4},{4,0},{8,12},{12,8},{16,20},{20,16},{24,28},{28,24},{1,5},{5... | collective-permute-start | bytes 1081352 | tf_op jit(solution)/shard_map/ppermute | solution.py:486
  290.4 27.9 %collective-permute-start.48 = (bf16[352,512]{1,0:T(8,128)(2,1)S(1)}, bf16[352,512]{1,0:T(8,128)(2,1)S(1)}, u32[]{:S(2)}, u32[]{:S(2)}) collective-permute-start(bf16[352,512]{1,0:T(8,128)(2,1)S(1)} %get-tuple-element.323.b_ref), channel_id=1, source_target_pairs={{0,24},{4,28},{8,0},{12,4},{16,8},{20,12},{24,16},{28,20},{1,25},{... | collective-permute-start | bytes 1081352 | tf_op jit(solution)/shard_map/ppermute | solution.py:493
  293.9 24.3 %collective-permute-start.49 = (bf16[352,512]{1,0:T(8,128)(2,1)S(1)}, bf16[352,512]{1,0:T(8,128)(2,1)S(1)}, u32[]{:S(2)}, u32[]{:S(2)}) collective-permute-start(bf16[352,512]{1,0:T(8,128)(2,1)S(1)} %get-tuple-element.322.c_ref), channel_id=1, source_target_pairs={{0,8},{4,12},{8,16},{12,20},{16,24},{20,28},{24,0},{28,4},{1,9},{5... | collective-permute-start | bytes 1081352 | tf_op jit(solution)/shard_map/ppermute | solution.py:493
  294.0 17.5 %collective-permute-start.46 = (bf16[64,512]{1,0:T(8,128)(2,1)S(1)}, bf16[64,512]{1,0:T(8,128)(2,1)S(1)}, u32[]{:S(2)}, u32[]{:S(2)}) collective-permute-start(bf16[64,512]{1,0:T(8,128)(2,1)S(1)} %fusion.56), channel_id=1, source_target_pairs={{0,24},{4,28},{8,16},{12,20},{16,8},{20,12},{24,0},{28,4},{1,25},{... | collective-permute-start | bytes 196616 | tf_op jit(solution)/shard_map/ppermute | solution.py:486
  298.3 14.7 %collective-permute-start.45 = (bf16[2,2,64,512]{3,2,1,0:T(8,128)(2,1)S(1)}, bf16[2,2,64,512]{3,2,1,0:T(8,128)(2,1)S(1)}, u32[]{:S(2)}, u32[]{:S(2)}) collective-permute-start(bf16[2,2,64,512]{3,2,1,0:T(8,128)(2,1)S(1)} %get-tuple-element.344), channel_id=1, source_target_pairs={{0,4},{4,0},{8,12},{12,8},{16,20},{20,16},{24,28},{28,24},{1,5},{5... | collective-permute-start | bytes 786440 | tf_op jit(solution)/shard_map/ppermute | solution.py:486
  341.3 9.0 %collective-permute-start.59 = (bf16[160,512]{1,0:T(8,128)(2,1)S(1)}, bf16[160,512]{1,0:T(8,128)(2,1)S(1)}, u32[]{:S(2)}, u32[]{:S(2)}) collective-permute-start(bf16[160,512]{1,0:T(8,128)(2,1)S(1)} %pad_maximum_fusion.9), channel_id=1, source_target_pairs={{0,3},{1,2},{2,1},{3,0},{4,7},{5,6},{6,5},{7,4},{8,11},{9,10},{10,... | collective-permute-start | bytes 491528 | tf_op jit(solution)/shard_map/ppermute | solution.py:486
  341.4 10.0 %collective-permute-start.60 = (bf16[160,512]{1,0:T(8,128)(2,1)S(1)}, bf16[160,512]{1,0:T(8,128)(2,1)S(1)}, u32[]{:S(2)}, u32[]{:S(2)}) collective-permute-start(bf16[160,512]{1,0:T(8,128)(2,1)S(1)} %pad_maximum_fusion.9), channel_id=1, source_target_pairs={{0,2},{1,3},{2,0},{3,1},{4,6},{5,7},{6,4},{7,5},{8,10},{9,11},{10,... | collective-permute-start | bytes 491528 | tf_op jit(solution)/shard_map/ppermute | solution.py:486
  342.9 8.4 %collective-permute-start.61 = (bf16[160,512]{1,0:T(8,128)(2,1)S(1)}, bf16[160,512]{1,0:T(8,128)(2,1)S(1)}, u32[]{:S(2)}, u32[]{:S(2)}) collective-permute-start(bf16[160,512]{1,0:T(8,128)(2,1)S(1)} %pad_maximum_fusion.9), channel_id=1, source_target_pairs={{0,1},{1,0},{2,3},{3,2},{4,5},{5,4},{6,7},{7,6},{8,9},{9,8},{10,11... | collective-permute-start | bytes 491528 | tf_op jit(solution)/shard_map/ppermute | solution.py:486
  (71 other events, 1102.8 us)

commit v4 on v0

--- a/solution.py
+++ b/solution.py
@@ -3,14 +3,620 @@
 import jax
 import jax.numpy as jnp
 from jax import lax
+from jax.experimental import pallas as pl
+from jax.experimental.pallas import tpu as pltpu
 from jax.sharding import PartitionSpec as P
 
 HEADS = 8
 HEAD_DIM = 64
-
-
 EPS = 1e-05
 MASKED = -1000000000.0
+SCALE = HEAD_DIM ** (-0.5)
+QUAD = 4 * HEAD_DIM
+BF = jnp.bfloat16
+F32 = jnp.float32
+
+
+def mm(a, b, ca=1, cb=0):
+    return lax.dot_general(a, b, (((ca,), (cb,)), ((), ())), preferred_element_type=F32)
+
+
+def norm_parts(values):
+    center = jnp.mean(values, axis=-1, keepdims=True)
+    spread = values - center
+    variance = jnp.mean(spread * spread, axis=-1, keepdims=True)
+    inverse = lax.rsqrt(variance + EPS)
+    return spread * inverse, inverse
+
+
+def norm_back(grad, unit, inverse, gain):
+    scaled = grad * gain
+    first = jnp.mean(scaled, axis=-1, keepdims=True)
+    second = jnp.mean(scaled * unit, axis=-1, keepdims=True)
+    return (scaled - first - unit * second) * inverse
+
+
+def lane_ids(rows):
+    return lax.broadcasted_iota(jnp.int32, (rows, 128), 1)
+
+
+def group_reduce(values, op, fill):
+    rows = values.shape[0]
+    low = lane_ids(rows) < HEAD_DIM
+    outs = []
+    for t in range(values.shape[1] // 128):
+        tile = values[:, t * 128 : (t + 1) * 128]
+        left = op(jnp.where(low, tile, fill), axis=1, keepdims=True)
+        right = op(jnp.where(low, fill, tile), axis=1, keepdims=True)
+        outs.append(jnp.where(low, left, right))
+    return jnp.concatenate(outs, axis=1)
+
+
+def head_masks(dtype):
+    lanes = lax.broadcasted_iota(jnp.int32, (1, QUAD), 1) // HEAD_DIM
+    return [jnp.where(lanes == h, 1.0, 0.0).astype(dtype) for h in range(4)]
+
+
+def stack_heads(part, masks):
+    return jnp.concatenate([part * m for m in masks], axis=0)
+
+
+def pick_heads(stacked, masks):
+    rows = stacked.shape[0] // 4
+    total = stacked[:rows] * masks[0]
+    for h in range(1, 4):
+        total = total + stacked[h * rows : (h + 1) * rows] * masks[h]
+    return total
+
+
+def attend(q, k, v, masks, allow):
+    outs, probs = [], []
+    for quad in range(2):
+        cols = slice(quad * QUAD, (quad + 1) * QUAD)
+        scores = mm(q[:, cols], stack_heads(k[:, cols], masks), 1, 1)
+        if allow is not None:
+            scores = jnp.where(allow, scores, MASKED)
+        raised = jnp.exp(scores - group_reduce(scores, jnp.max, -jnp.inf))
+        prob = raised / group_reduce(raised, jnp.sum, 0.0)
+        outs.append(mm(prob.astype(BF), stack_heads(v[:, cols], masks)))
+        probs.append(prob)
+    return jnp.concatenate(outs, axis=1), jnp.concatenate(probs, axis=1)
+
+
+def attend_back(q, k, v, prob, grad, masks, masks32):
+    dqs, dks, dvs = [], [], []
+    for quad in range(2):
+        cols = slice(quad * QUAD, (quad + 1) * QUAD)
+        p, g = prob[:, cols], grad[:, cols]
+        back = mm(g, stack_heads(v[:, cols], masks), 1, 1)
+        inner = group_reduce(p * back, jnp.sum, 0.0)
+        gs = (p * (back - inner)).astype(BF)
+        dqs.append(mm(gs, stack_heads(k[:, cols], masks)) * SCALE)
+        dks.append(pick_heads(mm(gs, q[:, cols], 0, 0), masks32))
+        dvs.append(pick_heads(mm(p.astype(BF), g, 0, 0), masks32))
+    join = lambda parts: jnp.concatenate(parts, axis=1).astype(BF)
+    return join(dqs), join(dks), join(dvs)
+
+
+def swap_matrix(n):
+    r = lax.broadcasted_iota(jnp.int32, (n, n), 0)
+    c = lax.broadcasted_iota(jnp.int32, (n, n), 1)
+    return jnp.where((r // 16 == c % 16) & (r % 16 == c // 16), 1.0, 0.0).astype(BF)
+
+
+def swap(matrix, values):
+    return mm(matrix, values).astype(BF)
+
+
+def gelu_parts(u):
+    cdf = 0.5 * (1.0 + lax.erf(u * (2.0**-0.5)))
+    density = jnp.exp(u * u * -0.5) * 0.3989422804014327
+    return cdf, density
+
+
+def col_sum(values):
+    return jnp.sum(values.astype(F32), axis=0, keepdims=True)
+
+
+def turn_in(me_ref, x_ref, out_ref):
+    matrix = swap_matrix(256)
+    for d in range(4):
+        rows = x_ref[d * 256 : (d + 1) * 256]
+        out_ref[:, d] = swap(matrix, rows).reshape(16, 16, 512)
+
+
+def turn_out(me_ref, got_ref, out_ref):
+    matrix = swap_matrix(256)
+    for d in range(4):
+        out_ref[d * 256 : (d + 1) * 256] = swap(matrix, got_ref[:, d].reshape(256, 512))
+
+
+def forward_one(
+    me_ref, x_ref, own_ref, context_ref, gain_ref, shift_ref, w_ref, b_ref,
+    o_ref, q_ref, k_ref, v_ref, p_ref,
+):
+    root = me_ref[1]
+    gain, shift = gain_ref[...], shift_ref[...]
+    masks = head_masks(BF)
+    allow = own_ref[...] == context_ref[...]
+    for e in range(2):
+        unit, _ = norm_parts(x_ref[:, e].reshape(512, 512).astype(F32))
+        act = (unit * gain + shift).astype(BF)
+        q = (mm(act, w_ref[:, :512]) + b_ref[:, :512]).astype(BF) * jnp.asarray(SCALE, BF)
+        unit, _ = norm_parts(x_ref[root, e].astype(F32))
+        kv = mm((unit * gain + shift).astype(BF), w_ref[:, 512:])
+        k = kv[:, :512].astype(BF)
+        v = (kv[:, 512:] + b_ref[:, 512:]).astype(BF)
+        out, prob = attend(q, k, v, masks, allow)
+        o_ref[:, :, e] = out.astype(BF).reshape(8, 4, 16, 512)
+        q_ref[e], k_ref[e], v_ref[e], p_ref[e] = q, k, v, prob
+
+
+def middle(
+    me_ref, o1_ref, x0, x1, x2, x3, c0, c1, c2, c3,
+    wm1_ref, off1_ref, g2_ref, s2_ref, wf_ref, bf_ref, wm2_ref, off2_ref,
+    g3_ref, s3_ref, we_ref, be_ref, wr_ref, br_ref,
+    out0, out2, out13, gb1_ref,
+    a2_ref, dqkv_ref, o2_ref, gb2_ref, a3_ref, gu_ref, hid_ref, gb3_ref, vec_ref, bias_ref,
+    o_scr, g_scr,
+):
+    samples = 4
+    me, step = me_ref[0], pl.program_id(0)
+    matrix = swap_matrix(256)
+    now = pl.ds(pl.multiple_of(step * 64, 64), 64)
+
+    @pl.when(step == 0)
+    def _():
+        for f in range(4):
+            o_scr[f] = swap(matrix, o1_ref[:, f].reshape(256, 512))
+
+    def gather(*refs):
+        return jnp.concatenate(
+            [ref[s * 16 : (s + 1) * 16] for s in range(samples) for ref in refs], axis=0
+        )
+
+    def scatter(values, *refs):
+        for s in range(samples):
+            for d, ref in enumerate(refs):
+                at = (s * 4 + d) * 16
+                ref[s * 16 : (s + 1) * 16] = values[at : at + 16]
+
+    masks, masks32 = head_masks(BF), head_masks(F32)
+    attended = gather(*(o_scr[d ^ me, now] for d in range(4)))
+    cot = gather(c0, c1, c2, c3)
+    gb3_ref[...] = cot
+    r1 = gather(x0, x1, x2, x3).astype(F32) + mm(attended, wm1_ref[...]) + off1_ref[...]
+    unit2, inv2 = norm_parts(r1)
+    act2 = (unit2 * g2_ref[...] + s2_ref[...]).astype(BF)
+    a2_ref[...] = act2
+    qkv = mm(act2, wf_ref[...])
+    q = (qkv[:, :512] + bf_ref[:, :512]).astype(BF) * jnp.asarray(SCALE, BF)
+    k = qkv[:, 512:1024].astype(BF)
+    v = (qkv[:, 1024:] + bf_ref[:, 512:]).astype(BF)
+    parts = []
+    for s in range(samples):
+        rows = slice(s * 64, (s + 1) * 64)
+        parts.append(attend(q[rows], k[rows], v[rows], masks, None))
+    o2 = jnp.concatenate([part[0] for part in parts], axis=0).astype(BF)
+    o2_ref[...] = o2
+    r2 = r1 + mm(o2, wm2_ref[...]) + off2_ref[...]
+    unit3, inv3 = norm_parts(r2)
+    act3 = (unit3 * g3_ref[...] + s3_ref[...]).astype(BF)
+    a3_ref[...] = act3
+    out = r2 + br_ref[...]
+    back = None
+    bias = []
+    for b in range(4):
+        cols = slice(b * 512, (b + 1) * 512)
+        u = mm(act3, we_ref[:, cols]) + be_ref[:, cols]
+        cdf, density = gelu_parts(u)
+        hidden = (u * cdf).astype(BF)
+        hid_ref[:, cols] = hidden
+        out = out + mm(hidden, wr_ref[cols, :])
+        gh = mm(cot, wr_ref[cols, :], 1, 1).astype(BF).astype(F32)
+        gu = (gh * (cdf + u * density)).astype(BF)
+        gu_ref[:, cols] = gu
+        bias.append(col_sum(gu))
+        term = mm(gu, we_ref[:, cols], 1, 1)
+        back = term if back is None else back + term
+    scatter(out.astype(BF), out0, out13.at[0], out2, out13.at[1])
+    vecs = [col_sum(back * unit3), col_sum(back)]
+    gr2 = cot.astype(F32) + norm_back(back, unit3, inv3, g3_ref[...])
+    gb2 = gr2.astype(BF)
+    gb2_ref[...] = gb2
+    go2 = mm(gb2, wm2_ref[...], 1, 1).astype(BF)
+    grads = []
+    for s in range(samples):
+        rows = slice(s * 64, (s + 1) * 64)
+        grads.append(
+            jnp.concatenate(
+                attend_back(q[rows], k[rows], v[rows], parts[s][1], go2[rows], masks, masks32),
+                axis=1,
+            )
+        )
+    dqkv = jnp.concatenate(grads, axis=0)
+    dqkv_ref[...] = dqkv
+    back = mm(dqkv, wf_ref[...], 1, 1)
+    vecs += [col_sum(back * unit2), col_sum(back)]
+    gr1 = gr2 + norm_back(back, unit2, inv2, g2_ref[...])
+    scatter(gr1.astype(BF), *(g_scr.at[d ^ me, now] for d in range(4)))
+
+    @pl.when(step == 3)
+    def _():
+        for f in range(4):
+            gb1_ref[:, f] = swap(matrix, g_scr[f]).reshape(8, 2, 16, 512)
+
+    vecs += [col_sum(gb2), col_sum(cot), col_sum(dqkv[:, :512]), col_sum(dqkv[:, 1024:])]
+
+    @pl.when(step == 0)
+    def _():
+        vec_ref[...] = jnp.zeros_like(vec_ref)
+        bias_ref[...] = jnp.zeros_like(bias_ref)
+
+    vec_ref[...] += jnp.concatenate(vecs, axis=0)
+    bias_ref[...] += jnp.concatenate(bias, axis=1)
+
+
+def backward_one(
+    me_ref, gb1_ref, x_ref, q_ref, k_ref, v_ref, p_ref, gain_ref, shift_ref, w_ref, wm_ref,
+    grad_ref, act_ref, dq_ref, cact_ref, dkv_ref, vec_ref,
+    a_scr,
+):
+    root = me_ref[1]
+    gain, shift = gain_ref[...], shift_ref[...]
+    masks, masks32 = head_masks(BF), head_masks(F32)
+    zero = jnp.zeros((1, 512), F32)
+    gain_sum, shift_sum, off_sum, q_sum, v_sum = (zero,) * 5
+    for e in range(2):
+        gb1 = gb1_ref[:, :, e].reshape(512, 512)
+        go = mm(gb1, wm_ref[...], 1, 1).astype(BF)
+        dq, dk, dv = attend_back(q_ref[e], k_ref[e], v_ref[e], p_ref[e], go, masks, masks32)
+        dq_ref[e], dkv_ref[e, :, :512], dkv_ref[e, :, 512:] = dq, dk, dv
+        a_scr[...] = mm(dq, w_ref[:, :512], 1, 1).reshape(8, 64, 512)
+        a_scr[root] += mm(dkv_ref[e], w_ref[:, 512:], 1, 1)
+        back = a_scr[...].reshape(512, 512)
+        unit, inverse = norm_parts(x_ref[:, e].reshape(512, 512).astype(F32))
+        act_ref[e] = (unit * gain + shift).astype(BF)
+        grad = gb1.astype(F32) + norm_back(back, unit, inverse, gain)
+        grad_ref[:, e] = grad.astype(BF).reshape(8, 64, 512)
+        cact_ref[e] = act_ref[e, pl.ds(pl.multiple_of(root * 64, 64), 64)]
+        gain_sum += col_sum(back * unit)
+        shift_sum += col_sum(back)
+        off_sum += col_sum(gb1)
+        q_sum += col_sum(dq)
+        v_sum += col_sum(dv)
+    vec_ref[...] = jnp.concatenate(
+        [gain_sum, shift_sum, off_sum, q_sum, v_sum, zero, zero, zero], axis=0
+    )
+
+
+def place(me_ref, b0, b1, b2, b3, out_ref):
+    for d, ref in enumerate((b0, b1, b2, b3)):
+        out_ref[d ^ me_ref[0]] = ref[...]
+
+
+def lay_out(me_ref, read, order, *pairs):
+    core, xx, yy, zz = me_ref[2], me_ref[3], me_ref[4], me_ref[5]
+    for bits in range(16):
+        index = tuple((bits >> i) & 1 for i in (3, 2, 1, 0))
+        dx, dy, d1, d2 = (index[order.index(name)] for name in ("x", "y", "z", "w"))
+        shard = (zz ^ d1 ^ (2 * d2)) * 2 + (yy ^ dy)
+        for keep_ref, send_ref, start, rows in pairs:
+            keep_ref[index] = read(2 * core + (dx ^ xx), shard, start, rows)
+            send_ref[index] = read(2 * (1 - core) + (dx ^ xx), shard, start, rows)
+
+
+def read_units(scr):
+    def read(unit, shard, start, rows):
+        return scr[unit, pl.ds(pl.multiple_of(shard * 64 + start, rows), rows)]
+
+    return read
+
+
+def grads_reduce(me_ref, hid_ref, gb3_ref, keep_ref, send_ref, scr):
+    for i in range(8):
+        cols = slice(i * 256, (i + 1) * 256)
+        scr[cols] = mm(hid_ref[:, cols], gb3_ref[...], 0, 0).astype(BF)
+
+    def read(unit, shard, start, rows):
+        return scr[pl.ds(pl.multiple_of(shard * 256 + unit * 64, 64), 64)]
+
+    lay_out(me_ref, read, "zxyw", (keep_ref, send_ref, 0, 64))
+
+
+def grads_expand(me_ref, act_ref, gu_ref, keep_ref, send_ref, scr):
+    for n in range(4):
+        scr[n] = mm(act_ref[...], gu_ref[:, n * 512 : (n + 1) * 512], 0, 0).astype(BF)
+    lay_out(me_ref, read_units(scr), "yxzw", (keep_ref, send_ref, 0, 64))
+
+
+def grads_feature(me_ref, act_ref, dqkv_ref, o_ref, gb_ref, keep_ref, send_ref, scr):
+    for n in range(3):
+        scr[n] = mm(act_ref[...], dqkv_ref[:, n * 512 : (n + 1) * 512], 0, 0).astype(BF)
+    scr[3] = mm(o_ref[...], gb_ref[...], 0, 0).astype(BF)
+    lay_out(me_ref, read_units(scr), "xyzw", (keep_ref, send_ref, 0, 64))
+
+
+def grads_sample(
+    me_ref, act_ref, dq_ref, cact_ref, dkv_ref, o_ref, gb1_ref,
+    keepa_ref, senda_ref, keepb_ref, sendb_ref, scr,
+):
+    scr[0] = mm(act_ref[...], dq_ref[...], 0, 0).astype(BF)
+    scr[1] = mm(cact_ref[...], dkv_ref[:, :512], 0, 0).astype(BF)
+    scr[2] = mm(cact_ref[...], dkv_ref[:, 512:], 0, 0).astype(BF)
+    scr[3] = mm(o_ref[...], gb1_ref[...], 0, 0).astype(BF)
+    lay_out(me_ref, read_units(scr), "xyzw", (keepa_ref, senda_ref, 0, 32))
+    lay_out(me_ref, read_units(scr), "yxzw", (keepb_ref, sendb_ref, 32, 32))
+
+
+def spec(shape, index=None):
+    return pl.BlockSpec(shape, index if index is not None else (lambda *a: (0,) * len(shape)))
+
+
+def sds(shape, dtype=BF):
+    return jax.ShapeDtypeStruct(shape, dtype)
+
+
+def params(limit):
+    return pltpu.CompilerParams(vmem_limit_bytes=limit << 20)
+
+
+def row(vector):
+    return vector.reshape(1, -1)
+
+
+def whole(kernel, name, limit, outs, scratch, *inputs):
+    arrays, specs = [inputs[0]], [pl.BlockSpec(memory_space=pltpu.SMEM)]
+    for entry in inputs[1:]:
+        array, block, index = entry if isinstance(entry, tuple) else (entry, None, None)
+        arrays.append(array)
+        block = array.shape if block is None else block
+        index = (0,) * array.ndim if index is None else index
+        specs.append(pl.BlockSpec(block, lambda i, index=index: index))
+    single = not isinstance(outs, tuple)
+    return pl.pallas_call(
+        kernel,
+        grid=(1,),
+        out_shape=outs,
+        in_specs=specs,
+        out_specs=jax.tree.map(lambda o: pl.BlockSpec(o.shape, lambda i: (0,) * len(o.shape)), outs),
+        scratch_shapes=scratch,
+        compiler_params=params(limit),
+        name=name,
+    )(*arrays)
+
+
+def shuffle(value, axis, mask):
+    size = lax.axis_size(axis)
+    return lax.ppermute(value, axis, [(i, i ^ mask) for i in range(size)])
+
+
+CORE, X, Y, Z, W = ("feat", 1), ("feat", 2), ("samp", 1), ("samp", 2), ("samp", 4)
+
+
+def at(stacked, index, axis=0):
+    return lax.dynamic_index_in_dim(stacked, index, axis, keepdims=False)
+
+
+def fence(tree):
+    return lax.optimization_barrier(tree)
+
+
+def plus(a, b):
+    return (a.astype(F32) + b.astype(F32)).astype(BF)
+
+
+class Chain:
+    def __init__(self, keep, sent, dims):
+        self.keep, self.sent, self.dims = keep, sent, (CORE,) + dims
+
+    def start(self):
+        return shuffle(self.sent, *self.dims[0])
+
+    def take(self, got):
+        self.dims = self.dims[1:]
+        if self.dims:
+            self.keep, self.sent = plus(self.keep[0], got[0]), plus(self.keep[1], got[1])
+        else:
+            self.keep = plus(self.keep, got)
+
+
+def together(chains, make=lambda: ()):
+    got = [chain.start() for chain in chains]
+    got, other = fence((got, make()))
+    for chain, value in zip(chains, got):
+        chain.take(value)
+    return other
+
+
+def last_round(parts):
+    joined = jnp.concatenate([part.reshape(-1, 512) for part in parts], axis=0)
+    return joined, [shuffle(joined, "feat", mask) for mask in (1, 2, 3)]
+
+
+def pick_join(rows, core, xx):
+    place = core * 2 + xx
+    outs = []
+    for target in range(4):
+        value = rows[0]
+        for mask, index in ((1, 2), (2, 1), (3, 3)):
+            value = jnp.where((place ^ target) == index, rows[mask], value)
+        outs.append(value.astype(F32))
+    return jnp.stack(outs)
+
+
+def local_small(
+    layer_input, segment_ids, context_flags,
+    first_gain, first_shift, sample_weight, sample_bias, sample_mixer, sample_offset,
+    second_gain, second_shift, feature_weight, feature_bias, feature_mixer, feature_offset,
+    third_gain, third_shift, expand_weight, expand_bias, reduce_weight, reduce_bias, cotangent,
+):
+    samp, feat = lax.axis_index("samp"), lax.axis_index("feat")
+    core, xx = feat % 2, feat // 2
+    flags = context_flags.reshape(8, 64)[:, 0]
+    root = jnp.sum(jnp.where(flags == 1, jnp.arange(8, dtype=jnp.int32), 0))
+    me = jnp.stack([feat, root, core, xx, samp % 2, samp // 2]).astype(jnp.int32)
+
+    turned = whole(
+        turn_in, "turn_in", 8, sds((16, 4, 16, 512)), [], me, layer_input.reshape(1024, 512)
+    )
+    x_t = lax.all_to_all(turned.reshape(8, 2, 64, 512), "samp", 0, 0)
+    x4, cot4 = layer_input.reshape(4, 256, 512), cotangent.reshape(4, 256, 512)
+    block = lambda value, d: at(value, feat ^ d)
+    to_core = jnp.stack([block(x4, 1), block(cot4, 1), block(x4, 3), block(cot4, 3)])
+    from_core = shuffle(to_core, *CORE)
+    x_far = shuffle(jnp.stack([block(x4, 2), from_core[2]]), *X)
+    cot_far = shuffle(jnp.stack([block(cot4, 2), from_core[3]]), *X)
+    x_t, from_core, x_far, cot_far = fence((x_t, from_core, x_far, cot_far))
+
+    tasks = segment_ids.reshape(8, 64)
+    context_tasks = jnp.concatenate([at(tasks, root)] * 4).reshape(1, 256)
+    half = sds((2, 512, 512))
+    o1, q1, k1, v1, p1 = whole(
+        forward_one, "forward_one", 24,
+        (sds((8, 4, 2, 16, 512)), half, sds((2, 64, 512)), sds((2, 64, 512)), sds((2, 512, 512), F32)),
+        [],
+        me, x_t, segment_ids.reshape(512, 1), context_tasks, row(first_gain), row(first_shift),
+        sample_weight, row(sample_bias),
+    )
+    both = ("samp", "feat")
+    o1_f = lax.all_to_all(o1.reshape(32, 2, 16, 512), both, 0, 0).reshape(8, 4, 2, 16, 512)
+
+    weights = [
+        sample_mixer, row(sample_offset), row(second_gain), row(second_shift), feature_weight,
+        row(feature_bias), feature_mixer, row(feature_offset), row(third_gain), row(third_shift),
+        expand_weight, row(expand_bias), reduce_weight, row(reduce_bias),
+    ]
+    flat = spec((64, 512), lambda i, m: (i, 0))
+    own = spec((None, 64, 512), lambda i, m: (m[0], i, 0))
+    part = lambda n: spec((None, 64, 512), lambda i, m: (n, i, 0))
+    wide = lambda n: spec((256, n), lambda i, m: (i, 0))
+    still = lambda shape: spec(shape, lambda i, m: (0,) * len(shape))
+    quarter = sds((256, 512))
+    (
+        out0, out2, out13, gb1_f,
+        act2, dqkv, o2, gb2, act3, gu, hidden, gb3, vec2, bias2,
+    ) = pl.pallas_call(
+        middle,
+        grid_spec=pltpu.PrefetchScalarGridSpec(
+            num_scalar_prefetch=1,
+            grid=(4,),
+            in_specs=[still((8, 4, 2, 16, 512))]
+            + [own, part(0), part(0), part(1), own, part(1), part(0), part(1)]
+            + [
+                pl.BlockSpec(w.shape, lambda i, m: (0, 0), pipeline_mode=pl.Buffered(1))
+                for w in weights
+            ],
+            out_specs=[
+                flat, flat, spec((2, 64, 512), lambda i, m: (0, i, 0)), still((8, 4, 2, 16, 512)),
+                wide(512), wide(1536), wide(512), wide(512), wide(512), wide(2048), wide(2048),
+                wide(512), still((8, 512)), still((1, 2048)),
+            ],
+            scratch_shapes=[pltpu.VMEM((4, 256, 512), BF), pltpu.VMEM((4, 256, 512), BF)],
+        ),
+        out_shape=(
+            quarter, quarter, sds((2, 256, 512)), sds((8, 4, 2, 16, 512)),
+            sds((1024, 512)), sds((1024, 1536)), sds((1024, 512)), sds((1024, 512)),
+            sds((1024, 512)), sds((1024, 2048)), sds((1024, 2048)), sds((1024, 512)),
+            sds((8, 512), F32), sds((1, 2048), F32),
+        ),
+        compiler_params=params(44),
+        name="middle",
+    )(me, o1_f, x4, from_core, x_far, x_far, cot4, from_core, cot_far, cot_far, *weights)
+
+    gb1 = lax.all_to_all(gb1_f.reshape(32, 2, 16, 512), both, 0, 0).reshape(8, 4, 2, 16, 512)
+    parts = sds((2, 2, 2, 2, 64, 512))
+    rk, rs = whole(
+        grads_reduce, "grads_reduce", 16, (parts, parts), [pltpu.VMEM((2048, 512), BF)],
+        me, hidden, gb3,
+    )
+    units = [pltpu.VMEM((4, 512, 512), BF)]
+    ek, es = whole(grads_expand, "grads_expand", 16, (parts, parts), units, me, act3, gu)
+    fk, fs = whole(
+        grads_feature, "grads_feature", 16, (parts, parts), units, me, act2, dqkv, o2, gb2
+    )
+    r_chain = Chain(rk, rs, (Z, X, Y, W))
+    e_chain = Chain(ek, es, (Y, X, Z, W))
+    f_chain = Chain(fk, fs, (X, Y, Z, W))
+    chains = [r_chain, e_chain, f_chain]
+    together(chains)
+    gb1, near = together(chains, lambda: (gb1, shuffle(out13, *CORE)))
+
+    grad_t, act1, dq1, cact, dkv, vec1 = together(
+        chains,
+        lambda: whole(
+            backward_one, "backward_one", 32,
+            (sds((8, 2, 64, 512)), half, half, sds((2, 64, 512)), sds((2, 64, 1024)), sds((8, 512), F32)),
+            [pltpu.VMEM((8, 64, 512), F32)],
+            me, gb1, x_t, q1, k1, v1, p1, row(first_gain), row(first_shift), sample_weight,
+            sample_mixer,
+        ),
+    )
+    got = lax.all_to_all(grad_t, "samp", 0, 0)
+
+    small = sds((2, 2, 2, 2, 32, 512))
+    flat2 = lambda a: a.reshape(-1, a.shape[-1])
+    ak, as_, bk, bs = whole(
+        grads_sample, "grads_sample", 16, (small,) * 4, units,
+        me, flat2(act1), flat2(dq1), flat2(cact), flat2(dkv), flat2(o1), flat2(gb1),
+    )
+    far = shuffle(jnp.stack([out2, near[1]]), *X)
+    vectors = jnp.concatenate([vec2.reshape(-1), bias2.reshape(-1), vec1.reshape(-1)])
+    vector_dims = [CORE, X, Y, Z, W]
+
+    def add_vectors():
+        return shuffle(vectors, *vector_dims.pop(0))
+
+    samples = [Chain(ak, as_, (X, Y, Z, W)), Chain(bk, bs, (Y, X, Z, W))]
+    far, v = together(samples + chains, lambda: (far, add_vectors()))
+    vectors = vectors + v
+    layer_output = whole(
+        place, "place", 16, sds((4, 256, 512)), [], me, out0,
+        (near, (None, 256, 512), (0, 0, 0)), (far, (None, 256, 512), (0, 0, 0)),
+        (far, (None, 256, 512), (1, 0, 0)),
+    ).reshape(64, 16, 512)
+    v, layer_output = together(samples + chains, lambda: (add_vectors(), layer_output))
+    vectors = vectors + v
+    rows_a, others = last_round([chain.keep for chain in chains])
+    v, others = together(samples, lambda: (add_vectors(), others))
+    rows_a = [rows_a] + others
+    vectors = vectors + v
+    (v,) = together(samples, lambda: (add_vectors(),))
+    vectors = vectors + v
+    v, got = together(samples, lambda: (add_vectors(), got))
+    vectors = vectors + v
+    rows_b, others = last_round([chain.keep for chain in samples])
+    input_grad = whole(
+        turn_out, "turn_out", 8, sds((1024, 512)), [], me, got.reshape(16, 4, 16, 512)
+    ).reshape(64, 16, 512)
+    others, input_grad = fence((others, input_grad))
+    rows_b = [rows_b] + others
+
+    cut = lambda rows, start, count: [r[start : start + count] for r in rows]
+    reduce_grad = pick_join(cut(rows_a, 0, 64), core, xx).reshape(256, 512)
+    expand = pick_join(cut(rows_a, 64, 64), core, xx)
+    feature = pick_join(cut(rows_a, 128, 64), core, xx)
+    sample = jnp.concatenate(
+        [pick_join(cut(rows_b, start, 32), core, xx) for start in (0, 32)], axis=1
+    )
+
+    def vector(start, size):
+        return lax.dynamic_slice_in_dim(vectors[start : start + size], samp * (size // 8), size // 8)
+
+    gain3, shift3, gain2, shift2, off2, bias_r = (vector(i * 512, 512) for i in range(6))
+    expand_b = vector(4096, 2048)
+    gain1, shift1, off1 = (vector(6144 + i * 512, 512) for i in range(3))
+    columns = lambda blocks: jnp.concatenate(blocks, axis=1)
+
+    return (
+        layer_output, input_grad,
+        gain1, shift1, columns([sample[i] for i in range(3)]), vector(6144 + 3 * 512, 1024),
+        sample[3], off1,
+        gain2, shift2, columns([feature[i] for i in range(3)]), vector(6 * 512, 1024),
+        feature[3], off2,
+        gain3, shift3, columns([expand[i] for i in range(4)]), expand_b,
+        reduce_grad, bias_r,
+    )
 
 
 def spread_2(block, axis, owner):
@@ -117,7 +723,7 @@
     return (join_heads(grad_queries), join_heads(grad_keys), join_heads(grad_values))
 
 
-def local(
+def local_large(
     layer_input,
     segment_ids,
     context_flags,
@@ -362,8 +968,9 @@
 
 
 def solution(mesh):
+    small = mesh.shape["samp"] == 8 and mesh.shape["feat"] == 4
     return jax.shard_map(
-        local,
+        local_small if small else local_large,
         mesh=mesh,
         in_specs=(
             P("samp", "feat", None),

time: 1240 us -> 286 us (0.23)
  waiting for transfers between devices: 795 us -> 67.6 us
  matrix products: 188 us -> 0 us
  local copies, waits for them, and re-layouts: 131 us -> 21.7 us
  Pallas kernels: 0 us -> 84.6 us
  starting transfers between devices: 1.82 us -> 56.1 us
  other arithmetic: 52.2 us -> 20.2 us
  between operations: 20 us -> 3.44 us
    reduce_scatter x9 -> x0, waiting for transfers between devices: 636 us -> none  [the longest x1 91.6 us: local(): lax.psum_scatter(summed[14], 'samp', scatter_dimension=0, tiled=True)]
    dot_general x30 -> x0, matrix products: 188 us -> none  [the longest x6 38.4 us: apply_weight(): jnp.einsum('sfd,de->sfe', active, weight, preferred_element_type=jnp.floa...]
    psum x2 -> x0, waiting for transfers between devices: 106 us -> none  [the longest x1 98.7 us: spread_2(): return lax.psum(block, axis)]
    pallas_call x0 -> x10, Pallas kernels: none -> 84.6 us  [the longest x1 52.6 us: local_small(): pl.pallas_call(middle, grid_spec=pltpu.PrefetchScalarGridSpec(num_scalar_...]
    reshape x13 -> x3, local copies, waits for them, and re-layouts: 71.9 us -> 0.29 us  [the longest x1 0.14 us: local_small(): segment_ids.reshape(512, 1)]
    ppermute x0 -> x41, waiting for transfers between devices: none -> 67.6 us  [shuffle(): return lax.ppermute(value, axis, [(i, i ^ mask) for i in range(size)])]
    all_gather x3 -> x0, waiting for transfers between devices: 53.2 us -> none  [the longest x1 28.1 us: local(): lax.all_gather(keys_two, 'feat', axis=1, tiled=True)]
    ppermute x0 -> x41, starting transfers between devices: none -> 41.6 us  [shuffle(): return lax.ppermute(value, axis, [(i, i ^ mask) for i in range(size)])]
  transfers between devices with their start and end apart: 14 -> 44, of which waited for: 14 -> 18; matrix products, arithmetic and copies ran while one was open for 11% -> 9% of each run, Pallas kernels for 0% -> 8%
where the time goes in v4:
time: 286 us; the launch traced here: 285 us
  Pallas kernels  84.6 us (30%)
  waiting for transfers between devices  67.6 us (24%)
  starting transfers between devices  56.1 us (20%)
  blocking collectives  31.9 us (11%)
  local copies, waits for them, and re-layouts  21.7 us (8%)
  other arithmetic  20.2 us (7%)
  between operations  3.44 us (1%)
    ppermute x41, waiting for transfers between devices, shuffle(): return lax.ppermute(value, axis, [(i, i ^ mask) for i in range(size)])  67.6 us
    pallas_call x1, Pallas kernels, local_small(): pl.pallas_call(middle, grid_spec=pltpu.PrefetchScalarGridSpec(num_scalar_...  52.6 us
    ppermute x41, starting transfers between devices, shuffle(): return lax.ppermute(value, axis, [(i, i ^ mask) for i in range(size)])  41.6 us
    pallas_call x9, Pallas kernels, whole(): pl.pallas_call(kernel, grid=(1,), out_shape=outs, in_specs=specs, out_spe...  32 us
    all_to_all x1, blocking collectives, local_small(): lax.all_to_all(o1.reshape(32, 2, 16, 512), both, 0, 0)  31.9 us
    convert_element_type x24, other arithmetic, plus(): return (a.astype(F32) + b.astype(F32)).astype(BF)  12.5 us
    unnamed x98, local copies, waits for them, and re-layouts  10.8 us
    dynamic_slice x12, local copies, waits for them, and re-layouts, vector(): lax.dynamic_slice_in_dim(vectors[start:start + size], samp * (size // 8),...  7.04 us
  transfers between devices with their start and end apart: 44, of which 18 were waited for; matrix products, arithmetic and copies ran while one was open for 9% of the time, Pallas kernels for 8%

profile of v4, /device:TPU:0, one launch (start us, length us, event | category | flops | bytes accessed | tf_op | source)
XLA Modules:
  0.0 285.5 jit_solution(9306005389715135763)
XLA Ops:
  0.7 1.9 constant_dynamic-slice_fusion.1
  5.8 2.0 turn_in.1
  7.8 7.0 %all-to-all-start = ((bf16[8,2,64,512]{3,2,1,0:T(8,128)(2,1)}), bf16[8,2,64,512]{3,2,1,0:T(8,128)(2,1)S(1)}, u32[]{:S(2)}, u32[]{:S(2)}) async-start(bf16[8,2,64,512]{3,2,1,0:T(8,128)(2,1)} %bitcast.7), calls=%async_computation | async-start | bytes 2097152 | tf_op jit(solution)/shard_map/all_to_all | solution.py:463
  16.6 1.5 collective-permute-start.2
  21.6 10.0 %collective-permute-done.2.c2.c3 = bf16[2,256,512]{2,1,0:T(8,128)(2,1)S(1)} collective-permute-done((bf16[2,256,512]{2,1,0:T(8,128)(2,1)}, bf16[2,256,512]{2,1,0:T(8,128)(2,1)S(1)}, u32[]{:S(2)}, u32[]{:S(2)}) %collective-permute-start.2) | collective-permute-done | bytes 524320 | tf_op jit(solution)/shard_map/ppermute | solution.py:391
  31.6 10.5 %collective-permute-done.1.x2.x3 = bf16[2,256,512]{2,1,0:T(8,128)(2,1)S(1)} collective-permute-done((bf16[2,256,512]{2,1,0:T(8,128)(2,1)S(1)}, bf16[2,256,512]{2,1,0:T(8,128)(2,1)S(1)}, u32[]{:S(2)}, u32[]{:S(2)}) %collective-permute-start.1) | collective-permute-done | bytes 524320 | tf_op jit(solution)/shard_map/ppermute | solution.py:391
  44.3 4.9 %forward_one.1 = (bf16[8,4,2,16,512]{4,3,2,1,0:T(8,128)(2,1)S(1)}, bf16[2,512,512]{2,1,0:T(8,128)(2,1)S(1)}, bf16[2,64,512]{2,1,0:T(8,128)(2,1)S(1)}, bf16[2,64,512]{2,1,0:T(8,128)(2,1)S(1)}, f32[2,512,512]{2,1,0:T(8,128)S(1)}) custom-call(s32[6]{0:T(128)S(1)} %stack.108.me_ref, bf16[8,2,64,512]{3,2,1,0:T(8,128)(2,1)S(1)} %all-to-all-done.x_ref, ...), custom_call_target="tpu_custom_call" | custom-call | tf_op jit(solution)/shard_map/forward_one/pallas_call | solution.py:377
  51.5 31.9 %all_to_all.20 = bf16[32,2,16,512]{3,2,1,0:T(8,128)(2,1)} all-to-all(bf16[32,2,16,512]{3,2,1,0:T(8,128)(2,1)S(1)} %bitcast.300), channel_id=1, replica_groups=mesh['samp'=8,'feat'=4] {'samp','feat'}, dimensions={0} | all-to-all | bytes 2097152 | tf_op jit(solution)/shard_map/all_to_all | solution.py:483
  83.5 52.6 %middle.1 = (bf16[256,512]{1,0:T(8,128)(2,1)S(1)}, bf16[256,512]{1,0:T(8,128)(2,1)S(1)}, bf16[2,256,512]{2,1,0:T(8,128)(2,1)S(1)}, bf16[8,4,2,16,512]{4,3,2,1,0:...) custom-call(s32[6]{0:T(128)S(1)} %stack.108.me_ref, ...), custom_call_target="tpu_custom_call" | custom-call | tf_op jit(solution)/shard_map/middle/pallas_call | solution.py:499
  136.2 2.5 copy-done.5
  138.7 4.0 %grads_feature.1 = (bf16[2,2,2,2,64,512]{5,4,3,2,1,0:T(8,128)(2,1)S(1)}, bf16[2,2,2,2,64,512]{5,4,3,2,1,0:T(8,128)(2,1)}) custom-call(s32[6]{0:T(128)S(1)} %stack.108.me_ref, bf16[1024,512]{1,0:T(8,128)(2,1)S(1)} %get-tuple-element.119.act_ref, bf16[1024,1536]{1,0:T(8,128)(2,1)S(1)} %copy-done.5, bf16[1024,512]{1,0:T(8,128)(2,1)S(1)} %get-tuple-element.121.o_ref, ...), custom_call_target="tpu_custom_call" | custom-call | tf_op jit(solution)/shard_map/grads_feature/pallas_call | solution.py:377
  143.7 4.0 %grads_expand.1 = (bf16[2,2,2,2,64,512]{5,4,3,2,1,0:T(8,128)(2,1)S(1)}, bf16[2,2,2,2,64,512]{5,4,3,2,1,0:T(8,128)(2,1)}) custom-call(s32[6]{0:T(128)S(1)} %stack.108.me_ref, bf16[1024,512]{1,0:T(8,128)(2,1)S(1)} %get-tuple-element.116.act_ref, bf16[1024,2048]{1,0:T(8,128)(2,1)S(1)} %copy-done.4), custom_call_target="tpu_custom_call" | custom-call | tf_op jit(solution)/shard_map/grads_expand/pallas_call | solution.py:377
  148.2 4.0 %grads_reduce.1 = (bf16[2,2,2,2,64,512]{5,4,3,2,1,0:T(8,128)(2,1)S(1)}, bf16[2,2,2,2,64,512]{5,4,3,2,1,0:T(8,128)(2,1)}) custom-call(s32[6]{0:T(128)S(1)} %stack.108.me_ref, bf16[1024,2048]{1,0:T(8,128)(2,1)S(1)} %copy-done.3, bf16[1024,512]{1,0:T(8,128)(2,1)S(1)} %get-tuple-element.113.gb3_ref), custom_call_target="tpu_custom_call" | custom-call | tf_op jit(solution)/shard_map/grads_reduce/pallas_call | solution.py:377
  153.3 4.0 %all-to-all-start.2 = ((bf16[32,2,16,512]{3,2,1,0:T(8,128)(2,1)}), bf16[32,2,16,512]{3,2,1,0:T(8,128)(2,1)S(1)}, u32[]{:S(2)}, u32[]{:S(2)}) async-start(bf16[32,2,16,512]{3,2,1,0:T(8,128)(2,1)} %bitcast.305), calls=%async_computation.2 | async-start | bytes 2097152 | tf_op jit(solution)/shard_map/all_to_all | solution.py:527
  157.4 2.7 add_convert_fusion
  160.1 1.6 collective-permute-start.8
  161.8 2.3 add_convert_fusion.1
  164.1 1.5 collective-permute-start.7
  165.6 2.4 fusion
  167.9 1.5 collective-permute-start.6
  169.4 12.8 %collective-permute-done.8 = bf16[2,2,2,64,512]{4,3,2,1,0:T(8,128)(2,1)S(1)} collective-permute-done((bf16[2,2,2,64,512]{4,3,2,1,0:T(8,128)(2,1)S(1)}, bf16[2,2,2,64,512]{4,3,2,1,0:T(8,128)(2,1)S(1)}, u32[]{:S(2)}, u32[]{:S(2)}) %collective-permute-start.8) | collective-permute-done | bytes 524320 | tf_op jit(solution)/shard_map/ppermute | solution.py:391
  182.2 1.8 collective-permute-done.7
  184.9 3.2 %collective-permute-done.6 = bf16[2,2,2,64,512]{4,3,2,1,0:T(8,128)(2,1)} collective-permute-done((bf16[2,2,2,64,512]{4,3,2,1,0:T(8,128)(2,1)S(1)}, bf16[2,2,2,64,512]{4,3,2,1,0:T(8,128)(2,1)}, u32[]{:S(2)}, u32[]{:S(2)}) %collective-permute-start.6) | collective-permute-done | bytes 524320 | tf_op jit(solution)/shard_map/ppermute | solution.py:391
  189.6 1.6 collective-permute-start.12
  191.2 1.5 fusion.4
  192.7 1.5 collective-permute-start.11
  196.2 1.5 collective-permute-start.18
  197.8 7.4 %backward_one.1 = (bf16[8,2,64,512]{3,2,1,0:T(8,128)(2,1)}, bf16[2,512,512]{2,1,0:T(8,128)(2,1)S(1)}, bf16[2,512,512]{2,1,0:T(8,128)(2,1)S(1)}, bf16[2,64,512]{2...) custom-call(s32[6]{0:T(128)S(1)} %stack.108.me_ref, ...), custom_call_target="tpu_custom_call" | custom-call | tf_op jit(solution)/shard_map/backward_one/pallas_call | solution.py:377
  205.2 2.4 collective-permute-done.10
  208.3 2.2 grads_sample.1
  211.3 1.6 collective-permute-start.16
  214.2 2.7 collective-permute-done.16
  217.0 1.9 collective-permute-done.15
  218.9 1.5 collective-permute-start.25
  220.4 2.5 collective-permute-start.24
  225.0 2.5 collective-permute-start.22
  227.5 1.6 place.1
  229.1 1.9 collective-permute-done.23
  234.6 1.6 collective-permute-start.27
  236.2 1.6 collective-permute-done.28
  238.5 3.6 %all-to-all-start.3 = ((bf16[8,2,64,512]{3,2,1,0:T(8,128)(2,1)}), bf16[8,2,64,512]{3,2,1,0:T(8,128)(2,1)S(1)}, u32[]{:S(2)}, u32[]{:S(2)}) async-start(bf16[8,2,64,512]{3,2,1,0:T(8,128)(2,1)} %get-tuple-element.182), calls=%async_computation.3 | async-start | bytes 2097152 | tf_op jit(solution)/shard_map/all_to_all | solution.py:555
  242.1 4.2 %collective-permute-done.27 = bf16[2,2,32,512]{3,2,1,0:T(8,128)(2,1)S(1)} collective-permute-done((bf16[2,2,32,512]{3,2,1,0:T(8,128)(2,1)S(1)}, bf16[2,2,32,512]{3,2,1,0:T(8,128)(2,1)S(1)}, u32[]{:S(2)}, u32[]{:S(2)}) %collective-permute-start.27) | collective-permute-done | bytes 131104 | tf_op jit(solution)/shard_map/ppermute | solution.py:391
  246.4 2.1 collective-permute-start.33
  251.1 9.9 %collective-permute-done.34 = f32[10240]{0:T(1024)S(1)} collective-permute-done((f32[10240]{0:T(1024)S(1)}, f32[10240]{0:T(1024)S(1)}, u32[]{:S(2)}, u32[]{:S(2)}) %collective-permute-start.34) | collective-permute-done | bytes 40992 | tf_op jit(solution)/shard_map/ppermute | solution.py:391
  262.4 4.8 %collective-permute-start.37 = (f32[10240]{0:T(1024)S(1)}, f32[10240]{0:T(1024)S(1)}, u32[]{:S(2)}, u32[]{:S(2)}) collective-permute-start(f32[10240]{0:T(1024)S(1)} %add.292), channel_id=1, source_target_pairs={{0,16},{4,20},{8,24},{12,28},{16,0},{20,4},{24,8},{28,12},{1,17},{... | collective-permute-start | bytes 122888 | tf_op jit(solution)/shard_map/ppermute | solution.py:391
  267.3 3.0 %collective-permute-start.35 = (bf16[32,512]{1,0:T(8,128)(2,1)S(1)}, bf16[32,512]{1,0:T(8,128)(2,1)S(1)}, u32[]{:S(2)}, u32[]{:S(2)}) collective-permute-start(bf16[32,512]{1,0:T(8,128)(2,1)S(1)} %fusion.57), channel_id=1, source_target_pairs={{0,16},{4,20},{8,24},{12,28},{16,0},{20,4},{24,8},{28,12},{1,17},{... | collective-permute-start | bytes 98312 | tf_op jit(solution)/shard_map/ppermute | solution.py:391
  273.0 1.4 collective-permute-start.39
  274.9 2.0 turn_out.1
  (227 shorter events, 43.1 us)
Async XLA Ops:
  3.8 11.0 %collective-permute-start = (bf16[4,256,512]{2,1,0:T(8,128)(2,1)}, bf16[4,256,512]{2,1,0:T(8,128)(2,1)S(1)}, u32[]{:S(2)}, u32[]{:S(2)}) collective-permute-start(bf16[4,256,512]{2,1,0:T(8,128)(2,1)} %pad_maximum_fusion), channel_id=1, source_target_pairs={{0,1},{1,0},{2,3},{3,2},{4,5},{5,4},{6,7},{7,6},{8,9},{9,8},{10,11... | collective-permute-start | bytes 3145736 | tf_op jit(solution)/shard_map/ppermute | solution.py:391
  7.8 34.3 %all-to-all-start = ((bf16[8,2,64,512]{3,2,1,0:T(8,128)(2,1)}), bf16[8,2,64,512]{3,2,1,0:T(8,128)(2,1)S(1)}, u32[]{:S(2)}, u32[]{:S(2)}) async-start(bf16[8,2,64,512]{3,2,1,0:T(8,128)(2,1)} %bitcast.7), calls=%async_computation | async-start | bytes 2097152 | tf_op jit(solution)/shard_map/all_to_all | solution.py:463
  16.6 15.0 %collective-permute-start.2 = (bf16[2,256,512]{2,1,0:T(8,128)(2,1)}, bf16[2,256,512]{2,1,0:T(8,128)(2,1)S(1)}, u32[]{:S(2)}, u32[]{:S(2)}) collective-permute-start(bf16[2,256,512]{2,1,0:T(8,128)(2,1)} %pad_maximum_fusion.2), channel_id=1, source_target_pairs={{0,2},{1,3},{2,0},{3,1},{4,6},{5,7},{6,4},{7,5},{8,10},{9,11},{10,... | collective-permute-start | bytes 1572872 | tf_op jit(solution)/shard_map/ppermute | solution.py:391
  18.2 24.0 %collective-permute-start.1 = (bf16[2,256,512]{2,1,0:T(8,128)(2,1)S(1)}, bf16[2,256,512]{2,1,0:T(8,128)(2,1)S(1)}, u32[]{:S(2)}, u32[]{:S(2)}) collective-permute-start(bf16[2,256,512]{2,1,0:T(8,128)(2,1)S(1)} %pad_maximum_fusion.1), channel_id=1, source_target_pairs={{0,2},{1,3},{2,0},{3,1},{4,6},{5,7},{6,4},{7,5},{8,10},{9,11},{10,... | collective-permute-start | bytes 1572872 | tf_op jit(solution)/shard_map/ppermute | solution.py:391
  44.2 39.2 %copy-start.32 = (f32[1024]{0:T(1024)S(1)}, f32[1024]{0:T(1024)}, u32[]{:S(2)}) copy-start(f32[1024]{0:T(1024)} %param.34) | copy-start | bytes 12292
  44.2 39.2 %copy-start.33 = (f32[512]{0:T(512)S(1)}, f32[512]{0:T(512)}, u32[]{:S(2)}) copy-start(f32[512]{0:T(512)} %param.30) | copy-start | bytes 6148
  44.3 39.2 %copy-start.34 = (f32[512]{0:T(512)S(1)}, f32[512]{0:T(512)}, u32[]{:S(2)}) copy-start(f32[512]{0:T(512)} %param.31) | copy-start | bytes 6148
  44.3 39.2 %copy-start.35 = (f32[512]{0:T(512)S(1)}, f32[512]{0:T(512)}, u32[]{:S(2)}) copy-start(f32[512]{0:T(512)} %param.32) | copy-start | bytes 6148
  143.7 13.7 %collective-permute-start.5 = (bf16[2,2,2,2,64,512]{5,4,3,2,1,0:T(8,128)(2,1)}, bf16[2,2,2,2,64,512]{5,4,3,2,1,0:T(8,128)(2,1)}, u32[]{:S(2)}, u32[]{:S(2)}) collective-permute-start(bf16[2,2,2,2,64,512]{5,4,3,2,1,0:T(8,128)(2,1)} %get-tuple-element.123), channel_id=1, source_target_pairs={{0,1},{1,0},{2,3},{3,2},{4,5},{5,4},{6,7},{7,6},{8,9},{9,8},{10,11... | collective-permute-start | bytes 3145736 | tf_op jit(solution)/shard_map/ppermute | solution.py:391
  147.7 9.7 %collective-permute-start.4 = (bf16[2,2,2,2,64,512]{5,4,3,2,1,0:T(8,128)(2,1)}, bf16[2,2,2,2,64,512]{5,4,3,2,1,0:T(8,128)(2,1)}, u32[]{:S(2)}, u32[]{:S(2)}) collective-permute-start(bf16[2,2,2,2,64,512]{5,4,3,2,1,0:T(8,128)(2,1)} %get-tuple-element.118), channel_id=1, source_target_pairs={{0,1},{1,0},{2,3},{3,2},{4,5},{5,4},{6,7},{7,6},{8,9},{9,8},{10,11... | collective-permute-start | bytes 3145736 | tf_op jit(solution)/shard_map/ppermute | solution.py:391
  153.3 4.1 %collective-permute-start.3 = (bf16[2,2,2,2,64,512]{5,4,3,2,1,0:T(8,128)(2,1)}, bf16[2,2,2,2,64,512]{5,4,3,2,1,0:T(8,128)(2,1)}, u32[]{:S(2)}, u32[]{:S(2)}) collective-permute-start(bf16[2,2,2,2,64,512]{5,4,3,2,1,0:T(8,128)(2,1)} %get-tuple-element.115), channel_id=1, source_target_pairs={{0,1},{1,0},{2,3},{3,2},{4,5},{5,4},{6,7},{7,6},{8,9},{9,8},{10,11... | collective-permute-start | bytes 3145736 | tf_op jit(solution)/shard_map/ppermute | solution.py:391
  153.3 34.8 %all-to-all-start.2 = ((bf16[32,2,16,512]{3,2,1,0:T(8,128)(2,1)}), bf16[32,2,16,512]{3,2,1,0:T(8,128)(2,1)S(1)}, u32[]{:S(2)}, u32[]{:S(2)}) async-start(bf16[32,2,16,512]{3,2,1,0:T(8,128)(2,1)} %bitcast.305), calls=%async_computation.2 | async-start | bytes 2097152 | tf_op jit(solution)/shard_map/all_to_all | solution.py:527
  157.3 12.1 %collective-permute-start.9 = (bf16[2,256,512]{2,1,0:T(8,128)(2,1)}, bf16[2,256,512]{2,1,0:T(8,128)(2,1)S(1)}, u32[]{:S(2)}, u32[]{:S(2)}) collective-permute-start(bf16[2,256,512]{2,1,0:T(8,128)(2,1)} %copy-done.41), channel_id=1, source_target_pairs={{0,1},{1,0},{2,3},{3,2},{4,5},{5,4},{6,7},{7,6},{8,9},{9,8},{10,11... | collective-permute-start | bytes 1572872 | tf_op jit(solution)/shard_map/ppermute | solution.py:391
  160.1 22.1 %collective-permute-start.8 = (bf16[2,2,2,64,512]{4,3,2,1,0:T(8,128)(2,1)S(1)}, bf16[2,2,2,64,512]{4,3,2,1,0:T(8,128)(2,1)S(1)}, u32[]{:S(2)}, u32[]{:S(2)}) collective-permute-start(bf16[2,2,2,64,512]{4,3,2,1,0:T(8,128)(2,1)S(1)} %get-tuple-element.195), channel_id=1, source_target_pairs={{0,2},{1,3},{2,0},{3,1},{4,6},{5,7},{6,4},{7,5},{8,10},{9,11},{10,... | collective-permute-start | bytes 1572872 | tf_op jit(solution)/shard_map/ppermute | solution.py:391
  164.1 20.0 %collective-permute-start.7 = (bf16[2,2,2,64,512]{4,3,2,1,0:T(8,128)(2,1)S(1)}, bf16[2,2,2,64,512]{4,3,2,1,0:T(8,128)(2,1)S(1)}, u32[]{:S(2)}, u32[]{:S(2)}) collective-permute-start(bf16[2,2,2,64,512]{4,3,2,1,0:T(8,128)(2,1)S(1)} %get-tuple-element.197), channel_id=1, source_target_pairs={{0,4},{4,0},{8,12},{12,8},{16,20},{20,16},{24,28},{28,24},{1,5},{5... | collective-permute-start | bytes 1572872 | tf_op jit(solution)/shard_map/ppermute | solution.py:391
  167.9 20.2 %collective-permute-start.6 = (bf16[2,2,2,64,512]{4,3,2,1,0:T(8,128)(2,1)S(1)}, bf16[2,2,2,64,512]{4,3,2,1,0:T(8,128)(2,1)}, u32[]{:S(2)}, u32[]{:S(2)}) collective-permute-start(bf16[2,2,2,64,512]{4,3,2,1,0:T(8,128)(2,1)S(1)} %get-tuple-element.198), channel_id=1, source_target_pairs={{0,8},{4,12},{8,0},{12,4},{16,24},{20,28},{24,16},{28,20},{1,9},{5... | collective-permute-start | bytes 1572872 | tf_op jit(solution)/shard_map/ppermute | solution.py:391
  189.6 15.6 %collective-permute-start.12 = (bf16[2,2,64,512]{3,2,1,0:T(8,128)(2,1)S(1)}, bf16[2,2,64,512]{3,2,1,0:T(8,128)(2,1)S(1)}, u32[]{:S(2)}, u32[]{:S(2)}) collective-permute-start(bf16[2,2,64,512]{3,2,1,0:T(8,128)(2,1)S(1)} %get-tuple-element.205), channel_id=1, source_target_pairs={{0,4},{4,0},{8,12},{12,8},{16,20},{20,16},{24,28},{28,24},{1,5},{5... | collective-permute-start | bytes 786440 | tf_op jit(solution)/shard_map/ppermute | solution.py:391
  192.7 12.5 %collective-permute-start.11 = (bf16[2,2,64,512]{3,2,1,0:T(8,128)(2,1)S(1)}, bf16[2,2,64,512]{3,2,1,0:T(8,128)(2,1)S(1)}, u32[]{:S(2)}, u32[]{:S(2)}) collective-permute-start(bf16[2,2,64,512]{3,2,1,0:T(8,128)(2,1)S(1)} %get-tuple-element.207), channel_id=1, source_target_pairs={{0,2},{1,3},{2,0},{3,1},{4,6},{5,7},{6,4},{7,5},{8,10},{9,11},{10,... | collective-permute-start | bytes 786440 | tf_op jit(solution)/shard_map/ppermute | solution.py:391
  195.5 12.1 %collective-permute-start.10 = (bf16[2,2,64,512]{3,2,1,0:T(8,128)(2,1)S(1)}, bf16[2,2,64,512]{3,2,1,0:T(8,128)(2,1)S(1)}, u32[]{:S(2)}, u32[]{:S(2)}) collective-permute-start(bf16[2,2,64,512]{3,2,1,0:T(8,128)(2,1)S(1)} %get-tuple-element.209), channel_id=1, source_target_pairs={{0,2},{1,3},{2,0},{3,1},{4,6},{5,7},{6,4},{7,5},{8,10},{9,11},{10,... | collective-permute-start | bytes 786440 | tf_op jit(solution)/shard_map/ppermute | solution.py:391
  196.2 22.6 %collective-permute-start.18 = (bf16[2,256,512]{2,1,0:T(8,128)(2,1)S(1)}, bf16[2,256,512]{2,1,0:T(8,128)(2,1)S(1)}, u32[]{:S(2)}, u32[]{:S(2)}) collective-permute-start(bf16[2,256,512]{2,1,0:T(8,128)(2,1)S(1)} %pad_maximum_fusion.3), channel_id=1, source_target_pairs={{0,2},{1,3},{2,0},{3,1},{4,6},{5,7},{6,4},{7,5},{8,10},{9,11},{10,... | collective-permute-start | bytes 1572872 | tf_op jit(solution)/shard_map/ppermute | solution.py:391
  207.6 3.7 %collective-permute-start.19 = (f32[10240]{0:T(1024)S(1)}, f32[10240]{0:T(1024)S(1)}, u32[]{:S(2)}, u32[]{:S(2)}) collective-permute-start(f32[10240]{0:T(1024)S(1)} %pad_maximum_fusion.8), channel_id=1, source_target_pairs={{0,1},{1,0},{2,3},{3,2},{4,5},{5,4},{6,7},{7,6},{8,9},{9,8},{10,11... | collective-permute-start | bytes 122888 | tf_op jit(solution)/shard_map/ppermute | solution.py:391
  207.7 6.0 %collective-permute-start.17 = (bf16[2,64,512]{2,1,0:T(8,128)(2,1)S(1)}, bf16[2,64,512]{2,1,0:T(8,128)(2,1)S(1)}, u32[]{:S(2)}, u32[]{:S(2)}) collective-permute-start(bf16[2,64,512]{2,1,0:T(8,128)(2,1)S(1)} %get-tuple-element.239), channel_id=1, source_target_pairs={{0,8},{4,12},{8,0},{12,4},{16,24},{20,28},{24,16},{28,20},{1,9},{5... | collective-permute-start | bytes 393224 | tf_op jit(solution)/shard_map/ppermute | solution.py:391
  210.6 8.3 %collective-permute-start.13 = (bf16[2,2,2,2,32,512]{5,4,3,2,1,0:T(8,128)(2,1)S(1)}, bf16[2,2,2,2,32,512]{5,4,3,2,1,0:T(8,128)(2,1)S(1)}, u32[]{:S(2)}, u32[]{:S(2)}) collective-permute-start(bf16[2,2,2,2,32,512]{5,4,3,2,1,0:T(8,128)(2,1)S(1)} %get-tuple-element.150), channel_id=1, source_target_pairs={{0,1},{1,0},{2,3},{3,2},{4,5},{5,4},{6,7},{7,6},{8,9},{9,8},{10,11... | collective-permute-start | bytes 1572872 | tf_op jit(solution)/shard_map/ppermute | solution.py:391
  210.8 8.0 %collective-permute-start.14 = (bf16[2,2,2,2,32,512]{5,4,3,2,1,0:T(8,128)(2,1)S(1)}, bf16[2,2,2,2,32,512]{5,4,3,2,1,0:T(8,128)(2,1)S(1)}, u32[]{:S(2)}, u32[]{:S(2)}) collective-permute-start(bf16[2,2,2,2,32,512]{5,4,3,2,1,0:T(8,128)(2,1)S(1)} %get-tuple-element.151), channel_id=1, source_target_pairs={{0,1},{1,0},{2,3},{3,2},{4,5},{5,4},{6,7},{7,6},{8,9},{9,8},{10,11... | collective-permute-start | bytes 1572872 | tf_op jit(solution)/shard_map/ppermute | solution.py:391
  211.3 5.7 %collective-permute-start.16 = (bf16[2,64,512]{2,1,0:T(8,128)(2,1)S(1)}, bf16[2,64,512]{2,1,0:T(8,128)(2,1)S(1)}, u32[]{:S(2)}, u32[]{:S(2)}) collective-permute-start(bf16[2,64,512]{2,1,0:T(8,128)(2,1)S(1)} %get-tuple-element.241), channel_id=1, source_target_pairs={{0,8},{4,12},{8,0},{12,4},{16,24},{20,28},{24,16},{28,20},{1,9},{5... | collective-permute-start | bytes 393224 | tf_op jit(solution)/shard_map/ppermute | solution.py:391
  213.7 5.1 %collective-permute-start.15 = (bf16[2,64,512]{2,1,0:T(8,128)(2,1)S(1)}, bf16[2,64,512]{2,1,0:T(8,128)(2,1)S(1)}, u32[]{:S(2)}, u32[]{:S(2)}) collective-permute-start(bf16[2,64,512]{2,1,0:T(8,128)(2,1)S(1)} %get-tuple-element.243), channel_id=1, source_target_pairs={{0,4},{4,0},{8,12},{12,8},{16,20},{20,16},{24,28},{28,24},{1,5},{5... | collective-permute-start | bytes 393224 | tf_op jit(solution)/shard_map/ppermute | solution.py:391
  218.9 6.2 %collective-permute-start.25 = (f32[10240]{0:T(1024)S(1)}, f32[10240]{0:T(1024)S(1)}, u32[]{:S(2)}, u32[]{:S(2)}) collective-permute-start(f32[10240]{0:T(1024)S(1)} %fusion.62), channel_id=1, source_target_pairs={{0,2},{1,3},{2,0},{3,1},{4,6},{5,7},{6,4},{7,5},{8,10},{9,11},{10,... | collective-permute-start | bytes 122888 | tf_op jit(solution)/shard_map/ppermute | solution.py:391
  220.4 8.7 %collective-permute-start.24 = (bf16[64,512]{1,0:T(8,128)(2,1)S(1)}, bf16[64,512]{1,0:T(8,128)(2,1)S(1)}, u32[]{:S(2)}, u32[]{:S(2)}) collective-permute-start(bf16[64,512]{1,0:T(8,128)(2,1)S(1)} %fusion.44), channel_id=1, source_target_pairs={{0,16},{4,20},{8,24},{12,28},{16,0},{20,4},{24,8},{28,12},{1,17},{... | collective-permute-start | bytes 196616 | tf_op jit(solution)/shard_map/ppermute | solution.py:391
  222.9 8.1 %collective-permute-start.23 = (bf16[64,512]{1,0:T(8,128)(2,1)S(1)}, bf16[64,512]{1,0:T(8,128)(2,1)S(1)}, u32[]{:S(2)}, u32[]{:S(2)}) collective-permute-start(bf16[64,512]{1,0:T(8,128)(2,1)S(1)} %fusion.43), channel_id=1, source_target_pairs={{0,16},{4,20},{8,24},{12,28},{16,0},{20,4},{24,8},{28,12},{1,17},{... | collective-permute-start | bytes 196616 | tf_op jit(solution)/shard_map/ppermute | solution.py:391
  223.7 8.0 %collective-permute-start.21 = (bf16[2,2,2,32,512]{4,3,2,1,0:T(8,128)(2,1)S(1)}, bf16[2,2,2,32,512]{4,3,2,1,0:T(8,128)(2,1)S(1)}, u32[]{:S(2)}, u32[]{:S(2)}) collective-permute-start(bf16[2,2,2,32,512]{4,3,2,1,0:T(8,128)(2,1)S(1)} %get-tuple-element.201), channel_id=1, source_target_pairs={{0,4},{4,0},{8,12},{12,8},{16,20},{20,16},{24,28},{28,24},{1,5},{5... | collective-permute-start | bytes 786440 | tf_op jit(solution)/shard_map/ppermute | solution.py:391
  224.4 7.3 %collective-permute-start.20 = (bf16[2,2,2,32,512]{4,3,2,1,0:T(8,128)(2,1)S(1)}, bf16[2,2,2,32,512]{4,3,2,1,0:T(8,128)(2,1)S(1)}, u32[]{:S(2)}, u32[]{:S(2)}) collective-permute-start(bf16[2,2,2,32,512]{4,3,2,1,0:T(8,128)(2,1)S(1)} %get-tuple-element.203), channel_id=1, source_target_pairs={{0,2},{1,3},{2,0},{3,1},{4,6},{5,7},{6,4},{7,5},{8,10},{9,11},{10,... | collective-permute-start | bytes 786440 | tf_op jit(solution)/shard_map/ppermute | solution.py:391
  225.0 6.7 %collective-permute-start.22 = (bf16[64,512]{1,0:T(8,128)(2,1)S(1)}, bf16[64,512]{1,0:T(8,128)(2,1)S(1)}, u32[]{:S(2)}, u32[]{:S(2)}) collective-permute-start(bf16[64,512]{1,0:T(8,128)(2,1)S(1)} %fusion.42), channel_id=1, source_target_pairs={{0,16},{4,20},{8,24},{12,28},{16,0},{20,4},{24,8},{28,12},{1,17},{... | collective-permute-start | bytes 196616 | tf_op jit(solution)/shard_map/ppermute | solution.py:391
  231.8 14.4 %collective-permute-start.29 = (bf16[192,512]{1,0:T(8,128)(2,1)S(1)}, bf16[192,512]{1,0:T(8,128)(2,1)S(1)}, u32[]{:S(2)}, u32[]{:S(2)}) collective-permute-start(bf16[192,512]{1,0:T(8,128)(2,1)S(1)} %pad_maximum_fusion.6), channel_id=1, source_target_pairs={{0,1},{1,0},{2,3},{3,2},{4,5},{5,4},{6,7},{7,6},{8,9},{9,8},{10,11... | collective-permute-start | bytes 589832 | tf_op jit(solution)/shard_map/ppermute | solution.py:391
  231.9 14.3 %collective-permute-start.30 = (bf16[192,512]{1,0:T(8,128)(2,1)S(1)}, bf16[192,512]{1,0:T(8,128)(2,1)S(1)}, u32[]{:S(2)}, u32[]{:S(2)}) collective-permute-start(bf16[192,512]{1,0:T(8,128)(2,1)S(1)} %pad_maximum_fusion.6), channel_id=1, source_target_pairs={{0,2},{1,3},{2,0},{3,1},{4,6},{5,7},{6,4},{7,5},{8,10},{9,11},{10,... | collective-permute-start | bytes 589832 | tf_op jit(solution)/shard_map/ppermute | solution.py:391
  232.7 13.5 %collective-permute-start.31 = (bf16[192,512]{1,0:T(8,128)(2,1)S(1)}, bf16[192,512]{1,0:T(8,128)(2,1)S(1)}, u32[]{:S(2)}, u32[]{:S(2)}) collective-permute-start(bf16[192,512]{1,0:T(8,128)(2,1)S(1)} %pad_maximum_fusion.6), channel_id=1, source_target_pairs={{0,3},{1,2},{2,1},{3,0},{4,7},{5,6},{6,5},{7,4},{8,11},{9,10},{10,... | collective-permute-start | bytes 589832 | tf_op jit(solution)/shard_map/ppermute | solution.py:391
  233.8 4.0 %collective-permute-start.28 = (f32[10240]{0:T(1024)S(1)}, f32[10240]{0:T(1024)S(1)}, u32[]{:S(2)}, u32[]{:S(2)}) collective-permute-start(f32[10240]{0:T(1024)S(1)} %add.276), channel_id=1, source_target_pairs={{0,4},{4,0},{8,12},{12,8},{16,20},{20,16},{24,28},{28,24},{1,5},{5... | collective-permute-start | bytes 122888 | tf_op jit(solution)/shard_map/ppermute | solution.py:391
  234.6 11.7 %collective-permute-start.27 = (bf16[2,2,32,512]{3,2,1,0:T(8,128)(2,1)S(1)}, bf16[2,2,32,512]{3,2,1,0:T(8,128)(2,1)S(1)}, u32[]{:S(2)}, u32[]{:S(2)}) collective-permute-start(bf16[2,2,32,512]{3,2,1,0:T(8,128)(2,1)S(1)} %get-tuple-element.235), channel_id=1, source_target_pairs={{0,2},{1,3},{2,0},{3,1},{4,6},{5,7},{6,4},{7,5},{8,10},{9,11},{10,... | collective-permute-start | bytes 393224 | tf_op jit(solution)/shard_map/ppermute | solution.py:391
  237.8 8.5 %collective-permute-start.26 = (bf16[2,2,32,512]{3,2,1,0:T(8,128)(2,1)S(1)}, bf16[2,2,32,512]{3,2,1,0:T(8,128)(2,1)S(1)}, u32[]{:S(2)}, u32[]{:S(2)}) collective-permute-start(bf16[2,2,32,512]{3,2,1,0:T(8,128)(2,1)S(1)} %get-tuple-element.236), channel_id=1, source_target_pairs={{0,4},{4,0},{8,12},{12,8},{16,20},{20,16},{24,28},{28,24},{1,5},{5... | collective-permute-start | bytes 393224 | tf_op jit(solution)/shard_map/ppermute | solution.py:391
  238.5 34.3 %all-to-all-start.3 = ((bf16[8,2,64,512]{3,2,1,0:T(8,128)(2,1)}), bf16[8,2,64,512]{3,2,1,0:T(8,128)(2,1)S(1)}, u32[]{:S(2)}, u32[]{:S(2)}) async-start(bf16[8,2,64,512]{3,2,1,0:T(8,128)(2,1)} %get-tuple-element.182), calls=%async_computation.3 | async-start | bytes 2097152 | tf_op jit(solution)/shard_map/all_to_all | solution.py:555
  246.3 14.7 %collective-permute-start.34 = (f32[10240]{0:T(1024)S(1)}, f32[10240]{0:T(1024)S(1)}, u32[]{:S(2)}, u32[]{:S(2)}) collective-permute-start(f32[10240]{0:T(1024)S(1)} %add.287), channel_id=1, source_target_pairs={{0,8},{4,12},{8,0},{12,4},{16,24},{20,28},{24,16},{28,20},{1,9},{5... | collective-permute-start | bytes 122888 | tf_op jit(solution)/shard_map/ppermute | solution.py:391
  246.4 15.3 %collective-permute-start.33 = (bf16[2,32,512]{2,1,0:T(8,128)(2,1)S(1)}, bf16[2,32,512]{2,1,0:T(8,128)(2,1)S(1)}, u32[]{:S(2)}, u32[]{:S(2)}) collective-permute-start(bf16[2,32,512]{2,1,0:T(8,128)(2,1)S(1)} %get-tuple-element.245), channel_id=1, source_target_pairs={{0,8},{4,12},{8,0},{12,4},{16,24},{20,28},{24,16},{28,20},{1,9},{5... | collective-permute-start | bytes 196616 | tf_op jit(solution)/shard_map/ppermute | solution.py:391
  248.5 13.9 %collective-permute-start.32 = (bf16[2,32,512]{2,1,0:T(8,128)(2,1)S(1)}, bf16[2,32,512]{2,1,0:T(8,128)(2,1)S(1)}, u32[]{:S(2)}, u32[]{:S(2)}) collective-permute-start(bf16[2,32,512]{2,1,0:T(8,128)(2,1)S(1)} %get-tuple-element.246), channel_id=1, source_target_pairs={{0,8},{4,12},{8,0},{12,4},{16,24},{20,28},{24,16},{28,20},{1,9},{5... | collective-permute-start | bytes 196616 | tf_op jit(solution)/shard_map/ppermute | solution.py:391
  262.4 10.4 %collective-permute-start.37 = (f32[10240]{0:T(1024)S(1)}, f32[10240]{0:T(1024)S(1)}, u32[]{:S(2)}, u32[]{:S(2)}) collective-permute-start(f32[10240]{0:T(1024)S(1)} %add.292), channel_id=1, source_target_pairs={{0,16},{4,20},{8,24},{12,28},{16,0},{20,4},{24,8},{28,12},{1,17},{... | collective-permute-start | bytes 122888 | tf_op jit(solution)/shard_map/ppermute | solution.py:391
  267.2 5.2 %collective-permute-start.36 = (bf16[32,512]{1,0:T(8,128)(2,1)S(1)}, bf16[32,512]{1,0:T(8,128)(2,1)S(1)}, u32[]{:S(2)}, u32[]{:S(2)}) collective-permute-start(bf16[32,512]{1,0:T(8,128)(2,1)S(1)} %fusion.58), channel_id=1, source_target_pairs={{0,16},{4,20},{8,24},{12,28},{16,0},{20,4},{24,8},{28,12},{1,17},{... | collective-permute-start | bytes 98312 | tf_op jit(solution)/shard_map/ppermute | solution.py:391
  267.3 5.5 %collective-permute-start.35 = (bf16[32,512]{1,0:T(8,128)(2,1)S(1)}, bf16[32,512]{1,0:T(8,128)(2,1)S(1)}, u32[]{:S(2)}, u32[]{:S(2)}) collective-permute-start(bf16[32,512]{1,0:T(8,128)(2,1)S(1)} %fusion.57), channel_id=1, source_target_pairs={{0,16},{4,20},{8,24},{12,28},{16,0},{20,4},{24,8},{28,12},{1,17},{... | collective-permute-start | bytes 98312 | tf_op jit(solution)/shard_map/ppermute | solution.py:391
  272.9 11.0 %collective-permute-start.38 = (bf16[64,512]{1,0:T(8,128)(2,1)S(1)}, bf16[64,512]{1,0:T(8,128)(2,1)S(1)}, u32[]{:S(2)}, u32[]{:S(2)}) collective-permute-start(bf16[64,512]{1,0:T(8,128)(2,1)S(1)} %pad_maximum_fusion.7), channel_id=1, source_target_pairs={{0,1},{1,0},{2,3},{3,2},{4,5},{5,4},{6,7},{7,6},{8,9},{9,8},{10,11... | collective-permute-start | bytes 196616 | tf_op jit(solution)/shard_map/ppermute | solution.py:391
  273.0 10.9 %collective-permute-start.39 = (bf16[64,512]{1,0:T(8,128)(2,1)S(1)}, bf16[64,512]{1,0:T(8,128)(2,1)S(1)}, u32[]{:S(2)}, u32[]{:S(2)}) collective-permute-start(bf16[64,512]{1,0:T(8,128)(2,1)S(1)} %pad_maximum_fusion.7), channel_id=1, source_target_pairs={{0,2},{1,3},{2,0},{3,1},{4,6},{5,7},{6,4},{7,5},{8,10},{9,11},{10,... | collective-permute-start | bytes 196616 | tf_op jit(solution)/shard_map/ppermute | solution.py:391
  274.4 9.5 %collective-permute-start.40 = (bf16[64,512]{1,0:T(8,128)(2,1)S(1)}, bf16[64,512]{1,0:T(8,128)(2,1)S(1)}, u32[]{:S(2)}, u32[]{:S(2)}) collective-permute-start(bf16[64,512]{1,0:T(8,128)(2,1)S(1)} %pad_maximum_fusion.7), channel_id=1, source_target_pairs={{0,3},{1,2},{2,1},{3,0},{4,7},{5,6},{6,5},{7,4},{8,11},{9,10},{10,... | collective-permute-start | bytes 196616 | tf_op jit(solution)/shard_map/ppermute | solution.py:391
  (45 other events, 565.8 us)
